TPU v7x, 128 devices: a whole 4x4x4 slice. The times are simulated.
128 devices in a mesh: space: 64 (over z, y, x_lo, core), mem: 2 (over x_hi).
Axes of the slice: x: 4 (x_hi: 2, x_lo: 2; x = x_hi * 2 + x_lo), y: 4, z: 4, core: 2. Of those that a mesh axis runs over, the one named last changes fastest.
Arguments:
- state: float32 [64, 1048576], P('mem', 'space'), may hold values from -6 to 6
- obs_index: int32 [4, 16384], P(None, 'space'), may hold values from 0 to 1048575, as said below
- obs_value: float32 [4, 16384], P(None, 'space'), may hold values from -8 to 8
- obs_var: float32 [4, 16384], P(None, 'space'), may hold values from 0.02 to 5
Outputs:
- posterior: float32 [64, 1048576], P('mem', 'space')
Inputs may be any that keep to these rules, and one draw needn't show every extreme that they name: `obs_index`: observation k of every batch measures a column of the block owned by index k // 256 of space, that is a column between (k // 256) * 16384 and (k // 256 + 1) * 16384 - 1.
All inputs are finite; a program needn't handle non-finite values.
Results may differ from a plain program's by a relative error of at most 0.0075.
Values may be sent and summed in bfloat16 or wider, within the bound.
No kernel may reach another device: no remote copies, remote signals or barrier semaphores. Data moves between devices by JAX's collectives and lax.ppermute only.
A program may use at most 64 MiB of HBM per device.

v0:
```python
import jax
import jax.numpy as jnp
from jax import lax
from jax.sharding import PartitionSpec as P

RADIUS = 32768


def shifted(block, axis, distance):
    devices = range(lax.axis_size(axis))
    route = [(i - distance, i) for i in devices if i - distance in devices]
    return lax.ppermute(block, axis, route)


def summarize(prior_obs, values, variances):
    members = prior_obs.shape[0]
    obs_mean = jnp.mean(prior_obs, axis=0)
    anomaly = prior_obs - obs_mean
    spread = jnp.sum(anomaly * anomaly, axis=0) / (members - 1) + 1e-06
    post_var = 1.0 / (1.0 / spread + 1.0 / variances)
    post_mean = post_var * (obs_mean / spread + values / variances)
    change = post_mean - obs_mean + (jnp.sqrt(post_var / spread) - 1.0) * anomaly
    weighted = (change / ((members - 1) * spread)).astype(jnp.bfloat16)
    return (anomaly.astype(jnp.bfloat16), weighted)


def position_band(obs_index):
    pieces = []
    for offset in (2, 1, 0, -1, -2):
        if offset == 0:
            pieces.append(obs_index)
        else:
            pieces.append(shifted(obs_index, "space", offset))
    return jnp.concatenate(pieces, axis=1)


def summary_band(stacked):
    pieces = []
    for offset in (2, 1, 0, -1, -2):
        if offset == 0:
            pieces.append(stacked)
        else:
            pieces.append(shifted(stacked, "space", offset))
    return jnp.concatenate(pieces, axis=2)


def shards(state, obs_index, obs_value, obs_var):
    mem_index = lax.axis_index("mem")
    space_index = lax.axis_index("space")
    pair_count = lax.axis_size("mem")
    columns = lax.all_to_all(state, "mem", split_axis=1, concat_axis=0, tiled=True)
    width = columns.shape[1]
    col_start = space_index * (pair_count * width) + mem_index * width
    band_positions = position_band(obs_index)
    block_width = min(1024, state.shape[1] // 2)
    block_count = width // block_width
    column_base = col_start + lax.iota(jnp.int32, block_width)
    for batch in range(obs_index.shape[0]):
        local_col = obs_index[batch] - col_start
        inside = (local_col >= 0) & (local_col < width)
        picked = jnp.take(columns, jnp.clip(local_col, 0, width - 1), axis=1)
        partial_value = jnp.where(inside[None, :], picked, 0.0)
        prior_obs = lax.psum(partial_value, "mem")
        anomaly, weighted = summarize(prior_obs, obs_value[batch], obs_var[batch])
        band_data = summary_band(jnp.stack([anomaly, weighted]))
        band_anom = band_data[0]
        band_weight = band_data[1]
        band_pos = band_positions[batch]
        state_anom = (columns - jnp.mean(columns, axis=0)).astype(jnp.bfloat16)

        def update(step, current):
            block_start = step * block_width
            spread_piece = lax.dynamic_slice_in_dim(state_anom, block_start, block_width, 1)
            cov = lax.dot_general(
                band_anom,
                spread_piece,
                (((0,), (0,)), ((), ())),
                preferred_element_type=jnp.float32,
            )
            distance = jnp.abs(column_base[None, :] + block_start - band_pos[:, None]).astype(
                jnp.float32
            )
            taper = jnp.square(jnp.maximum(0.0, 1.0 - distance / RADIUS))
            gain = (taper * cov).astype(jnp.bfloat16)
            increment = jnp.dot(band_weight, gain, preferred_element_type=jnp.float32)
            before = lax.dynamic_slice_in_dim(current, block_start, block_width, 1)
            return lax.dynamic_update_slice_in_dim(current, before + increment, block_start, 1)

        columns = lax.fori_loop(0, block_count, update, columns)
    return lax.all_to_all(
        columns.astype(jnp.bfloat16), "mem", split_axis=0, concat_axis=1, tiled=True
    ).astype(columns.dtype)


def solution(mesh):
    placed = (P("mem", "space"), P(None, "space"), P(None, "space"), P(None, "space"))
    return jax.shard_map(
        shards, mesh=mesh, in_specs=placed, out_specs=P("mem", "space"), check_vma=False
    )
```

profile of v0, /device:TPU:0, one launch (start us, length us, event | category | flops | bytes accessed | tf_op | source)
XLA Modules:
  0.0 422.6 jit_solution(1460003583755461608)
XLA Ops:
  6.5 3.5 collective-permute-start
  17.2 4.0 all-to-all-start
  21.5 25.6 %all-to-all-done = f32[32,2,8192]{2,0,1:T(8,128)S(1)} async-done(((f32[32,2,8192]{2,0,1:T(8,128)}), f32[32,2,8192]{2,0,1:T(8,128)S(1)}, u32[]{:S(2)}, u32[]{:S(2)}) %all-to-all-start) | async-done | bytes 2097184 | tf_op jit(solution)/shard_map/all_to_all | solution.py:51
  53.8 34.5 %all-reduce.5.cloned.1.call-done = f32[64,256]{0,1:T(8,128)} async-done(((f32[64,256]{0,1:T(8,128)}), f32[64,256]{0,1:T(8,128)}) %all-reduce.5.cloned.1.call-update) | async-done | bytes 65552 | tf_op jit(solution)/shard_map/psum | solution.py:63
  102.3 6.5 %collective-permute-done.7 = bf16[2,64,256]{1,2,0:T(8,128)(2,1)S(1)} collective-permute-done((bf16[2,64,256]{1,2,0:T(8,128)(2,1)S(1)}, bf16[2,64,256]{1,2,0:T(8,128)(2,1)S(1)}, u32[]{:S(2)}, u32[]{:S(2)}) %collective-permute-start.7) | collective-permute-done | bytes 65568 | tf_op jit(solution)/shard_map/ppermute | solution.py:12
  109.3 27.5 %while.56 = (s32[]{:T(128)}, f32[64,8192]{1,0:T(8,128)S(1)}, s32[1,1280]{1,0:T(1,128)S(1)}, bf16[64,8192]{1,0:T(8,128)(2,1)}, bf16[64,1280]{1,0:T(8,128)(2,1)S(1...) while((s32[]{:T(128)}, f32[64,8192]{1,0:T(8,128)S(1)}, ...), condition=%wide.region_5.7_spmd.clone, body=%wide.region_4.6_spmd.clone.sunk | while | flops 347408384 | bytes 1010855 | solution.py:89
  112.8 3.4 fusion.96
  119.6 3.4 fusion.96
  126.5 3.4 fusion.96
  133.4 3.4 fusion.96
  143.4 31.6 %all-reduce.7.cloned.1.call-done = f32[64,256]{0,1:T(8,128)} async-done(((f32[64,256]{0,1:T(8,128)}), f32[64,256]{0,1:T(8,128)}) %all-reduce.7.cloned.1.call-update) | async-done | bytes 65552 | tf_op jit(solution)/shard_map/psum | solution.py:63
  189.0 6.5 %collective-permute-done.11 = bf16[2,64,256]{1,2,0:T(8,128)(2,1)S(1)} collective-permute-done((bf16[2,64,256]{1,2,0:T(8,128)(2,1)S(1)}, bf16[2,64,256]{1,2,0:T(8,128)(2,1)S(1)}, u32[]{:S(2)}, u32[]{:S(2)}) %collective-permute-start.11) | collective-permute-done | bytes 65568 | tf_op jit(solution)/shard_map/ppermute | solution.py:12
  196.0 27.5 %while.57 = (s32[]{:T(128)}, f32[64,8192]{1,0:T(8,128)S(1)}, s32[1,1280]{1,0:T(1,128)S(1)}, bf16[64,8192]{1,0:T(8,128)(2,1)}, bf16[64,1280]{1,0:T(8,128)(2,1)S(1...) while((s32[]{:T(128)}, f32[64,8192]{1,0:T(8,128)S(1)}, ...), condition=%wide.region_11.13_spmd.clone, body=%wide.region_10.12_spmd.clone.sunk | while | flops 347408384 | bytes 1010855 | solution.py:89
  196.0 3.4 fusion.100
  202.9 3.4 fusion.100
  206.3 3.4 fusion.100
  209.8 3.4 fusion.100
  213.2 3.4 fusion.100
  216.6 3.4 fusion.100
  220.1 3.4 fusion.100
  230.1 31.6 %all-reduce.9.cloned.1.call-done = f32[64,256]{0,1:T(8,128)} async-done(((f32[64,256]{0,1:T(8,128)}), f32[64,256]{0,1:T(8,128)}) %all-reduce.9.cloned.1.call-update) | async-done | bytes 65552 | tf_op jit(solution)/shard_map/psum | solution.py:63
  275.7 6.5 %collective-permute-done.15 = bf16[2,64,256]{1,2,0:T(8,128)(2,1)S(1)} collective-permute-done((bf16[2,64,256]{1,2,0:T(8,128)(2,1)S(1)}, bf16[2,64,256]{1,2,0:T(8,128)(2,1)S(1)}, u32[]{:S(2)}, u32[]{:S(2)}) %collective-permute-start.15) | collective-permute-done | bytes 65568 | tf_op jit(solution)/shard_map/ppermute | solution.py:12
  282.6 27.5 %while.58 = (s32[]{:T(128)}, f32[64,8192]{1,0:T(8,128)S(1)}, s32[1,1280]{1,0:T(1,128)S(1)}, bf16[64,8192]{1,0:T(8,128)(2,1)}, bf16[64,1280]{1,0:T(8,128)(2,1)S(1...) while((s32[]{:T(128)}, f32[64,8192]{1,0:T(8,128)S(1)}, ...), condition=%wide.region_17.19_spmd.clone, body=%wide.region_16.18_spmd.clone.sunk | while | flops 347408384 | bytes 1010855 | solution.py:89
  286.1 3.4 fusion.104
  293.0 3.4 fusion.104
  316.7 31.6 %all-reduce.11.cloned.1.call-done = f32[64,256]{0,1:T(8,128)} async-done(((f32[64,256]{0,1:T(8,128)}), f32[64,256]{0,1:T(8,128)}) %all-reduce.11.cloned.1.call-update) | async-done | bytes 65552 | tf_op jit(solution)/shard_map/psum | solution.py:63
  362.4 6.5 %collective-permute-done.19 = bf16[2,64,256]{1,2,0:T(8,128)(2,1)S(1)} collective-permute-done((bf16[2,64,256]{1,2,0:T(8,128)(2,1)S(1)}, bf16[2,64,256]{1,2,0:T(8,128)(2,1)S(1)}, u32[]{:S(2)}, u32[]{:S(2)}) %collective-permute-start.19) | collective-permute-done | bytes 65568 | tf_op jit(solution)/shard_map/ppermute | solution.py:12
  369.3 27.5 %while.59 = (s32[]{:T(128)}, f32[64,8192]{1,0:T(8,128)S(1)}, s32[1,1280]{1,0:T(1,128)S(1)}, bf16[64,8192]{1,0:T(8,128)(2,1)}, bf16[64,1280]{1,0:T(8,128)(2,1)S(1...) while((s32[]{:T(128)}, f32[64,8192]{1,0:T(8,128)S(1)}, ...), condition=%wide.region_23.25_spmd.clone, body=%wide.region_22.24_spmd.clone.sunk | while | flops 347408384 | bytes 1010855 | solution.py:89
  376.2 3.4 fusion.108
  383.1 3.4 fusion.108
  390.0 3.4 fusion.108
  396.9 17.6 %all_to_all.32 = bf16[2,32,8192]{2,1,0:T(8,128)(2,1)S(1)} all-to-all(bf16[2,32,8192]{2,1,0:T(8,128)(2,1)S(1)} %bitcast.188), channel_id=1, replica_groups=mesh['space'=64,'mem'=2] {'mem'}, dimensions={0} | all-to-all | bytes 2097152 | tf_op jit(solution)/shard_map/all_to_all | solution.py:90
  (240 shorter events, 147.6 us)
Async XLA Ops:
  6.5 14.8 %collective-permute-start = (s32[4,256]{1,0:T(4,128)}, s32[4,256]{1,0:T(4,128)S(1)}, u32[]{:S(2)}, u32[]{:S(2)}) collective-permute-start(s32[4,256]{1,0:T(4,128)} %param.15), channel_id=1, source_target_pairs={{0,4},{2,6},{4,8},{6,10},{8,12},{10,14},{12,16},{14,18},{16,20},{1... | collective-permute-start | bytes 12296 | tf_op jit(solution)/shard_map/ppermute | solution.py:12
  10.0 11.4 %collective-permute-start.1 = (s32[4,256]{1,0:T(4,128)}, s32[4,256]{1,0:T(4,128)S(1)}, u32[]{:S(2)}, u32[]{:S(2)}) collective-permute-start(s32[4,256]{1,0:T(4,128)} %param.15), channel_id=1, source_target_pairs={{0,2},{2,4},{4,6},{6,8},{8,10},{10,12},{12,14},{14,16},{16,18},{18... | collective-permute-start | bytes 12296 | tf_op jit(solution)/shard_map/ppermute | solution.py:12
  11.5 9.9 %collective-permute-start.2 = (s32[4,256]{1,0:T(4,128)}, s32[4,256]{1,0:T(4,128)S(1)}, u32[]{:S(2)}, u32[]{:S(2)}) collective-permute-start(s32[4,256]{1,0:T(4,128)} %param.15), channel_id=1, source_target_pairs={{2,0},{4,2},{6,4},{8,6},{10,8},{12,10},{14,12},{16,14},{18,16},{20... | collective-permute-start | bytes 12296 | tf_op jit(solution)/shard_map/ppermute | solution.py:12
  12.8 8.7 %collective-permute-start.3 = (s32[4,256]{1,0:T(4,128)}, s32[4,256]{1,0:T(4,128)S(1)}, u32[]{:S(2)}, u32[]{:S(2)}) collective-permute-start(s32[4,256]{1,0:T(4,128)} %param.15), channel_id=1, source_target_pairs={{4,0},{6,2},{8,4},{10,6},{12,8},{14,10},{16,12},{18,14},{20,16},{2... | collective-permute-start | bytes 12296 | tf_op jit(solution)/shard_map/ppermute | solution.py:12
  14.1 7.1 %copy-start = (s32[4,256]{1,0:T(4,128)S(1)}, s32[4,256]{1,0:T(4,128)}, u32[]{:S(2)}) copy-start(s32[4,256]{1,0:T(4,128)} %param.15) | copy-start | bytes 12292
  17.2 30.0 %all-to-all-start = ((f32[32,2,8192]{2,0,1:T(8,128)}), f32[32,2,8192]{2,0,1:T(8,128)S(1)}, u32[]{:S(2)}, u32[]{:S(2)}) async-start(f32[32,2,8192]{2,0,1:T(8,128)} %bitcast.187), calls=%async_computation | async-start | bytes 4194304 | tf_op jit(solution)/shard_map/all_to_all | solution.py:51
  21.2 67.1 %all-reduce.5.cloned.1.call-start = ((), (), s32[]{:S(2)}) async-start(), calls=%async_computation.2 | async-start | bytes 262144 | tf_op jit(solution)/shard_map/psum | solution.py:63
  47.1 43.2 %copy-start.1 = (f32[4,256]{1,0:T(4,128)S(1)}, f32[4,256]{1,0:T(4,128)}, u32[]{:S(2)}) copy-start(f32[4,256]{1,0:T(4,128)} %param.16) | copy-start | bytes 12292
  47.1 43.3 %copy-start.2 = (f32[4,256]{1,0:T(4,128)S(1)}, f32[4,256]{1,0:T(4,128)}, u32[]{:S(2)}) copy-start(f32[4,256]{1,0:T(4,128)} %param.17) | copy-start | bytes 12292
  53.6 121.4 %all-reduce.7.cloned.1.call-start = ((), (), s32[]{:S(2)}) async-start(), calls=%async_computation.3 | async-start | bytes 262144 | tf_op jit(solution)/shard_map/psum | solution.py:63
  91.6 7.5 %collective-permute-start.4 = (bf16[2,64,256]{1,2,0:T(8,128)(2,1)S(1)}, bf16[2,64,256]{1,2,0:T(8,128)(2,1)S(1)}, u32[]{:S(2)}, u32[]{:S(2)}) collective-permute-start(bf16[2,64,256]{1,2,0:T(8,128)(2,1)S(1)} %pad_maximum_fusion), channel_id=1, source_target_pairs={{0,4},{2,6},{4,8},{6,10},{8,12},{10,14},{12,16},{14,18},{16,20},{1... | collective-permute-start | bytes 196616 | tf_op jit(solution)/shard_map/ppermute | solution.py:12
  95.2 3.9 collective-permute-start.5
  96.5 5.8 %collective-permute-start.6 = (bf16[2,64,256]{1,2,0:T(8,128)(2,1)S(1)}, bf16[2,64,256]{1,2,0:T(8,128)(2,1)S(1)}, u32[]{:S(2)}, u32[]{:S(2)}) collective-permute-start(bf16[2,64,256]{1,2,0:T(8,128)(2,1)S(1)} %pad_maximum_fusion), channel_id=1, source_target_pairs={{2,0},{4,2},{6,4},{8,6},{10,8},{12,10},{14,12},{16,14},{18,16},{20... | collective-permute-start | bytes 196616 | tf_op jit(solution)/shard_map/ppermute | solution.py:12
  97.8 11.1 %collective-permute-start.7 = (bf16[2,64,256]{1,2,0:T(8,128)(2,1)S(1)}, bf16[2,64,256]{1,2,0:T(8,128)(2,1)S(1)}, u32[]{:S(2)}, u32[]{:S(2)}) collective-permute-start(bf16[2,64,256]{1,2,0:T(8,128)(2,1)S(1)} %pad_maximum_fusion), channel_id=1, source_target_pairs={{4,0},{6,2},{8,4},{10,6},{12,8},{14,10},{16,12},{18,14},{20,16},{2... | collective-permute-start | bytes 196616 | tf_op jit(solution)/shard_map/ppermute | solution.py:12
  143.3 118.3 %all-reduce.9.cloned.1.call-start = ((), (), s32[]{:S(2)}) async-start(), calls=%async_computation.4 | async-start | bytes 262144 | tf_op jit(solution)/shard_map/psum | solution.py:63
  178.3 7.5 %collective-permute-start.8 = (bf16[2,64,256]{1,2,0:T(8,128)(2,1)S(1)}, bf16[2,64,256]{1,2,0:T(8,128)(2,1)S(1)}, u32[]{:S(2)}, u32[]{:S(2)}) collective-permute-start(bf16[2,64,256]{1,2,0:T(8,128)(2,1)S(1)} %pad_maximum_fusion.1), channel_id=1, source_target_pairs={{0,4},{2,6},{4,8},{6,10},{8,12},{10,14},{12,16},{14,18},{16,20},{1... | collective-permute-start | bytes 196616 | tf_op jit(solution)/shard_map/ppermute | solution.py:12
  181.9 3.9 collective-permute-start.9
  183.2 5.8 %collective-permute-start.10 = (bf16[2,64,256]{1,2,0:T(8,128)(2,1)S(1)}, bf16[2,64,256]{1,2,0:T(8,128)(2,1)S(1)}, u32[]{:S(2)}, u32[]{:S(2)}) collective-permute-start(bf16[2,64,256]{1,2,0:T(8,128)(2,1)S(1)} %pad_maximum_fusion.1), channel_id=1, source_target_pairs={{2,0},{4,2},{6,4},{8,6},{10,8},{12,10},{14,12},{16,14},{18,16},{20... | collective-permute-start | bytes 196616 | tf_op jit(solution)/shard_map/ppermute | solution.py:12
  184.5 11.1 %collective-permute-start.11 = (bf16[2,64,256]{1,2,0:T(8,128)(2,1)S(1)}, bf16[2,64,256]{1,2,0:T(8,128)(2,1)S(1)}, u32[]{:S(2)}, u32[]{:S(2)}) collective-permute-start(bf16[2,64,256]{1,2,0:T(8,128)(2,1)S(1)} %pad_maximum_fusion.1), channel_id=1, source_target_pairs={{4,0},{6,2},{8,4},{10,6},{12,8},{14,10},{16,12},{18,14},{20,16},{2... | collective-permute-start | bytes 196616 | tf_op jit(solution)/shard_map/ppermute | solution.py:12
  230.0 118.3 %all-reduce.11.cloned.1.call-start = ((), (), s32[]{:S(2)}) async-start(), calls=%async_computation.5 | async-start | bytes 262144 | tf_op jit(solution)/shard_map/psum | solution.py:63
  265.0 7.7 %collective-permute-start.12 = (bf16[2,64,256]{1,2,0:T(8,128)(2,1)S(1)}, bf16[2,64,256]{1,2,0:T(8,128)(2,1)S(1)}, u32[]{:S(2)}, u32[]{:S(2)}) collective-permute-start(bf16[2,64,256]{1,2,0:T(8,128)(2,1)S(1)} %pad_maximum_fusion.2), channel_id=1, source_target_pairs={{0,4},{2,6},{4,8},{6,10},{8,12},{10,14},{12,16},{14,18},{16,20},{1... | collective-permute-start | bytes 196616 | tf_op jit(solution)/shard_map/ppermute | solution.py:12
  268.6 4.1 collective-permute-start.13
  269.8 5.8 %collective-permute-start.14 = (bf16[2,64,256]{1,2,0:T(8,128)(2,1)S(1)}, bf16[2,64,256]{1,2,0:T(8,128)(2,1)S(1)}, u32[]{:S(2)}, u32[]{:S(2)}) collective-permute-start(bf16[2,64,256]{1,2,0:T(8,128)(2,1)S(1)} %pad_maximum_fusion.2), channel_id=1, source_target_pairs={{2,0},{4,2},{6,4},{8,6},{10,8},{12,10},{14,12},{16,14},{18,16},{20... | collective-permute-start | bytes 196616 | tf_op jit(solution)/shard_map/ppermute | solution.py:12
  271.1 11.1 %collective-permute-start.15 = (bf16[2,64,256]{1,2,0:T(8,128)(2,1)S(1)}, bf16[2,64,256]{1,2,0:T(8,128)(2,1)S(1)}, u32[]{:S(2)}, u32[]{:S(2)}) collective-permute-start(bf16[2,64,256]{1,2,0:T(8,128)(2,1)S(1)} %pad_maximum_fusion.2), channel_id=1, source_target_pairs={{4,0},{6,2},{8,4},{10,6},{12,8},{14,10},{16,12},{18,14},{20,16},{2... | collective-permute-start | bytes 196616 | tf_op jit(solution)/shard_map/ppermute | solution.py:12
  351.7 7.5 %collective-permute-start.16 = (bf16[2,64,256]{1,2,0:T(8,128)(2,1)S(1)}, bf16[2,64,256]{1,2,0:T(8,128)(2,1)S(1)}, u32[]{:S(2)}, u32[]{:S(2)}) collective-permute-start(bf16[2,64,256]{1,2,0:T(8,128)(2,1)S(1)} %pad_maximum_fusion.3), channel_id=1, source_target_pairs={{0,4},{2,6},{4,8},{6,10},{8,12},{10,14},{12,16},{14,18},{16,20},{1... | collective-permute-start | bytes 196616 | tf_op jit(solution)/shard_map/ppermute | solution.py:12
  355.2 3.9 collective-permute-start.17
  356.5 5.8 %collective-permute-start.18 = (bf16[2,64,256]{1,2,0:T(8,128)(2,1)S(1)}, bf16[2,64,256]{1,2,0:T(8,128)(2,1)S(1)}, u32[]{:S(2)}, u32[]{:S(2)}) collective-permute-start(bf16[2,64,256]{1,2,0:T(8,128)(2,1)S(1)} %pad_maximum_fusion.3), channel_id=1, source_target_pairs={{2,0},{4,2},{6,4},{8,6},{10,8},{12,10},{14,12},{16,14},{18,16},{20... | collective-permute-start | bytes 196616 | tf_op jit(solution)/shard_map/ppermute | solution.py:12
  357.8 11.1 %collective-permute-start.19 = (bf16[2,64,256]{1,2,0:T(8,128)(2,1)S(1)}, bf16[2,64,256]{1,2,0:T(8,128)(2,1)S(1)}, u32[]{:S(2)}, u32[]{:S(2)}) collective-permute-start(bf16[2,64,256]{1,2,0:T(8,128)(2,1)S(1)} %pad_maximum_fusion.3), channel_id=1, source_target_pairs={{4,0},{6,2},{8,4},{10,6},{12,8},{14,10},{16,12},{18,14},{20,16},{2... | collective-permute-start | bytes 196616 | tf_op jit(solution)/shard_map/ppermute | solution.py:12
Sparse Core Ops, SparseCore 0:
  53.7 34.5 all-reduce.4
  143.4 31.4 all-reduce.6
  230.1 31.4 all-reduce.8
  316.8 31.4 all-reduce.10
where the time goes:
time: 426 us; the launch traced here: 423 us
  waiting for transfers between devices  193 us (45%)
  matrix products  108 us (25%)
  starting transfers between devices  37.2 us (9%)
  local copies, waits for them, and re-layouts  28.8 us (7%)
  other arithmetic  22.6 us (5%)
  blocking collectives  17.6 us (4%)
  between operations  14 us (3%)
    psum x4, waiting for transfers between devices, shards(): prior_obs = lax.psum(partial_value, 'mem')  129 us
    dot_general x32, matrix products, update(): increment = jnp.dot(band_weight, gain, preferred_element_type=jnp.float32)  108 us
    ppermute x20, waiting for transfers between devices, shifted(): return lax.ppermute(block, axis, route)  38.4 us
    ppermute x20, starting transfers between devices, shifted(): return lax.ppermute(block, axis, route)  33.1 us
    all_to_all x1, waiting for transfers between devices, shards(): lax.all_to_all(state, 'mem', split_axis=1, concat_axis=0, tiled=True)  25.6 us
    all_to_all x1, blocking collectives, shards(): lax.all_to_all(columns.astype(jnp.bfloat16), 'mem', split_axis=0, concat_...  17.6 us
    gather x4, local copies, waits for them, and re-layouts, shards(): picked = jnp.take(columns, jnp.clip(local_col, 0, width - 1), axis=1)  11.6 us
    another operation x12, other arithmetic, shards(): band_data = summary_band(jnp.stack([anomaly, weighted]))  8.9 us
  transfers between devices with their start and end apart: 25, of which 13 were waited for; matrix products, arithmetic and copies ran while one was open for 2% of the time, Pallas kernels for 0%

commit v1 on v0

v1 whole, which is shorter than its diff:
```python
import functools

import jax
import jax.numpy as jnp
from jax import lax
from jax.experimental import pallas as pl
from jax.experimental.pallas import tpu as pltpu
from jax.sharding import PartitionSpec as P

RADIUS = 32768
OFFSETS = (-2, -1, 0, 1, 2)
CHUNK = 1024
WINDOW = 64
LANES = 128
FAR_AWAY = 100.0
BF16 = jnp.bfloat16
F32 = jnp.float32


def vmem_call(body, outs, ins, scratch=(), aliases=None, name=None, cost=None):
    return pl.pallas_call(
        body,
        out_shape=outs,
        in_specs=ins,
        out_specs=jax.tree.map(lambda _: pl.BlockSpec(memory_space=pltpu.VMEM), outs),
        scratch_shapes=list(scratch),
        input_output_aliases=aliases or {},
        compiler_params=pltpu.CompilerParams(vmem_limit_bytes=48 << 20),
        cost_estimate=cost,
        name=name,
    )


VM = pl.BlockSpec(memory_space=pltpu.VMEM)
SM = pl.BlockSpec(memory_space=pltpu.SMEM)


def cost(flops, moved):
    return pl.CostEstimate(flops=int(flops), bytes_accessed=int(moved), transcendentals=0)


def prep_body(half_ref, table_ref, x_ref, tracked_ref, sorted_ref, keep_ref, send_ref, mean_ref):
    batches = table_ref.shape[0] // 4
    count = table_ref.shape[1]
    rows = table_ref[...]
    cols = jnp.transpose(rows)
    sub = lax.broadcasted_iota(jnp.int32, (count, count), 0).astype(F32)
    lane = lax.broadcasted_iota(jnp.int32, (count, count), 1).astype(F32)
    del sub
    for b in range(batches):
        key_row = rows[b : b + 1]
        key_col = cols[:, b : b + 1]
        rank_col = jnp.sum(jnp.where(key_row < key_col, 1.0, 0.0), axis=1, keepdims=True)
        hit = rank_col == lane
        for q in range(3):
            piece = cols[:, (q + 1) * batches + b : (q + 1) * batches + b + 1]
            sorted_ref[q * batches + b : q * batches + b + 1, :] = jnp.sum(
                jnp.where(hit, piece, 0.0), axis=0, keepdims=True
            )
    tiles = batches * count // LANES
    members = x_ref.shape[0]
    index = []
    for t in range(tiles):
        b, start = divmod(t * LANES, count)
        pos = sorted_ref[b : b + 1, start : start + LANES].astype(jnp.int32)
        index.append(jnp.broadcast_to(pos, (8, LANES)))
    high = [i // LANES for i in index]
    low = [i % LANES for i in index]

    for group in range(members // 8):
        lines = slice(group * 8, group * 8 + 8)

        def visit(q, found, lines=lines):
            piece = x_ref[lines, pl.ds(pl.multiple_of(q * LANES, LANES), LANES)]
            new = []
            for t in range(tiles):
                picked = jnp.take_along_axis(piece, low[t], axis=1)
                new.append(jnp.where(high[t] == q, picked, found[t]))
            return tuple(new)

        zero = jnp.zeros((8, LANES), F32)
        found = lax.fori_loop(0, x_ref.shape[1] // LANES, visit, (zero,) * tiles, unroll=4)
        for t in range(tiles):
            tracked_ref[lines, t * LANES : (t + 1) * LANES] = found[t]

    half = half_ref[0]
    width = keep_ref.shape[1]
    step = 2048

    def split(i, carry):
        at = pl.ds(pl.multiple_of(i * step, step), step)
        here = pl.ds(pl.multiple_of(half * width + i * step, step), step)
        there = pl.ds(pl.multiple_of((1 - half) * width + i * step, step), step)
        keep_ref[:, at] = x_ref[:, here]
        out = x_ref[:, there]
        mean = jnp.sum(out, axis=0, keepdims=True) * (1.0 / members)
        mean_ref[:, at] = mean
        send_ref[:, at] = (out - mean).astype(BF16)
        return carry

    lax.fori_loop(0, width // step, split, 0)


def summary_rows(prior, values, variances):
    members = prior.shape[0]
    obs_mean = jnp.sum(prior, axis=0, keepdims=True) / members
    anomaly = prior - obs_mean
    spread = jnp.sum(anomaly * anomaly, axis=0, keepdims=True) / (members - 1) + 1e-06
    post_var = 1.0 / (1.0 / spread + 1.0 / variances)
    post_mean = post_var * (obs_mean / spread + values / variances)
    change = post_mean - obs_mean + (jnp.sqrt(post_var / spread) - 1.0) * anomaly
    weighted = change / ((members - 1) * spread)
    return jnp.concatenate([anomaly, weighted], axis=0)


def first_body(own_ref, other_ref, sorted_ref, tracked_ref, pay_ref):
    tracked_ref[: own_ref.shape[0], :] = own_ref[...]
    tracked_ref[own_ref.shape[0] :, :] = other_ref[...]
    count = sorted_ref.shape[1]
    batches = sorted_ref.shape[0] // 3
    prior = tracked_ref[:, :count]
    both = summary_rows(
        prior, sorted_ref[batches : batches + 1, :], sorted_ref[2 * batches : 2 * batches + 1, :]
    )
    pay_ref[:count, :] = jnp.transpose(both).astype(BF16)
    pos = sorted_ref[:batches, :].astype(jnp.int32)
    pieces = [pos[:, i * LANES : (i + 1) * LANES] for i in range(count // LANES)]
    pos = jnp.concatenate(pieces, axis=0)
    pay_ref[count:, :] = jnp.concatenate(
        [(pos // LANES).astype(F32), (pos % LANES).astype(F32)], axis=0
    ).astype(BF16)


def taper_of(position, column):
    near = jnp.maximum(1.0 - jnp.abs(column - position), 0.0)
    return near * near


def step_body(batch, aw0, aw1, aw2, aw3, aw4, pcol_ref, sorted_ref, old_ref, new_ref, pay_ref):
    count = sorted_ref.shape[1]
    batches = sorted_ref.shape[0] // 3
    old = old_ref[:, count:]
    members = old.shape[0]
    mean = jnp.sum(old, axis=0, keepdims=True) * (1.0 / members)
    anom = (old - mean).astype(BF16)
    column = jnp.concatenate([sorted_ref[b : b + 1, :] for b in range(batch, batches)], axis=1)
    column = column * (1.0 / RADIUS)
    total = old
    for o, aw_ref in enumerate((aw0, aw1, aw2, aw3, aw4)):
        at = aw_ref[:count, :members]
        wt = aw_ref[:count, members:]
        cov = jnp.dot(at, anom, preferred_element_type=F32)
        position = pcol_ref[o * count : (o + 1) * count, batch - 1 : batch]
        gain = (taper_of(position, column) * cov).astype(BF16)
        total = total + lax.dot_general(
            wt, gain, (((0,), (0,)), ((), ())), preferred_element_type=F32
        )
    new_ref[...] = total
    both = summary_rows(
        total[:, :count],
        sorted_ref[batches + batch : batches + batch + 1, :],
        sorted_ref[2 * batches + batch : 2 * batches + batch + 1, :],
    )
    pay_ref[...] = jnp.transpose(both).astype(BF16)


def bulk_body(
    batch, first, table_ref, aw0, aw1, aw2, aw3, aw4, pcol_ref, prow_ref, *rest
):
    if first:
        keep_ref, dev_ref, mean_ref, x_ref, w_ref, at_ref, gain_ref = rest
    else:
        old_ref, x_ref, w_ref, at_ref, gain_ref = rest
    aws = (aw0, aw1, aw2, aw3, aw4)
    count = pcol_ref.shape[0] // len(OFFSETS)
    members = x_ref.shape[0]
    total = count * len(OFFSETS)
    for o, aw_ref in enumerate(aws):
        both = jnp.transpose(aw_ref[:count, :].astype(F32))
        w_ref[:, o * count : (o + 1) * count] = both[members:, :]
        at_ref[o * count : (o + 1) * count, :] = aw_ref[:count, :members]
    position_row = prow_ref[batch : batch + 1, :]
    place = lax.broadcasted_iota(jnp.int32, (1, total), 1)
    ramp = (
        lax.broadcasted_iota(jnp.int32, (1, CHUNK), 1).astype(F32) - (CHUNK // 2)
    ) * (1.0 / RADIUS)
    half = table_ref[0]
    chunks = x_ref.shape[1] // CHUNK
    kinds = (0, 2, 4)
    base = half * x_ref.shape[1]

    def entry(c, kind, what):
        return table_ref[8 + ((batch * 3 + kind) * chunks + c) * 2 + what]

    def chunk(c, carry):
        span = pl.ds(pl.multiple_of(c * CHUNK, CHUNK), CHUNK)
        if first:
            x = jnp.concatenate(
                [keep_ref[:, span], dev_ref[:, span].astype(F32) + mean_ref[:, span]], axis=0
            )
        else:
            x = old_ref[:, span]
        mean = jnp.sum(x, axis=0, keepdims=True) * (1.0 / members)
        anom = (x - mean).astype(BF16)
        centre = (base + c * CHUNK + CHUNK // 2).astype(F32) * (1.0 / RADIUS)
        away = centre - position_row
        reach = 1.0 - jnp.abs(away)
        far = reach > 0.0
        starts = []
        for kind, o in enumerate(kinds):
            w0 = pl.multiple_of(entry(c, kind, 0), 16)
            starts.append(w0)
            lo = o * count + w0
            hi = lo + WINDOW * entry(c, kind, 1)
            far = far & ((place < lo) | (place >= hi))
        flat = jnp.where(far, 1.0, 0.0)
        reach = jnp.where(far, reach, 0.0)
        slope = jnp.where(away > 0.0, -2.0, 2.0) * reach
        weights = w_ref[...]
        scaled = jnp.concatenate(
            [
                (weights * (reach * reach)).astype(BF16),
                (weights * slope).astype(BF16),
                (weights * flat).astype(BF16),
            ],
            axis=0,
        )
        poly = jnp.dot(scaled, at_ref[...], preferred_element_type=F32).astype(BF16)
        near = [aws[o][pl.ds(starts[i], WINDOW), :] for i, o in enumerate(kinds)]
        lhs = jnp.concatenate([poly] + [n[:, :members] for n in near], axis=0)
        both = jnp.dot(lhs, anom, preferred_element_type=F32)
        column = centre + ramp
        for i, o in enumerate(kinds):
            position = pcol_ref[pl.ds(o * count + starts[i], WINDOW), batch : batch + 1]
            cov = both[3 * members + i * WINDOW : 3 * members + (i + 1) * WINDOW]
            gain_ref[i * WINDOW : (i + 1) * WINDOW, :] = (
                taper_of(position, column) * cov
            ).astype(BF16)
        wt = jnp.concatenate([n[:, members:] for n in near], axis=0)
        change = lax.dot_general(
            wt, gain_ref[...], (((0,), (0,)), ((), ())), preferred_element_type=F32
        )
        change = change + both[:members]
        change = change + ramp * (
            both[members : 2 * members] + ramp * both[2 * members : 3 * members]
        )
        x_ref[:, span] = x + change

        for i, o in enumerate(kinds):

            def more(n, carry, i=i, o=o):
                start = pl.multiple_of(starts[i] + n * WINDOW, 16)
                aw = aws[o][pl.ds(start, WINDOW), :]
                cov = jnp.dot(aw[:, :members], anom, preferred_element_type=F32)
                position = pcol_ref[pl.ds(o * count + start, WINDOW), batch : batch + 1]
                gain = (taper_of(position, column) * cov).astype(BF16)
                x_ref[:, span] = x_ref[:, span] + lax.dot_general(
                    aw[:, members:], gain, (((0,), (0,)), ((), ())), preferred_element_type=F32
                )
                return carry

            lax.fori_loop(1, entry(c, i, 1), more, 0)
        return carry

    lax.fori_loop(0, chunks, chunk, 0)


def cyclic(block, distance):
    n = lax.axis_size("space")
    return lax.ppermute(block, "space", [((i + distance) % n, i) for i in range(n)])


def band(block):
    return [block if o == 0 else cyclic(block, o) for o in OFFSETS]


def shards(state, obs_index, obs_value, obs_var):
    mem_index = lax.axis_index("mem")
    space_index = lax.axis_index("space")
    blocks = lax.axis_size("space")
    members_here, block_width = state.shape
    members = 2 * members_here
    width = block_width // 2
    batches, count = obs_index.shape
    swap = [(0, 1), (1, 0)]

    local = obs_index - space_index * block_width
    key = local * count + lax.broadcasted_iota(jnp.int32, local.shape, 1)
    table = jnp.concatenate([key.astype(F32), local.astype(F32), obs_value, obs_var], axis=0)
    half = mem_index.astype(jnp.int32).reshape(1)
    shape = jax.ShapeDtypeStruct
    own, srt, keep, send, mean = vmem_call(
        prep_body,
        (
            shape((members_here, batches * count), F32),
            shape((3 * batches, count), F32),
            shape((members_here, width), F32),
            shape((members_here, width), BF16),
            shape((1, width), F32),
        ),
        [SM, VM, VM],
        name="prep",
        cost=cost(1e7, 8e6),
    )(half, table, state)
    other = lax.ppermute(own, "mem", swap)
    dev = lax.ppermute(send, "mem", swap)
    dev_mean = lax.ppermute(mean, "mem", swap)

    tracked, pay = vmem_call(
        first_body,
        (shape((members, batches * count), F32), shape((count + 16, 2 * members), BF16)),
        [VM, VM, VM],
        name="first",
        cost=cost(1e6, 1e6),
    )(own, other, srt)

    aws = band(pay)
    position = jnp.stack([a[count:].astype(jnp.int32) for a in aws])
    position = position[:, :8] * LANES + position[:, 8:]
    position = position.reshape(5, count // LANES, batches, LANES).transpose(0, 2, 1, 3)
    position = position.reshape(5, batches, count)
    offset = jnp.asarray(OFFSETS, jnp.int32)
    source = space_index + offset
    valid = (source >= 0) & (source < blocks)
    relative = (position + (offset * block_width)[:, None, None]).astype(F32) * (1.0 / RADIUS)
    relative = jnp.where(valid[:, None, None], relative, FAR_AWAY)
    prow = relative.transpose(1, 0, 2).reshape(batches, 5 * count)
    pcol = prow.T

    chunks = width // CHUNK
    edges = mem_index * width + CHUNK * lax.iota(jnp.int32, chunks + 1)
    mixed = position[jnp.asarray((0, 2, 4))].transpose(1, 0, 2)
    below = jnp.sum((mixed[:, :, None, :] < edges[None, None, :, None]).astype(jnp.int32), axis=-1)
    k0, k1 = below[:, :, :-1], below[:, :, 1:]
    w0 = jnp.minimum(k0 // 16 * 16, count - WINDOW)
    nw = jnp.maximum((k1 - w0 + WINDOW - 1) // WINDOW, 1)
    w0 = jnp.minimum(w0, count - WINDOW * nw)
    windows = jnp.concatenate(
        [jnp.broadcast_to(half, (8,)), jnp.stack([w0, nw], axis=-1).reshape(-1)]
    )

    x = None
    for batch in range(batches):
        if batch + 1 < batches:
            later = (batches - batch - 1) * count
            tracked, pay = vmem_call(
                functools.partial(step_body, batch + 1),
                (shape((members, later), F32), shape((count, 2 * members), BF16)),
                [VM] * 8,
                name=f"step{batch + 1}",
                cost=cost(2 * 2 * 5 * count * members * later, 1e6),
            )(*aws, pcol, srt, tracked)
            following = band(pay)
        state_args = (keep, dev, dev_mean) if batch == 0 else (x,)
        x = vmem_call(
            functools.partial(bulk_body, batch, batch == 0),
            shape((members, width), F32),
            [SM] + [VM] * (7 + len(state_args)),
            scratch=[
                pltpu.VMEM((members, 5 * count), F32),
                pltpu.VMEM((5 * count, members), BF16),
                pltpu.VMEM((3 * WINDOW, CHUNK), BF16),
            ],
            name=f"bulk{batch}",
            cost=cost(2e9, 6e6),
        )(windows, *aws, pcol, prow, *state_args)
        if batch + 1 < batches:
            aws = following

    mine = x[:members_here]
    theirs = lax.ppermute(x[members_here:].astype(BF16), "mem", swap).astype(F32)
    first = mem_index == 0
    left = jnp.where(first, mine, theirs)
    right = jnp.where(first, theirs, mine)
    return jnp.concatenate([left, right], axis=1)


def solution(mesh):
    placed = (P("mem", "space"), P(None, "space"), P(None, "space"), P(None, "space"))
    return jax.shard_map(
        shards, mesh=mesh, in_specs=placed, out_specs=P("mem", "space"), check_vma=False
    )
```

time: 426 us -> 141 us (0.33)
  waiting for transfers between devices: 193 us -> 33.5 us
  matrix products: 108 us -> 0 us
  Pallas kernels: 0 us -> 53.6 us
  local copies, waits for them, and re-layouts: 28.8 us -> 5.24 us
  other arithmetic: 22.6 us -> 3.79 us
  blocking collectives: 17.6 us -> 0 us
  between operations: 14 us -> 0.28 us
  starting transfers between devices: 37.2 us -> 43.7 us
    psum x4 -> x0, waiting for transfers between devices: 129 us -> none  [shards(): prior_obs = lax.psum(partial_value, 'mem')]
    dot_general x32 -> x0, matrix products: 108 us -> none  [update(): increment = jnp.dot(band_weight, gain, preferred_element_type=jnp.float32)]
    pallas_call x0 -> x9, Pallas kernels: none -> 53.6 us  [the longest x4 27.8 us: shards(): vmem_call(functools.partial(bulk_body, batch, batch == 0), shape((members...]
    all_to_all x1 -> x0, waiting for transfers between devices: 25.6 us -> none  [shards(): lax.all_to_all(state, 'mem', split_axis=1, concat_axis=0, tiled=True)]
    all_to_all x1 -> x0, blocking collectives: 17.6 us -> none  [shards(): lax.all_to_all(columns.astype(jnp.bfloat16), 'mem', split_axis=0, concat_...]
    gather x4 -> x1, local copies, waits for them, and re-layouts: 11.6 us -> 0.57 us  [shards(): mixed = position[jnp.asarray((0, 2, 4))].transpose(1, 0, 2)]
    ppermute x20, starting transfers between devices: 33.1 us -> 43.7 us  [the longest x16 33.7 us: cyclic(): lax.ppermute(block, 'space', [((i + distance) % n, i) for i in range(n)])]
    another operation x12 -> x2, other arithmetic: 8.9 us -> 0.01 us  [the longest x1 0.01 us: shards(): position = jnp.stack([a[count:].astype(jnp.int32) for a in aws])]
  transfers between devices with their start and end apart: 25 -> 20, of which waited for: 13 -> 7; matrix products, arithmetic and copies ran while one was open for 2% -> 2% of each run, Pallas kernels for 0% -> 18%
where the time goes in v1:
time: 141 us; the launch traced here: 140 us
  Pallas kernels  53.6 us (38%)
  starting transfers between devices  43.7 us (31%)
  waiting for transfers between devices  33.5 us (24%)
  local copies, waits for them, and re-layouts  5.24 us (4%)
  other arithmetic  3.79 us (3%)
    ppermute x16, starting transfers between devices, cyclic(): lax.ppermute(block, 'space', [((i + distance) % n, i) for i in range(n)])  33.7 us
    pallas_call x4, Pallas kernels, shards(): vmem_call(functools.partial(bulk_body, batch, batch == 0), shape((members...  27.8 us
    pallas_call x1, Pallas kernels, shards(): vmem_call(prep_body, (shape((members_here, batches * count), F32), shape(...  21.3 us
    ppermute x16, waiting for transfers between devices, cyclic(): lax.ppermute(block, 'space', [((i + distance) % n, i) for i in range(n)])  17.8 us
    ppermute x1, waiting for transfers between devices, shards(): lax.ppermute(x[members_here:].astype(BF16), 'mem', swap).astype(F32)  12.2 us
    ppermute x1, starting transfers between devices, shards(): lax.ppermute(x[members_here:].astype(BF16), 'mem', swap).astype(F32)  4.56 us
    pallas_call x3, Pallas kernels, shards(): vmem_call(functools.partial(step_body, batch + 1), (shape((members, later...  4.43 us
    unnamed x14, local copies, waits for them, and re-layouts  3.81 us
  transfers between devices with their start and end apart: 20, of which 7 were waited for; matrix products, arithmetic and copies ran while one was open for 2% of the time, Pallas kernels for 18%

profile of v1, /device:TPU:0, one launch (start us, length us, event | category | flops | bytes accessed | tf_op | source)
XLA Modules:
  0.0 140.1 jit_solution(12877602635751783557)
XLA Ops:
  0.0 0.7 add_convert_fusion
  0.7 0.7 pad_maximum_fusion.1.table_ref
  1.5 1.6 %copy-done = f32[32,16384]{1,0:T(8,128)S(1)} copy-done((f32[32,16384]{1,0:T(8,128)S(1)}, f32[32,16384]{1,0:T(8,128)}, u32[]{:S(2)}) %copy-start) | copy-done | bytes 2097176
  3.0 21.3 %prep.1 = (f32[32,1024]{1,0:T(8,128)S(1)}, f32[12,256]{1,0:T(8,128)S(1)}, f32[32,8192]{1,0:T(8,128)S(1)}, bf16[32,8192]{1,0:T(8,128)(2,1)S(1)}, f32[1,8192]{1,0:T(1,128)S(1)}) custom-call(s32[1]{0:T(128)} %bitcast.half_ref, f32[16,256]{1,0:T(8,128)S(1)} %pad_maximum_fusion.1.table_ref, f32[32,16384]{1,0:T(8,128)S(1)} %copy-done), custom_call_target="tpu_custom_call" | custom-call | flops 10000000 | bytes 8000000 | tf_op jit(solution)/shard_map/prep/pallas_call | solution.py:292
  24.3 1.0 copy-done.1
  25.3 3.1 %collective-permute-start = (f32[32,1024]{1,0:T(8,128)S(1)}, f32[32,1024]{1,0:T(8,128)S(1)}, u32[]{:S(2)}, u32[]{:S(2)}) collective-permute-start(f32[32,1024]{1,0:T(8,128)S(1)} %get-tuple-element.17.own_ref), channel_id=1, source_target_pairs={{0,1},{1,0},{2,3},{3,2},{4,5},{5,4},{6,7},{7,6},{8,9},{9,8},{10,11... | collective-permute-start | bytes 393224 | tf_op jit(solution)/shard_map/ppermute | solution.py:305
  28.9 3.5 %collective-permute-done.other_ref = f32[32,1024]{1,0:T(8,128)S(1)} collective-permute-done((f32[32,1024]{1,0:T(8,128)S(1)}, f32[32,1024]{1,0:T(8,128)S(1)}, u32[]{:S(2)}, u32[]{:S(2)}) %collective-permute-start) | collective-permute-done | bytes 131104 | tf_op jit(solution)/shard_map/ppermute | solution.py:305
  32.5 2.4 %collective-permute-start.1 = (bf16[272,128]{1,0:T(8,128)(2,1)S(1)}, bf16[272,128]{1,0:T(8,128)(2,1)S(1)}, u32[]{:S(2)}, u32[]{:S(2)}) collective-permute-start(bf16[272,128]{1,0:T(8,128)(2,1)S(1)} %get-tuple-element.19.aw2), channel_id=1, source_target_pairs={{124,0},{126,2},{0,4},{2,6},{4,8},{6,10},{8,12},{10,14},{12,16},{1... | collective-permute-start | bytes 208904 | tf_op jit(solution)/shard_map/ppermute | solution.py:270
  34.8 6.0 %collective-permute-start.3 = (bf16[272,128]{1,0:T(8,128)(2,1)S(1)}, bf16[272,128]{1,0:T(8,128)(2,1)S(1)}, u32[]{:S(2)}, u32[]{:S(2)}) collective-permute-start(bf16[272,128]{1,0:T(8,128)(2,1)S(1)} %get-tuple-element.19.aw2), channel_id=1, source_target_pairs={{2,0},{4,2},{6,4},{8,6},{10,8},{12,10},{14,12},{16,14},{18,16},{20... | collective-permute-start | bytes 208904 | tf_op jit(solution)/shard_map/ppermute | solution.py:270
  40.8 1.8 %collective-permute-start.4 = (bf16[272,128]{1,0:T(8,128)(2,1)S(1)}, bf16[272,128]{1,0:T(8,128)(2,1)S(1)}, u32[]{:S(2)}, u32[]{:S(2)}) collective-permute-start(bf16[272,128]{1,0:T(8,128)(2,1)S(1)} %get-tuple-element.19.aw2), channel_id=1, source_target_pairs={{4,0},{6,2},{8,4},{10,6},{12,8},{14,10},{16,12},{18,14},{20,16},{2... | collective-permute-start | bytes 208904 | tf_op jit(solution)/shard_map/ppermute | solution.py:270
  42.6 9.4 %collective-permute-done.1.aw0 = bf16[272,128]{1,0:T(8,128)(2,1)S(1)} collective-permute-done((bf16[272,128]{1,0:T(8,128)(2,1)S(1)}, bf16[272,128]{1,0:T(8,128)(2,1)S(1)}, u32[]{:S(2)}, u32[]{:S(2)}) %collective-permute-start.1) | collective-permute-done | bytes 69664 | tf_op jit(solution)/shard_map/ppermute | solution.py:270
  52.5 1.5 %step1.1 = (f32[64,768]{1,0:T(8,128)S(1)}, bf16[256,128]{1,0:T(8,128)(2,1)S(1)}) custom-call(bf16[272,128]{1,0:T(8,128)(2,1)S(1)} %collective-permute-done.1.aw0, bf16[272,128]{1,0:T(8,128)(2,1)S(1)} %collective-permute-done.2.aw1, bf16[272,128]{1,0:T(8,128)(2,1)S(1)} %get-tuple-element.19.aw2, bf16[272,128]{1,0:T(8,128)(2,1)S(1)} %collective-permute-done.3.aw3, ...), custom_call_target="tpu_custom_call" | custom-call | flops 251658240 | bytes 1000000 | tf_op jit(solution)/shard_map/step1/pallas_call | solution.py:346
  54.1 6.0 %collective-permute-start.7 = (bf16[256,128]{1,0:T(8,128)(2,1)S(1)}, bf16[256,128]{1,0:T(8,128)(2,1)S(1)}, u32[]{:S(2)}, u32[]{:S(2)}) collective-permute-start(bf16[256,128]{1,0:T(8,128)(2,1)S(1)} %get-tuple-element.21.aw2), channel_id=1, source_target_pairs={{2,0},{4,2},{6,4},{8,6},{10,8},{12,10},{14,12},{16,14},{18,16},{20... | collective-permute-start | bytes 196616 | tf_op jit(solution)/shard_map/ppermute | solution.py:270
  60.1 1.9 %collective-permute-start.8 = (bf16[256,128]{1,0:T(8,128)(2,1)S(1)}, bf16[256,128]{1,0:T(8,128)(2,1)S(1)}, u32[]{:S(2)}, u32[]{:S(2)}) collective-permute-start(bf16[256,128]{1,0:T(8,128)(2,1)S(1)} %get-tuple-element.21.aw2), channel_id=1, source_target_pairs={{4,0},{6,2},{8,4},{10,6},{12,8},{14,10},{16,12},{18,14},{20,16},{2... | collective-permute-start | bytes 196616 | tf_op jit(solution)/shard_map/ppermute | solution.py:270
  62.6 0.6 convert_reduce_fusion
  63.2 1.9 %collective-permute-start.18 = (f32[1,8192]{1,0:T(1,128)S(1)}, f32[1,8192]{1,0:T(1,128)S(1)}, u32[]{:S(2)}, u32[]{:S(2)}) collective-permute-start(f32[1,8192]{1,0:T(1,128)S(1)} %get-tuple-element.28), channel_id=1, source_target_pairs={{0,1},{1,0},{2,3},{3,2},{4,5},{5,4},{6,7},{7,6},{8,9},{9,8},{10,11... | collective-permute-start | bytes 98312 | tf_op jit(solution)/shard_map/ppermute | solution.py:307
  65.2 1.4 step2.1
  66.9 5.9 %collective-permute-start.11 = (bf16[256,128]{1,0:T(8,128)(2,1)S(1)}, bf16[256,128]{1,0:T(8,128)(2,1)S(1)}, u32[]{:S(2)}, u32[]{:S(2)}) collective-permute-start(bf16[256,128]{1,0:T(8,128)(2,1)S(1)} %get-tuple-element.23.aw2), channel_id=1, source_target_pairs={{2,0},{4,2},{6,4},{8,6},{10,8},{12,10},{14,12},{16,14},{18,16},{20... | collective-permute-start | bytes 196616 | tf_op jit(solution)/shard_map/ppermute | solution.py:270
  72.8 1.2 collective-permute-start.12
  75.3 1.8 %collective-permute-done.12.aw4 = bf16[256,128]{1,0:T(8,128)(2,1)S(1)} collective-permute-done((bf16[256,128]{1,0:T(8,128)(2,1)S(1)}, bf16[256,128]{1,0:T(8,128)(2,1)S(1)}, u32[]{:S(2)}, u32[]{:S(2)}) %collective-permute-start.12) | collective-permute-done | bytes 65568 | tf_op jit(solution)/shard_map/ppermute | solution.py:270
  77.1 5.9 %collective-permute-done.9.aw0 = bf16[256,128]{1,0:T(8,128)(2,1)S(1)} collective-permute-done((bf16[256,128]{1,0:T(8,128)(2,1)S(1)}, bf16[256,128]{1,0:T(8,128)(2,1)S(1)}, u32[]{:S(2)}, u32[]{:S(2)}) %collective-permute-start.9) | collective-permute-done | bytes 65568 | tf_op jit(solution)/shard_map/ppermute | solution.py:270
  83.0 1.6 %step3.1 = (f32[64,256]{1,0:T(8,128)}, bf16[256,128]{1,0:T(8,128)(2,1)S(1)}) custom-call(bf16[256,128]{1,0:T(8,128)(2,1)S(1)} %collective-permute-done.9.aw0, bf16[256,128]{1,0:T(8,128)(2,1)S(1)} %collective-permute-done.10.aw1, bf16[256,128]{1,0:T(8,128)(2,1)S(1)} %get-tuple-element.23.aw2, bf16[256,128]{1,0:T(8,128)(2,1)S(1)} %collective-permute-done.11.aw3, ...), custom_call_target="tpu_custom_call" | custom-call | flops 83886080 | bytes 1000000 | tf_op jit(solution)/shard_map/step3/pallas_call | solution.py:346
  84.6 6.0 %collective-permute-start.15 = (bf16[256,128]{1,0:T(8,128)(2,1)S(1)}, bf16[256,128]{1,0:T(8,128)(2,1)S(1)}, u32[]{:S(2)}, u32[]{:S(2)}) collective-permute-start(bf16[256,128]{1,0:T(8,128)(2,1)S(1)} %get-tuple-element.25.aw2), channel_id=1, source_target_pairs={{2,0},{4,2},{6,4},{8,6},{10,8},{12,10},{14,12},{16,14},{18,16},{20... | collective-permute-start | bytes 196616 | tf_op jit(solution)/shard_map/ppermute | solution.py:270
  90.5 2.0 %collective-permute-start.16 = (bf16[256,128]{1,0:T(8,128)(2,1)S(1)}, bf16[256,128]{1,0:T(8,128)(2,1)S(1)}, u32[]{:S(2)}, u32[]{:S(2)}) collective-permute-start(bf16[256,128]{1,0:T(8,128)(2,1)S(1)} %get-tuple-element.25.aw2), channel_id=1, source_target_pairs={{4,0},{6,2},{8,4},{10,6},{12,8},{14,10},{16,12},{18,14},{20,16},{2... | collective-permute-start | bytes 196616 | tf_op jit(solution)/shard_map/ppermute | solution.py:270
  92.6 1.2 copy-done.2
  93.8 6.7 %bulk0.1.rest_0_ = f32[64,8192]{1,0:T(8,128)S(1)} custom-call(s32[200]{0:T(256)S(1)} %concatenate.10.table_ref, bf16[272,128]{1,0:T(8,128)(2,1)S(1)} %collective-permute-done.1.aw0, bf16[272,128]{1,0:T(8,128)(2,1)S(1)} %collective-permute-done.2.aw1, bf16[272,128]{1,0:T(8,128)(2,1)S(1)} %get-tuple-element.19.aw2, ...), custom_call_target="tpu_custom_call" | custom-call | flops 2000000000 | bytes 6000000 | tf_op jit(solution)/shard_map/bulk0/pallas_call | solution.py:355
  100.5 6.7 %bulk1.1.rest_0_ = f32[64,8192]{1,0:T(8,128)S(1)} custom-call(s32[200]{0:T(256)S(1)} %concatenate.10.table_ref, bf16[256,128]{1,0:T(8,128)(2,1)S(1)} %collective-permute-done.5.aw0, bf16[256,128]{1,0:T(8,128)(2,1)S(1)} %collective-permute-done.6.aw1, bf16[256,128]{1,0:T(8,128)(2,1)S(1)} %get-tuple-element.21.aw2, ...), custom_call_target="tpu_custom_call" | custom-call | flops 2000000000 | bytes 6000000 | tf_op jit(solution)/shard_map/bulk1/pallas_call | solution.py:355
  107.3 7.6 %bulk2.1.rest_0_ = f32[64,8192]{1,0:T(8,128)S(1)} custom-call(s32[200]{0:T(256)S(1)} %concatenate.10.table_ref, bf16[256,128]{1,0:T(8,128)(2,1)S(1)} %collective-permute-done.9.aw0, bf16[256,128]{1,0:T(8,128)(2,1)S(1)} %collective-permute-done.10.aw1, bf16[256,128]{1,0:T(8,128)(2,1)S(1)} %get-tuple-element.23.aw2, ...), custom_call_target="tpu_custom_call" | custom-call | flops 2000000000 | bytes 6000000 | tf_op jit(solution)/shard_map/bulk2/pallas_call | solution.py:355
  114.9 6.7 %bulk3.1 = f32[64,8192]{1,0:T(8,128)S(1)} custom-call(s32[200]{0:T(256)S(1)} %concatenate.10.table_ref, bf16[256,128]{1,0:T(8,128)(2,1)S(1)} %collective-permute-done.13.aw0, bf16[256,128]{1,0:T(8,128)(2,1)S(1)} %collective-permute-done.14.aw1, bf16[256,128]{1,0:T(8,128)(2,1)S(1)} %get-tuple-element.25.aw2, ...), custom_call_target="tpu_custom_call" | custom-call | flops 2000000000 | bytes 6000000 | tf_op jit(solution)/shard_map/bulk3/pallas_call | solution.py:355
  121.7 4.6 %collective-permute-start.19 = (bf16[32,8192]{1,0:T(8,128)(2,1)S(1)}, bf16[32,8192]{1,0:T(8,128)(2,1)S(1)}, u32[]{:S(2)}, u32[]{:S(2)}) collective-permute-start(bf16[32,8192]{1,0:T(8,128)(2,1)S(1)} %slice.87), channel_id=1, source_target_pairs={{0,1},{1,0},{2,3},{3,2},{4,5},{5,4},{6,7},{7,6},{8,9},{9,8},{10,11... | collective-permute-start | bytes 1572872 | tf_op jit(solution)/shard_map/ppermute | solution.py:371
  126.3 12.2 %collective-permute-done.19 = bf16[32,8192]{1,0:T(8,128)(2,1)S(1)} collective-permute-done((bf16[32,8192]{1,0:T(8,128)(2,1)S(1)}, bf16[32,8192]{1,0:T(8,128)(2,1)S(1)}, u32[]{:S(2)}, u32[]{:S(2)}) %collective-permute-start.19) | collective-permute-done | bytes 524320 | tf_op jit(solution)/shard_map/ppermute | solution.py:371
  138.6 1.5 %pad_maximum_fusion = f32[32,16384]{1,0:T(8,128)} fusion(f32[32,8192]{1,0:T(8,128)S(1)} %get-tuple-element.32, f32[32,8192]{1,0:T(8,128)S(1)} %get-tuple-element.31), kind=kLoop, calls=%fused_computation.1 | loop fusion | flops 524288 | bytes 4194304 | tf_op jit(solution)/shard_map/concatenate | solution.py:375
  (54 shorter events, 3.5 us)
Async XLA Ops:
  0.0 28.8 %copy-start.4 = (s32[5]{0:T(128)S(1)}, s32[5]{0:T(128)}, u32[]{:S(2)}) copy-start(s32[5]{0:T(128)} %constant.71.clone) | copy-start | bytes 64
  0.0 52.1 %copy-start.3 = (s32[5]{0:T(128)S(1)}, s32[5]{0:T(128)}, u32[]{:S(2)}) copy-start(s32[5]{0:T(128)} %constant.75) | copy-start | bytes 64
  1.4 1.6 %copy-start = (f32[32,16384]{1,0:T(8,128)S(1)}, f32[32,16384]{1,0:T(8,128)}, u32[]{:S(2)}) copy-start(f32[32,16384]{1,0:T(8,128)} %x_ref.1) | copy-start | bytes 6291460
  24.3 1.0 copy-start.1
  25.3 7.0 %collective-permute-start = (f32[32,1024]{1,0:T(8,128)S(1)}, f32[32,1024]{1,0:T(8,128)S(1)}, u32[]{:S(2)}, u32[]{:S(2)}) collective-permute-start(f32[32,1024]{1,0:T(8,128)S(1)} %get-tuple-element.17.own_ref), channel_id=1, source_target_pairs={{0,1},{1,0},{2,3},{3,2},{4,5},{5,4},{6,7},{7,6},{8,9},{9,8},{10,11... | collective-permute-start | bytes 393224 | tf_op jit(solution)/shard_map/ppermute | solution.py:305
  28.4 64.1 %collective-permute-start.17 = (bf16[32,8192]{1,0:T(8,128)(2,1)S(1)}, bf16[32,8192]{1,0:T(8,128)(2,1)S(1)}, u32[]{:S(2)}, u32[]{:S(2)}) collective-permute-start(bf16[32,8192]{1,0:T(8,128)(2,1)S(1)} %get-tuple-element.27), channel_id=1, source_target_pairs={{0,1},{1,0},{2,3},{3,2},{4,5},{5,4},{6,7},{7,6},{8,9},{9,8},{10,11... | collective-permute-start | bytes 1572872 | tf_op jit(solution)/shard_map/ppermute | solution.py:306
  32.5 19.5 %collective-permute-start.1 = (bf16[272,128]{1,0:T(8,128)(2,1)S(1)}, bf16[272,128]{1,0:T(8,128)(2,1)S(1)}, u32[]{:S(2)}, u32[]{:S(2)}) collective-permute-start(bf16[272,128]{1,0:T(8,128)(2,1)S(1)} %get-tuple-element.19.aw2), channel_id=1, source_target_pairs={{124,0},{126,2},{0,4},{2,6},{4,8},{6,10},{8,12},{10,14},{12,16},{1... | collective-permute-start | bytes 208904 | tf_op jit(solution)/shard_map/ppermute | solution.py:270
  34.8 17.2 %collective-permute-start.2 = (bf16[272,128]{1,0:T(8,128)(2,1)S(1)}, bf16[272,128]{1,0:T(8,128)(2,1)S(1)}, u32[]{:S(2)}, u32[]{:S(2)}) collective-permute-start(bf16[272,128]{1,0:T(8,128)(2,1)S(1)} %get-tuple-element.19.aw2), channel_id=1, source_target_pairs={{126,0},{0,2},{2,4},{4,6},{6,8},{8,10},{10,12},{12,14},{14,16},{16... | collective-permute-start | bytes 208904 | tf_op jit(solution)/shard_map/ppermute | solution.py:270
  34.8 17.2 %collective-permute-start.3 = (bf16[272,128]{1,0:T(8,128)(2,1)S(1)}, bf16[272,128]{1,0:T(8,128)(2,1)S(1)}, u32[]{:S(2)}, u32[]{:S(2)}) collective-permute-start(bf16[272,128]{1,0:T(8,128)(2,1)S(1)} %get-tuple-element.19.aw2), channel_id=1, source_target_pairs={{2,0},{4,2},{6,4},{8,6},{10,8},{12,10},{14,12},{16,14},{18,16},{20... | collective-permute-start | bytes 208904 | tf_op jit(solution)/shard_map/ppermute | solution.py:270
  40.8 11.3 %collective-permute-start.4 = (bf16[272,128]{1,0:T(8,128)(2,1)S(1)}, bf16[272,128]{1,0:T(8,128)(2,1)S(1)}, u32[]{:S(2)}, u32[]{:S(2)}) collective-permute-start(bf16[272,128]{1,0:T(8,128)(2,1)S(1)} %get-tuple-element.19.aw2), channel_id=1, source_target_pairs={{4,0},{6,2},{8,4},{10,6},{12,8},{14,10},{16,12},{18,14},{20,16},{2... | collective-permute-start | bytes 208904 | tf_op jit(solution)/shard_map/ppermute | solution.py:270
  54.0 9.3 %collective-permute-start.5 = (bf16[256,128]{1,0:T(8,128)(2,1)S(1)}, bf16[256,128]{1,0:T(8,128)(2,1)S(1)}, u32[]{:S(2)}, u32[]{:S(2)}) collective-permute-start(bf16[256,128]{1,0:T(8,128)(2,1)S(1)} %get-tuple-element.21.aw2), channel_id=1, source_target_pairs={{124,0},{126,2},{0,4},{2,6},{4,8},{6,10},{8,12},{10,14},{12,16},{1... | collective-permute-start | bytes 196616 | tf_op jit(solution)/shard_map/ppermute | solution.py:270
  54.0 11.1 %collective-permute-start.6 = (bf16[256,128]{1,0:T(8,128)(2,1)S(1)}, bf16[256,128]{1,0:T(8,128)(2,1)S(1)}, u32[]{:S(2)}, u32[]{:S(2)}) collective-permute-start(bf16[256,128]{1,0:T(8,128)(2,1)S(1)} %get-tuple-element.21.aw2), channel_id=1, source_target_pairs={{126,0},{0,2},{2,4},{4,6},{6,8},{8,10},{10,12},{12,14},{14,16},{16... | collective-permute-start | bytes 196616 | tf_op jit(solution)/shard_map/ppermute | solution.py:270
  54.1 11.0 %collective-permute-start.7 = (bf16[256,128]{1,0:T(8,128)(2,1)S(1)}, bf16[256,128]{1,0:T(8,128)(2,1)S(1)}, u32[]{:S(2)}, u32[]{:S(2)}) collective-permute-start(bf16[256,128]{1,0:T(8,128)(2,1)S(1)} %get-tuple-element.21.aw2), channel_id=1, source_target_pairs={{2,0},{4,2},{6,4},{8,6},{10,8},{12,10},{14,12},{16,14},{18,16},{20... | collective-permute-start | bytes 196616 | tf_op jit(solution)/shard_map/ppermute | solution.py:270
  60.1 5.1 %collective-permute-start.8 = (bf16[256,128]{1,0:T(8,128)(2,1)S(1)}, bf16[256,128]{1,0:T(8,128)(2,1)S(1)}, u32[]{:S(2)}, u32[]{:S(2)}) collective-permute-start(bf16[256,128]{1,0:T(8,128)(2,1)S(1)} %get-tuple-element.21.aw2), channel_id=1, source_target_pairs={{4,0},{6,2},{8,4},{10,6},{12,8},{14,10},{16,12},{18,14},{20,16},{2... | collective-permute-start | bytes 196616 | tf_op jit(solution)/shard_map/ppermute | solution.py:270
  63.2 27.3 %collective-permute-start.18 = (f32[1,8192]{1,0:T(1,128)S(1)}, f32[1,8192]{1,0:T(1,128)S(1)}, u32[]{:S(2)}, u32[]{:S(2)}) collective-permute-start(f32[1,8192]{1,0:T(1,128)S(1)} %get-tuple-element.28), channel_id=1, source_target_pairs={{0,1},{1,0},{2,3},{3,2},{4,5},{5,4},{6,7},{7,6},{8,9},{9,8},{10,11... | collective-permute-start | bytes 98312 | tf_op jit(solution)/shard_map/ppermute | solution.py:307
  66.5 8.0 %collective-permute-start.10 = (bf16[256,128]{1,0:T(8,128)(2,1)S(1)}, bf16[256,128]{1,0:T(8,128)(2,1)S(1)}, u32[]{:S(2)}, u32[]{:S(2)}) collective-permute-start(bf16[256,128]{1,0:T(8,128)(2,1)S(1)} %get-tuple-element.23.aw2), channel_id=1, source_target_pairs={{126,0},{0,2},{2,4},{4,6},{6,8},{8,10},{10,12},{12,14},{14,16},{16... | collective-permute-start | bytes 196616 | tf_op jit(solution)/shard_map/ppermute | solution.py:270
  66.9 8.4 %collective-permute-start.11 = (bf16[256,128]{1,0:T(8,128)(2,1)S(1)}, bf16[256,128]{1,0:T(8,128)(2,1)S(1)}, u32[]{:S(2)}, u32[]{:S(2)}) collective-permute-start(bf16[256,128]{1,0:T(8,128)(2,1)S(1)} %get-tuple-element.23.aw2), channel_id=1, source_target_pairs={{2,0},{4,2},{6,4},{8,6},{10,8},{12,10},{14,12},{16,14},{18,16},{20... | collective-permute-start | bytes 196616 | tf_op jit(solution)/shard_map/ppermute | solution.py:270
  72.8 4.3 %collective-permute-start.12 = (bf16[256,128]{1,0:T(8,128)(2,1)S(1)}, bf16[256,128]{1,0:T(8,128)(2,1)S(1)}, u32[]{:S(2)}, u32[]{:S(2)}) collective-permute-start(bf16[256,128]{1,0:T(8,128)(2,1)S(1)} %get-tuple-element.23.aw2), channel_id=1, source_target_pairs={{4,0},{6,2},{8,4},{10,6},{12,8},{14,10},{16,12},{18,14},{20,16},{2... | collective-permute-start | bytes 196616 | tf_op jit(solution)/shard_map/ppermute | solution.py:270
  74.5 8.5 %collective-permute-start.9 = (bf16[256,128]{1,0:T(8,128)(2,1)S(1)}, bf16[256,128]{1,0:T(8,128)(2,1)S(1)}, u32[]{:S(2)}, u32[]{:S(2)}) collective-permute-start(bf16[256,128]{1,0:T(8,128)(2,1)S(1)} %get-tuple-element.23.aw2), channel_id=1, source_target_pairs={{124,0},{126,2},{0,4},{2,6},{4,8},{6,10},{8,12},{10,14},{12,16},{1... | collective-permute-start | bytes 196616 | tf_op jit(solution)/shard_map/ppermute | solution.py:270
  84.6 30.3 %collective-permute-start.13 = (bf16[256,128]{1,0:T(8,128)(2,1)S(1)}, bf16[256,128]{1,0:T(8,128)(2,1)S(1)}, u32[]{:S(2)}, u32[]{:S(2)}) collective-permute-start(bf16[256,128]{1,0:T(8,128)(2,1)S(1)} %get-tuple-element.25.aw2), channel_id=1, source_target_pairs={{124,0},{126,2},{0,4},{2,6},{4,8},{6,10},{8,12},{10,14},{12,16},{1... | collective-permute-start | bytes 196616 | tf_op jit(solution)/shard_map/ppermute | solution.py:270
  84.6 30.3 %collective-permute-start.14 = (bf16[256,128]{1,0:T(8,128)(2,1)S(1)}, bf16[256,128]{1,0:T(8,128)(2,1)S(1)}, u32[]{:S(2)}, u32[]{:S(2)}) collective-permute-start(bf16[256,128]{1,0:T(8,128)(2,1)S(1)} %get-tuple-element.25.aw2), channel_id=1, source_target_pairs={{126,0},{0,2},{2,4},{4,6},{6,8},{8,10},{10,12},{12,14},{14,16},{16... | collective-permute-start | bytes 196616 | tf_op jit(solution)/shard_map/ppermute | solution.py:270
  84.6 30.3 %collective-permute-start.15 = (bf16[256,128]{1,0:T(8,128)(2,1)S(1)}, bf16[256,128]{1,0:T(8,128)(2,1)S(1)}, u32[]{:S(2)}, u32[]{:S(2)}) collective-permute-start(bf16[256,128]{1,0:T(8,128)(2,1)S(1)} %get-tuple-element.25.aw2), channel_id=1, source_target_pairs={{2,0},{4,2},{6,4},{8,6},{10,8},{12,10},{14,12},{16,14},{18,16},{20... | collective-permute-start | bytes 196616 | tf_op jit(solution)/shard_map/ppermute | solution.py:270
  90.5 24.4 %collective-permute-start.16 = (bf16[256,128]{1,0:T(8,128)(2,1)S(1)}, bf16[256,128]{1,0:T(8,128)(2,1)S(1)}, u32[]{:S(2)}, u32[]{:S(2)}) collective-permute-start(bf16[256,128]{1,0:T(8,128)(2,1)S(1)} %get-tuple-element.25.aw2), channel_id=1, source_target_pairs={{4,0},{6,2},{8,4},{10,6},{12,8},{14,10},{16,12},{18,14},{20,16},{2... | collective-permute-start | bytes 196616 | tf_op jit(solution)/shard_map/ppermute | solution.py:270
  92.6 1.2 copy-start.2
  121.7 16.8 %collective-permute-start.19 = (bf16[32,8192]{1,0:T(8,128)(2,1)S(1)}, bf16[32,8192]{1,0:T(8,128)(2,1)S(1)}, u32[]{:S(2)}, u32[]{:S(2)}) collective-permute-start(bf16[32,8192]{1,0:T(8,128)(2,1)S(1)} %slice.87), channel_id=1, source_target_pairs={{0,1},{1,0},{2,3},{3,2},{4,5},{5,4},{6,7},{7,6},{8,9},{9,8},{10,11... | collective-permute-start | bytes 1572872 | tf_op jit(solution)/shard_map/ppermute | solution.py:371

commit v2 on v1

v2 whole, which is shorter than its diff:
```python
import functools

import jax
import jax.numpy as jnp
from jax import lax
from jax.experimental import pallas as pl
from jax.experimental.pallas import tpu as pltpu
from jax.sharding import PartitionSpec as P


RADIUS = 32768
OFFSETS = (-2, -1, 0, 1, 2)
CHUNK = 1024
WINDOW = 32
MORE = 128
PAD = 128
UNROLL = 2
PIECES = 2
KINDS = (0, 2, 4)
LANES = 128
FAR_AWAY = 100.0
BF16 = jnp.bfloat16
F32 = jnp.float32


def vmem_call(body, outs, ins, scratch=(), aliases=None, cost=None):
    return pl.pallas_call(
        body,
        out_shape=outs,
        in_specs=ins,
        out_specs=jax.tree.map(lambda _: pl.BlockSpec(memory_space=pltpu.VMEM), outs),
        scratch_shapes=list(scratch),
        input_output_aliases=aliases or {},
        compiler_params=pltpu.CompilerParams(vmem_limit_bytes=48 << 20),
        cost_estimate=cost,
    )


VM = pl.BlockSpec(memory_space=pltpu.VMEM)
SM = pl.BlockSpec(memory_space=pltpu.SMEM)


def cost(flops, moved):
    return pl.CostEstimate(flops=int(flops), bytes_accessed=int(moved), transcendentals=0)


def thirds(x):
    high = x.astype(BF16)
    rest = x - high.astype(F32)
    middle = rest.astype(BF16)
    return high, middle, (rest - middle.astype(F32)).astype(BF16)


def placement(rows, cols, b):
    count = rows.shape[1]
    rank = jnp.sum(
        jnp.where(cols[:, b : b + 1] < rows[b : b + 1], 1.0, 0.0), axis=0, keepdims=True
    )
    place = lax.broadcasted_iota(jnp.int32, (count, count), 0).astype(F32)
    return jnp.where(rank == place, 1.0, 0.0).astype(BF16)


def gather_batch(b, members, rows, cols, hot, index_ref, turned_ref, rows_ref):
    count = rows.shape[1]
    batches = rows.shape[0] // 4
    unroll = 16

    def pick(i, carry):
        for u in range(unroll):
            k = i * unroll + u
            rows_ref[pl.ds(k, 1), :] = turned_ref[pl.ds(index_ref[8 + b * count + k], 1), :]
        return carry

    lax.fori_loop(0, count // unroll, pick, 0)
    group = (cols[:, batches + b : batches + b + 1].astype(jnp.int32) // LANES) % (LANES // members)
    lane = lax.broadcasted_iota(jnp.int32, (count, LANES), 1) // members
    found = jnp.where(lane == group, rows_ref[...], 0.0)
    parts = [jnp.dot(hot, t, preferred_element_type=F32) for t in thirds(found)]
    placed = jnp.transpose((parts[0] + parts[1]) + parts[2])
    total = placed[:members]
    for g in range(1, LANES // members):
        total = total + placed[g * members : (g + 1) * members]
    return total


def prep_body(index_ref, table_ref, x_ref, turned_ref, own_ref, sorted_ref, rows_ref):
    batches = table_ref.shape[0] // 4
    members = x_ref.shape[0]
    groups = LANES // members

    def turn(i, carry):
        at = [
            pl.ds(pl.multiple_of((i * groups + g) * LANES, LANES), LANES) for g in range(groups)
        ]
        block = jnp.concatenate([x_ref[:, a] for a in at], axis=0)
        turned_ref[pl.ds(pl.multiple_of(i * LANES, LANES), LANES), :] = jnp.transpose(block)
        return carry

    lax.fori_loop(0, x_ref.shape[1] // (groups * LANES), turn, 0, unroll=2)
    rows = table_ref[...]
    cols = jnp.transpose(rows)
    for b in range(batches):
        hot = placement(rows, cols, b)
        values = jnp.concatenate([rows[(q + 1) * batches + b : (q + 1) * batches + b + 1] for q in range(3)], axis=0)
        parts = [
            lax.dot_general(t, hot, (((1,), (1,)), ((), ())), preferred_element_type=F32)
            for t in thirds(values)
        ]
        ordered = (parts[0] + parts[1]) + parts[2]
        for q in range(3):
            sorted_ref[q * batches + b : q * batches + b + 1, :] = ordered[q : q + 1]
        if b == 0:
            own_ref[...] = gather_batch(
                b, members, rows, cols, hot, index_ref, turned_ref, rows_ref
            )


def prep_rest_body(
    index_ref, table_ref, x_ref, turned_ref, own_ref, keep_ref, send_ref, mean_ref, rows_ref
):
    batches = table_ref.shape[0] // 4
    count = table_ref.shape[1]
    members = x_ref.shape[0]
    half = index_ref[0]
    width = keep_ref.shape[1]
    step = 2048

    def split(i, carry):
        at = pl.ds(pl.multiple_of(i * step, step), step)
        here = pl.ds(pl.multiple_of(half * width + i * step, step), step)
        there = pl.ds(pl.multiple_of((1 - half) * width + i * step, step), step)
        keep_ref[:, at] = x_ref[:, here]
        out = x_ref[:, there]
        mean = jnp.sum(out, axis=0, keepdims=True) * (1.0 / members)
        mean_ref[:, at] = mean
        send_ref[:, at] = (out - mean).astype(BF16)
        return carry

    lax.fori_loop(0, width // step, split, 0)
    rows = table_ref[...]
    cols = jnp.transpose(rows)
    for b in range(1, batches):
        hot = placement(rows, cols, b)
        own_ref[:, (b - 1) * count : b * count] = gather_batch(
            b, members, rows, cols, hot, index_ref, turned_ref, rows_ref
        )


def summary_rows(prior, values, variances):
    members = prior.shape[0]
    obs_mean = jnp.sum(prior, axis=0, keepdims=True) / members
    anomaly = prior - obs_mean
    spread = jnp.sum(anomaly * anomaly, axis=0, keepdims=True) / (members - 1) + 1e-06
    post_var = 1.0 / (1.0 / spread + 1.0 / variances)
    post_mean = post_var * (obs_mean / spread + values / variances)
    change = post_mean - obs_mean + (jnp.sqrt(post_var / spread) - 1.0) * anomaly
    weighted = change / ((members - 1) * spread)
    return jnp.concatenate([anomaly, weighted], axis=0)


def first_body(own_ref, other_ref, sorted_ref, pay_ref):
    count = sorted_ref.shape[1]
    batches = sorted_ref.shape[0] // 3
    prior = jnp.concatenate([own_ref[...], other_ref[...]], axis=0)
    both = summary_rows(
        prior, sorted_ref[batches : batches + 1, :], sorted_ref[2 * batches : 2 * batches + 1, :]
    )
    pay_ref[:count, :] = jnp.transpose(both).astype(BF16)
    pos = sorted_ref[:batches, :].astype(jnp.int32)
    pieces = [pos[:, i * LANES : (i + 1) * LANES] for i in range(count // LANES)]
    pos = jnp.concatenate(pieces, axis=0)
    pay_ref[count:, :] = jnp.concatenate(
        [(pos // LANES).astype(F32), (pos % LANES).astype(F32)], axis=0
    ).astype(BF16)


def taper_of(position, column):
    near = jnp.maximum(1.0 - jnp.abs(column - position), 0.0)
    return near * near


def step_body(batch, aw0, aw1, aw2, aw3, aw4, pcol_ref, sorted_ref, *rest):
    count = sorted_ref.shape[1]
    batches = sorted_ref.shape[0] // 3
    new_ref, pay_ref = rest[-2:]
    if batch == 1:
        old = jnp.concatenate([rest[0][...], rest[1][...]], axis=0)
    else:
        old = rest[0][:, count:]
    members = old.shape[0]
    mean = jnp.sum(old, axis=0, keepdims=True) * (1.0 / members)
    anom = (old - mean).astype(BF16)
    column = jnp.concatenate([sorted_ref[b : b + 1, :] for b in range(batch, batches)], axis=1)
    column = column * (1.0 / RADIUS)
    total = old
    for o, aw_ref in enumerate((aw0, aw1, aw2, aw3, aw4)):
        at = aw_ref[:count, :members]
        wt = aw_ref[:count, members:]
        cov = jnp.dot(at, anom, preferred_element_type=F32)
        position = pcol_ref[o * count : (o + 1) * count, batch - 1 : batch]
        gain = (taper_of(position, column) * cov).astype(BF16)
        total = total + lax.dot_general(
            wt, gain, (((0,), (0,)), ((), ())), preferred_element_type=F32
        )
    new_ref[...] = total
    both = summary_rows(
        total[:, :count],
        sorted_ref[batches + batch : batches + batch + 1, :],
        sorted_ref[2 * batches + batch : 2 * batches + batch + 1, :],
    )
    pay_ref[...] = jnp.transpose(both).astype(BF16)


def bulk_body(
    batch, first_chunk, n_in, n_out, table_ref, aw0, aw1, aw2, aw3, aw4, pcol_ref, prow_ref, *rest
):
    first = n_in == 3
    last = n_out == 2
    ins, outs, scratch = rest[:n_in], rest[n_in : n_in + n_out], rest[n_in + n_out :]
    poly_ref, band_ref, place_ref, gain_ref, part_ref, total_scratch = scratch
    aws = (aw0, aw1, aw2, aw3, aw4)
    count = pcol_ref.shape[0] // len(OFFSETS)
    members = aw0.shape[1] // 2
    padded = count + PAD
    half = table_ref[0]
    chunks = outs[0].shape[1] // CHUNK
    all_chunks = table_ref[1]
    width = all_chunks * CHUNK
    base = half * width
    middle = (base + width // 2).astype(F32) * (1.0 / RADIUS)
    position_row = prow_ref[batch : batch + 1, :]

    def entry(c, kind, what):
        return table_ref[8 + ((batch * len(KINDS) + kind) * all_chunks + c) * 2 + what]

    def centre_of(c):
        return (base + c * CHUNK + CHUNK // 2).astype(F32) * (1.0 / RADIUS)

    def weights_of(o):
        return jnp.transpose(aws[o][:count, :].astype(F32))[members:, :]

    def terms(away, reach, far):
        flat = jnp.where(far, 1.0, 0.0)
        reach = jnp.where(far, reach, 0.0)
        slope = jnp.where(away > 0.0, -2.0, 2.0) * reach
        return reach * reach, slope, flat

    wide = None
    for o in (1, 3):
        weights = weights_of(o)
        away = middle - position_row[:, o * count : (o + 1) * count]
        scaled = jnp.concatenate(
            [
                (weights * k).astype(BF16)
                for k in terms(away, 1.0 - jnp.abs(away), jnp.abs(away) < 0.5 * FAR_AWAY)
            ],
            axis=0,
        )
        part = jnp.dot(scaled, aws[o][:count, :members], preferred_element_type=F32)
        wide = part if wide is None else wide + part
    wide = [wide[r * members : (r + 1) * members, :] for r in range(3)]

    order = lax.broadcasted_iota(jnp.int32, (1, count), 1)
    for n in range(chunks):
        shift = centre_of(first_chunk + n) - middle
        part_ref[n * 3 * members : (n + 1) * 3 * members, :] = jnp.concatenate(
            [
                wide[0] + shift * (wide[1] + shift * wide[2]),
                wide[1] + (2.0 * shift) * wide[2],
                wide[2],
            ],
            axis=0,
        )
    for i, o in enumerate(KINDS):
        band_ref[i * padded : i * padded + count, :] = aws[o][:count, :]
        band_ref[i * padded + count : (i + 1) * padded, :] = jnp.zeros((PAD, 2 * members), BF16)
        at = pcol_ref[o * count : (o + 1) * count, batch : batch + 1]
        at = at + (1.0, 0.0, -1.0)[i]
        place_ref[i * padded : i * padded + count, :] = at
        place_ref[i * padded + count : (i + 1) * padded, :] = jnp.zeros((PAD, 1), F32)
        weights = weights_of(o)
        row = position_row[:, o * count : (o + 1) * count]
        scaled = []
        for n in range(chunks):
            c = first_chunk + n
            away = centre_of(c) - row
            reach = 1.0 - jnp.abs(away)
            low = entry(c, i, 0)
            high = low + WINDOW + MORE * entry(c, i, 1)
            far = (reach > 0.0) & ((order < low) | (order >= high))
            scaled += [(weights * k).astype(BF16) for k in terms(away, reach, far)]
        part = jnp.dot(
            jnp.concatenate(scaled, axis=0), aws[o][:count, :members], preferred_element_type=F32
        )
        if i + 1 < len(KINDS):
            part_ref[...] = part_ref[...] + part
        else:
            poly_ref[...] = (part_ref[...] + part).astype(BF16)

    ramp = (
        lax.broadcasted_iota(jnp.int32, (1, CHUNK), 1).astype(F32) - (CHUNK // 2)
    ) * (1.0 / RADIUS)

    def taper(kind, position, column):
        if kind == 0:
            near = jnp.maximum(position - column, 0.0)
        elif kind == 1:
            near = 1.0 - jnp.abs(column - position)
        else:
            near = jnp.maximum(column - position, 0.0)
        return near * near

    total_ref = total_scratch if last else outs[0]

    def one(n, slot):
        c = first_chunk + n
        local = pl.ds(pl.multiple_of(n * CHUNK, CHUNK), CHUNK)
        span = pl.ds(pl.multiple_of(c * CHUNK, CHUNK), CHUNK)
        if first:
            x = jnp.concatenate(
                [ins[0][:, span], ins[1][:, span].astype(F32) + ins[2][:, span]], axis=0
            )
        else:
            x = ins[0][:, span]
        mean = jnp.sum(x, axis=0, keepdims=True) * (1.0 / members)
        anom = (x - mean).astype(BF16)
        column = centre_of(c) + ramp
        starts = [pl.multiple_of(entry(c, i, 0), 16) for i in range(len(KINDS))]
        near = [band_ref[pl.ds(i * padded + starts[i], WINDOW), :] for i in range(len(KINDS))]
        poly = poly_ref[pl.ds(pl.multiple_of(n * 3 * members, 3 * members), 3 * members), :]
        lhs = jnp.concatenate([poly] + [q[:, :members] for q in near], axis=0)
        both = jnp.dot(lhs, anom, preferred_element_type=F32)
        for i in range(len(KINDS)):
            position = place_ref[pl.ds(i * padded + starts[i], WINDOW), :]
            cov = both[3 * members + i * WINDOW : 3 * members + (i + 1) * WINDOW]
            row = (slot * len(KINDS) + i) * WINDOW
            gain_ref[row : row + WINDOW, :] = (taper(i, position, column) * cov).astype(BF16)
        wt = jnp.concatenate([q[:, members:] for q in near], axis=0)
        row = slot * len(KINDS) * WINDOW
        change = lax.dot_general(
            wt,
            gain_ref[row : row + len(KINDS) * WINDOW, :],
            (((0,), (0,)), ((), ())),
            preferred_element_type=F32,
        )
        change = change + both[:members]
        change = change + ramp * (
            both[members : 2 * members] + ramp * both[2 * members : 3 * members]
        )
        return x + change, anom, column, starts, c, local

    def extend(anom, column, starts, c, local):
        for i in range(len(KINDS)):

            def more(k, carry, i=i):
                start = pl.multiple_of(i * padded + starts[i] + WINDOW + k * MORE, 16)
                aw = band_ref[pl.ds(start, MORE), :]
                cov = jnp.dot(aw[:, :members], anom, preferred_element_type=F32)
                gain = (taper(i, place_ref[pl.ds(start, MORE), :], column) * cov).astype(BF16)
                total_ref[:, local] = total_ref[:, local] + lax.dot_general(
                    aw[:, members:], gain, (((0,), (0,)), ((), ())), preferred_element_type=F32
                )
                return carry

            lax.fori_loop(0, entry(c, i, 1), more, 0)

    def pair(m, carry):
        found = [one(m * UNROLL + slot, slot) for slot in range(UNROLL)]
        for total, anom, column, starts, c, local in found:
            total_ref[:, local] = total
        for total, anom, column, starts, c, local in found:
            extend(anom, column, starts, c, local)
            if last:
                outs[0][:, local] = total_ref[: members // 2, local]
                outs[1][:, local] = total_ref[members // 2 :, local].astype(BF16)
        return carry

    lax.fori_loop(0, chunks // UNROLL, pair, 0)


def cyclic(block, distance):
    n = lax.axis_size("space")
    return lax.ppermute(block, "space", [((i + distance) % n, i) for i in range(n)])


def band(block):
    pieces = []
    for o in OFFSETS:
        pieces.append(block if o == 0 else cyclic(block, o))
    return pieces


def traded(block):
    return lax.ppermute(block, "mem", [(0, 1), (1, 0)])


def shards(state, obs_index, obs_value, obs_var):
    mem_index = lax.axis_index("mem")
    space_index = lax.axis_index("space")
    blocks = lax.axis_size("space")
    members_here, block_width = state.shape
    members = 2 * members_here
    width = block_width // 2
    batches, count = obs_index.shape

    local = obs_index - space_index * block_width
    key = local * count + lax.broadcasted_iota(jnp.int32, local.shape, 1)
    table = jnp.concatenate([key.astype(F32), local.astype(F32), obs_value, obs_var], axis=0)
    half = mem_index.astype(jnp.int32).reshape(1)
    groups = LANES // members_here
    place = local // (groups * LANES) * LANES + local % LANES
    index = jnp.concatenate([jnp.broadcast_to(half, (8,)), place.reshape(-1)])
    shape = jax.ShapeDtypeStruct
    turned, own0, srt = vmem_call(
        prep_body,
        (
            shape((block_width // groups, LANES), F32),
            shape((members_here, count), F32),
            shape((3 * batches, count), F32),
        ),
        [SM, VM, VM],
        scratch=[pltpu.VMEM((count, LANES), F32)],
        cost=cost(1e7, 6e6),
    )(index, table, state)
    other0 = traded(own0)
    own, keep, send, mean = vmem_call(
        prep_rest_body,
        (
            shape((members_here, (batches - 1) * count), F32),
            shape((members_here, width), F32),
            shape((members_here, width), BF16),
            shape((1, width), F32),
        ),
        [SM, VM, VM, VM],
        scratch=[pltpu.VMEM((count, LANES), F32)],
        cost=cost(1e7, 6e6),
    )(index, table, state, turned)
    other = traded(own)
    dev = traded(send)
    dev_mean = traded(mean)

    pay = vmem_call(
        first_body, shape((count + 16, 2 * members), BF16), [VM, VM, VM], cost=cost(1e6, 1e6)
    )(own0, other0, srt)

    aws = band(pay)
    position = jnp.stack([a[count:].astype(jnp.int32) for a in aws])
    position = position[:, :8] * LANES + position[:, 8:]
    position = position.reshape(5, count // LANES, batches, LANES).transpose(0, 2, 1, 3)
    position = position.reshape(5, batches, count)
    offset = jnp.asarray(OFFSETS, jnp.int32)
    source = space_index + offset
    valid = (source >= 0) & (source < blocks)
    relative = (position + (offset * block_width)[:, None, None]).astype(F32) * (1.0 / RADIUS)
    beyond = jnp.where(offset < 0, -FAR_AWAY, FAR_AWAY)
    relative = jnp.where(valid[:, None, None], relative, beyond[:, None, None])
    prow = relative.transpose(1, 0, 2).reshape(batches, 5 * count)
    pcol = prow.T

    chunks = width // CHUNK
    edges = mem_index * width + CHUNK * lax.iota(jnp.int32, chunks + 1)
    mixed = position[jnp.asarray(KINDS)].transpose(1, 0, 2)
    below = jnp.sum((mixed[:, :, None, :] < edges[None, None, :, None]).astype(jnp.int32), axis=-1)
    k0, k1 = below[:, :, :-1], below[:, :, 1:]
    w0 = k0 // 16 * 16
    more = jnp.maximum((k1 - w0 - WINDOW + MORE - 1) // MORE, 0)
    head = jnp.where(lax.iota(jnp.int32, 8) == 1, chunks, half)
    windows = jnp.concatenate([head, jnp.stack([w0, more], axis=-1).reshape(-1)])

    def bulk(batch, state_args, outs, first_chunk):
        kinds = len(KINDS)
        here = outs[0].shape[1] // CHUNK
        return vmem_call(
            functools.partial(bulk_body, batch, first_chunk, len(state_args), len(outs)),
            outs,
            [SM] + [VM] * (7 + len(state_args)),
            scratch=[
                pltpu.VMEM((here * 3 * members, members), BF16),
                pltpu.VMEM((kinds * (count + PAD), 2 * members), BF16),
                pltpu.VMEM((kinds * (count + PAD), 1), F32),
                pltpu.VMEM((UNROLL * kinds * WINDOW, CHUNK), BF16),
                pltpu.VMEM((here * 3 * members, members), F32),
                pltpu.VMEM((members, outs[0].shape[1] if len(outs) == 2 else LANES), F32),
            ],
            cost=cost(2e9, 6e6),
        )(windows, *aws, pcol, prow, *state_args)

    x = None
    tracked = (own, other)
    for batch in range(batches - 1):
        later = (batches - batch - 1) * count
        extra = tracked
        new, pay = vmem_call(
            functools.partial(step_body, batch + 1),
            (shape((members, later), F32), shape((count, 2 * members), BF16)),
            [VM] * (7 + len(extra)),
            cost=cost(2 * 2 * 5 * count * members * later, 1e6),
        )(*aws, pcol, srt, *extra)
        tracked = (new,)
        following = band(pay)
        state_args = (keep, dev, dev_mean) if batch == 0 else (x,)
        (x,) = bulk(batch, state_args, (shape((members, width), F32),), 0)
        aws = following

    pieces = PIECES
    mine, theirs = [], []
    for piece in range(pieces):
        size = width // pieces
        kept, sent = bulk(
            batches - 1,
            (x,),
            (shape((members_here, size), F32), shape((members_here, size), BF16)),
            piece * size // CHUNK,
        )
        mine.append(kept)
        theirs.append(traded(sent))
    mine = jnp.concatenate(mine, axis=1)
    theirs = jnp.concatenate(theirs, axis=1).astype(F32)
    first = mem_index == 0
    left = jnp.where(first, mine, theirs)
    right = jnp.where(first, theirs, mine)
    return jnp.concatenate([left, right], axis=1)


def solution(mesh):
    placed = (P("mem", "space"), P(None, "space"), P(None, "space"), P(None, "space"))
    return jax.shard_map(
        shards, mesh=mesh, in_specs=placed, out_specs=P("mem", "space"), check_vma=False
    )
```

time: 141 us -> 123 us (0.87)
  Pallas kernels: 53.6 us -> 36.8 us
  waiting for transfers between devices: 33.5 us -> 35.8 us
  local copies, waits for them, and re-layouts: 5.24 us -> 3.07 us
    pallas_call x6 -> x8, Pallas kernels: 49.2 us -> 32.3 us  [the longest x5 25.1 us: bulk(): vmem_call(functools.partial(bulk_body, batch, first_chunk, len(state_args...]
    ppermute x16, waiting for transfers between devices: 17.8 us -> 24.5 us  [cyclic(): lax.ppermute(block, 'space', [((i + distance) % n, i) for i in range(n)])]
    ppermute x16, starting transfers between devices: 33.7 us -> 29.3 us  [cyclic(): lax.ppermute(block, 'space', [((i + distance) % n, i) for i in range(n)])]
    ppermute x4 -> x6, waiting for transfers between devices: 15.7 us -> 11.3 us  [traded(): return lax.ppermute(block, 'mem', [(0, 1), (1, 0)])]
    ppermute x4 -> x6, starting transfers between devices: 10 us -> 13.2 us  [traded(): return lax.ppermute(block, 'mem', [(0, 1), (1, 0)])]
    unnamed x14, local copies, waits for them, and re-layouts: 3.81 us -> 1.66 us
  transfers between devices with their start and end apart: 20 -> 22, of which waited for: 7 -> 6; matrix products, arithmetic and copies ran while one was open for 2% -> 2% of each run, Pallas kernels for 18% -> 21%
where the time goes in v2:
time: 123 us; the launch traced here: 122 us
  starting transfers between devices  42.5 us (35%)
  Pallas kernels  36.8 us (30%)
  waiting for transfers between devices  35.8 us (29%)
  other arithmetic  3.86 us (3%)
  local copies, waits for them, and re-layouts  3.07 us (2%)
    ppermute x16, starting transfers between devices, cyclic(): lax.ppermute(block, 'space', [((i + distance) % n, i) for i in range(n)])  29.3 us
    pallas_call x5, Pallas kernels, bulk(): vmem_call(functools.partial(bulk_body, batch, first_chunk, len(state_args...  25.1 us
    ppermute x16, waiting for transfers between devices, cyclic(): lax.ppermute(block, 'space', [((i + distance) % n, i) for i in range(n)])  24.5 us
    ppermute x6, starting transfers between devices, traded(): return lax.ppermute(block, 'mem', [(0, 1), (1, 0)])  13.2 us
    ppermute x6, waiting for transfers between devices, traded(): return lax.ppermute(block, 'mem', [(0, 1), (1, 0)])  11.3 us
    pallas_call x3, Pallas kernels, shards(): vmem_call(functools.partial(step_body, batch + 1), (shape((members, later...  4.44 us
    pallas_call x1, Pallas kernels, shards(): vmem_call(prep_body, (shape((block_width // groups, LANES), F32), shape((...  3.74 us
    pallas_call x1, Pallas kernels, shards(): vmem_call(prep_rest_body, (shape((members_here, (batches - 1) * count), F...  3.31 us
  transfers between devices with their start and end apart: 22, of which 6 were waited for; matrix products, arithmetic and copies ran while one was open for 2% of the time, Pallas kernels for 21%

profile of v2, /device:TPU:0, one launch (start us, length us, event | category | flops | bytes accessed | tf_op | source)
XLA Modules:
  0.0 122.3 jit_solution(3726330640454433799)
XLA Ops:
  0.0 0.7 add_convert_fusion
  0.8 0.7 pad_maximum_fusion.2.table_ref
  1.5 1.6 %copy-done = f32[32,16384]{1,0:T(8,128)S(1)} copy-done((f32[32,16384]{1,0:T(8,128)S(1)}, f32[32,16384]{1,0:T(8,128)}, u32[]{:S(2)}) %copy-start) | copy-done | bytes 2097176
  3.1 3.7 %shard_map.64 = (f32[4096,128]{1,0:T(8,128)S(1)}, f32[32,256]{1,0:T(8,128)S(1)}, f32[12,256]{1,0:T(8,128)S(1)}) custom-call(s32[1032]{0:T(1024)S(1)} %concatenate.18.index_ref, f32[16,256]{1,0:T(8,128)S(1)} %pad_maximum_fusion.2.table_ref, f32[32,16384]{1,0:T(8,128)S(1)} %copy-done), custom_call_target="tpu_custom_call" | custom-call | flops 10000000 | bytes 6000000 | tf_op jit(solution)/shard_map/pallas_call | solution.py:414
  6.8 3.2 %collective-permute-start = (f32[32,256]{1,0:T(8,128)S(1)}, f32[32,256]{1,0:T(8,128)S(1)}, u32[]{:S(2)}, u32[]{:S(2)}) collective-permute-start(f32[32,256]{1,0:T(8,128)S(1)} %get-tuple-element.21.own_ref), channel_id=1, source_target_pairs={{0,1},{1,0},{2,3},{3,2},{4,5},{5,4},{6,7},{7,6},{8,9},{9,8},{10,11... | collective-permute-start | bytes 98312 | tf_op jit(solution)/shard_map/ppermute | solution.py:394
  10.0 3.3 %shard_map.66 = (f32[32,768]{1,0:T(8,128)S(1)}, f32[32,8192]{1,0:T(8,128)S(1)}, bf16[32,8192]{1,0:T(8,128)(2,1)S(1)}, f32[1,8192]{1,0:T(1,128)S(1)}) custom-call(s32[1032]{0:T(1024)S(1)} %concatenate.18.index_ref, f32[16,256]{1,0:T(8,128)S(1)} %pad_maximum_fusion.2.table_ref, f32[32,16384]{1,0:T(8,128)S(1)} %copy-done, ...), custom_call_target="tpu_custom_call" | custom-call | flops 10000000 | bytes 6000000 | tf_op jit(solution)/shard_map/pallas_call | solution.py:426
  13.8 3.1 %collective-permute-start.5 = (f32[32,768]{1,0:T(8,128)S(1)}, f32[32,768]{1,0:T(8,128)S(1)}, u32[]{:S(2)}, u32[]{:S(2)}) collective-permute-start(f32[32,768]{1,0:T(8,128)S(1)} %get-tuple-element.24.rest_0_), channel_id=1, source_target_pairs={{0,1},{1,0},{2,3},{3,2},{4,5},{5,4},{6,7},{7,6},{8,9},{9,8},{10,11... | collective-permute-start | bytes 294920 | tf_op jit(solution)/shard_map/ppermute | solution.py:394
  17.2 0.7 collective-permute-start.1
  17.8 6.0 %collective-permute-start.3 = (bf16[272,128]{1,0:T(8,128)(2,1)S(1)}, bf16[272,128]{1,0:T(8,128)(2,1)S(1)}, u32[]{:S(2)}, u32[]{:S(2)}) collective-permute-start(bf16[272,128]{1,0:T(8,128)(2,1)S(1)} %shard_map.65.aw2), channel_id=1, source_target_pairs={{2,0},{4,2},{6,4},{8,6},{10,8},{12,10},{14,12},{16,14},{18,16},{20... | collective-permute-start | bytes 208904 | tf_op jit(solution)/shard_map/ppermute | solution.py:383
  23.8 13.3 %collective-permute-done.1.aw0 = bf16[272,128]{1,0:T(8,128)(2,1)S(1)} collective-permute-done((bf16[272,128]{1,0:T(8,128)(2,1)S(1)}, bf16[272,128]{1,0:T(8,128)(2,1)S(1)}, u32[]{:S(2)}, u32[]{:S(2)}) %collective-permute-start.1) | collective-permute-done | bytes 69664 | tf_op jit(solution)/shard_map/ppermute | solution.py:383
  37.6 4.4 %collective-permute-done.4.aw4 = bf16[272,128]{1,0:T(8,128)(2,1)S(1)} collective-permute-done((bf16[272,128]{1,0:T(8,128)(2,1)S(1)}, bf16[272,128]{1,0:T(8,128)(2,1)S(1)}, u32[]{:S(2)}, u32[]{:S(2)}) %collective-permute-start.4) | collective-permute-done | bytes 69664 | tf_op jit(solution)/shard_map/ppermute | solution.py:383
  42.5 1.5 %shard_map.67 = (f32[64,768]{1,0:T(8,128)S(1)}, bf16[256,128]{1,0:T(8,128)(2,1)S(1)}) custom-call(bf16[272,128]{1,0:T(8,128)(2,1)S(1)} %collective-permute-done.1.aw0, bf16[272,128]{1,0:T(8,128)(2,1)S(1)} %collective-permute-done.2.aw1, bf16[272,128]{1,0:T(8,128)(2,1)S(1)} %shard_map.65.aw2, bf16[272,128]{1,0:T(8,128)(2,1)S(1)} %collective-permute-done.3.aw3, ...), custom_call_target="tpu_custom_call" | custom-call | flops 251658240 | bytes 1000000 | tf_op jit(solution)/shard_map/pallas_call | solution.py:493
  44.1 6.0 %collective-permute-start.8 = (bf16[256,128]{1,0:T(8,128)(2,1)S(1)}, bf16[256,128]{1,0:T(8,128)(2,1)S(1)}, u32[]{:S(2)}, u32[]{:S(2)}) collective-permute-start(bf16[256,128]{1,0:T(8,128)(2,1)S(1)} %get-tuple-element.25.aw2), channel_id=1, source_target_pairs={{2,0},{4,2},{6,4},{8,6},{10,8},{12,10},{14,12},{16,14},{18,16},{20... | collective-permute-start | bytes 196616 | tf_op jit(solution)/shard_map/ppermute | solution.py:383
  50.1 1.9 %collective-permute-start.9 = (bf16[256,128]{1,0:T(8,128)(2,1)S(1)}, bf16[256,128]{1,0:T(8,128)(2,1)S(1)}, u32[]{:S(2)}, u32[]{:S(2)}) collective-permute-start(bf16[256,128]{1,0:T(8,128)(2,1)S(1)} %get-tuple-element.25.aw2), channel_id=1, source_target_pairs={{4,0},{6,2},{8,4},{10,6},{12,8},{14,10},{16,12},{18,14},{20,16},{2... | collective-permute-start | bytes 196616 | tf_op jit(solution)/shard_map/ppermute | solution.py:383
  53.4 2.8 %collective-permute-start.19 = (f32[1,8192]{1,0:T(1,128)S(1)}, f32[1,8192]{1,0:T(1,128)S(1)}, u32[]{:S(2)}, u32[]{:S(2)}) collective-permute-start(f32[1,8192]{1,0:T(1,128)S(1)} %get-tuple-element.32), channel_id=1, source_target_pairs={{0,1},{1,0},{2,3},{3,2},{4,5},{5,4},{6,7},{7,6},{8,9},{9,8},{10,11... | collective-permute-start | bytes 98312 | tf_op jit(solution)/shard_map/ppermute | solution.py:394
  56.2 1.4 %shard_map.68 = (f32[64,512]{1,0:T(8,128)S(1)}, bf16[256,128]{1,0:T(8,128)(2,1)S(1)}) custom-call(bf16[256,128]{1,0:T(8,128)(2,1)S(1)} %collective-permute-done.6.aw0, bf16[256,128]{1,0:T(8,128)(2,1)S(1)} %collective-permute-done.7.aw1, bf16[256,128]{1,0:T(8,128)(2,1)S(1)} %get-tuple-element.25.aw2, bf16[256,128]{1,0:T(8,128)(2,1)S(1)} %collective-permute-done.8.aw3, ...), custom_call_target="tpu_custom_call" | custom-call | flops 167772160 | bytes 1000000 | tf_op jit(solution)/shard_map/pallas_call | solution.py:493
  58.1 6.0 %collective-permute-start.12 = (bf16[256,128]{1,0:T(8,128)(2,1)S(1)}, bf16[256,128]{1,0:T(8,128)(2,1)S(1)}, u32[]{:S(2)}, u32[]{:S(2)}) collective-permute-start(bf16[256,128]{1,0:T(8,128)(2,1)S(1)} %get-tuple-element.27.aw2), channel_id=1, source_target_pairs={{2,0},{4,2},{6,4},{8,6},{10,8},{12,10},{14,12},{16,14},{18,16},{20... | collective-permute-start | bytes 196616 | tf_op jit(solution)/shard_map/ppermute | solution.py:383
  64.0 2.6 %collective-permute-done.10.aw0 = bf16[256,128]{1,0:T(8,128)(2,1)S(1)} collective-permute-done((bf16[256,128]{1,0:T(8,128)(2,1)S(1)}, bf16[256,128]{1,0:T(8,128)(2,1)S(1)}, u32[]{:S(2)}, u32[]{:S(2)}) %collective-permute-start.10) | collective-permute-done | bytes 65568 | tf_op jit(solution)/shard_map/ppermute | solution.py:383
  66.8 4.2 %collective-permute-done.13.aw4 = bf16[256,128]{1,0:T(8,128)(2,1)S(1)} collective-permute-done((bf16[256,128]{1,0:T(8,128)(2,1)S(1)}, bf16[256,128]{1,0:T(8,128)(2,1)S(1)}, u32[]{:S(2)}, u32[]{:S(2)}) %collective-permute-start.13) | collective-permute-done | bytes 65568 | tf_op jit(solution)/shard_map/ppermute | solution.py:383
  71.0 1.6 %shard_map.69 = (f32[64,256]{1,0:T(8,128)}, bf16[256,128]{1,0:T(8,128)(2,1)S(1)}) custom-call(bf16[256,128]{1,0:T(8,128)(2,1)S(1)} %collective-permute-done.10.aw0, bf16[256,128]{1,0:T(8,128)(2,1)S(1)} %collective-permute-done.11.aw1, bf16[256,128]{1,0:T(8,128)(2,1)S(1)} %get-tuple-element.27.aw2, bf16[256,128]{1,0:T(8,128)(2,1)S(1)} %collective-permute-done.12.aw3, ...), custom_call_target="tpu_custom_call" | custom-call | flops 83886080 | bytes 1000000 | tf_op jit(solution)/shard_map/pallas_call | solution.py:493
  72.5 6.0 %collective-permute-start.16 = (bf16[256,128]{1,0:T(8,128)(2,1)S(1)}, bf16[256,128]{1,0:T(8,128)(2,1)S(1)}, u32[]{:S(2)}, u32[]{:S(2)}) collective-permute-start(bf16[256,128]{1,0:T(8,128)(2,1)S(1)} %get-tuple-element.29.aw2), channel_id=1, source_target_pairs={{2,0},{4,2},{6,4},{8,6},{10,8},{12,10},{14,12},{16,14},{18,16},{20... | collective-permute-start | bytes 196616 | tf_op jit(solution)/shard_map/ppermute | solution.py:383
  78.5 2.0 %collective-permute-start.17 = (bf16[256,128]{1,0:T(8,128)(2,1)S(1)}, bf16[256,128]{1,0:T(8,128)(2,1)S(1)}, u32[]{:S(2)}, u32[]{:S(2)}) collective-permute-start(bf16[256,128]{1,0:T(8,128)(2,1)S(1)} %get-tuple-element.29.aw2), channel_id=1, source_target_pairs={{4,0},{6,2},{8,4},{10,6},{12,8},{14,10},{16,12},{18,14},{20,16},{2... | collective-permute-start | bytes 196616 | tf_op jit(solution)/shard_map/ppermute | solution.py:383
  80.5 6.9 %shard_map.70.rest_0_ = f32[64,8192]{1,0:T(8,128)S(1)} custom-call(s32[200]{0:T(256)S(1)} %pad_add_fusion.1.table_ref, bf16[272,128]{1,0:T(8,128)(2,1)S(1)} %collective-permute-done.1.aw0, bf16[272,128]{1,0:T(8,128)(2,1)S(1)} %collective-permute-done.2.aw1, bf16[272,128]{1,0:T(8,128)(2,1)S(1)} %shard_map.65.aw2, ...), custom_call_target="tpu_custom_call" | custom-call | flops 2000000000 | bytes 6000000 | tf_op jit(solution)/shard_map/pallas_call | solution.py:473
  87.4 5.0 %shard_map.71.rest_0_ = f32[64,8192]{1,0:T(8,128)S(1)} custom-call(s32[200]{0:T(256)S(1)} %pad_add_fusion.1.table_ref, bf16[256,128]{1,0:T(8,128)(2,1)S(1)} %collective-permute-done.6.aw0, bf16[256,128]{1,0:T(8,128)(2,1)S(1)} %collective-permute-done.7.aw1, bf16[256,128]{1,0:T(8,128)(2,1)S(1)} %get-tuple-element.25.aw2, ...), custom_call_target="tpu_custom_call" | custom-call | flops 2000000000 | bytes 6000000 | tf_op jit(solution)/shard_map/pallas_call | solution.py:473
  92.4 6.3 %shard_map.72.rest_0_ = f32[64,8192]{1,0:T(8,128)S(1)} custom-call(s32[200]{0:T(256)S(1)} %pad_add_fusion.1.table_ref, bf16[256,128]{1,0:T(8,128)(2,1)S(1)} %collective-permute-done.10.aw0, bf16[256,128]{1,0:T(8,128)(2,1)S(1)} %collective-permute-done.11.aw1, bf16[256,128]{1,0:T(8,128)(2,1)S(1)} %get-tuple-element.27.aw2, ...), custom_call_target="tpu_custom_call" | custom-call | flops 2000000000 | bytes 6000000 | tf_op jit(solution)/shard_map/pallas_call | solution.py:473
  98.8 3.6 %shard_map.73 = (f32[32,4096]{1,0:T(8,128)S(1)}, bf16[32,4096]{1,0:T(8,128)(2,1)S(1)}) custom-call(s32[200]{0:T(256)S(1)} %pad_add_fusion.1.table_ref, bf16[256,128]{1,0:T(8,128)(2,1)S(1)} %collective-permute-done.14.aw0, bf16[256,128]{1,0:T(8,128)(2,1)S(1)} %collective-permute-done.15.aw1, bf16[256,128]{1,0:T(8,128)(2,1)S(1)} %get-tuple-element.29.aw2, ...), custom_call_target="tpu_custom_call" | custom-call | flops 2000000000 | bytes 6000000 | tf_op jit(solution)/shard_map/pallas_call | solution.py:473
  102.5 3.3 %shard_map.74 = (f32[32,4096]{1,0:T(8,128)S(1)}, bf16[32,4096]{1,0:T(8,128)(2,1)S(1)}) custom-call(s32[200]{0:T(256)S(1)} %pad_add_fusion.1.table_ref, bf16[256,128]{1,0:T(8,128)(2,1)S(1)} %collective-permute-done.14.aw0, bf16[256,128]{1,0:T(8,128)(2,1)S(1)} %collective-permute-done.15.aw1, bf16[256,128]{1,0:T(8,128)(2,1)S(1)} %get-tuple-element.29.aw2, ...), custom_call_target="tpu_custom_call" | custom-call | flops 2000000000 | bytes 6000000 | tf_op jit(solution)/shard_map/pallas_call | solution.py:473
  105.8 1.5 %collective-permute-start.21 = (bf16[32,4096]{1,0:T(8,128)(2,1)S(1)}, bf16[32,4096]{1,0:T(8,128)(2,1)S(1)}, u32[]{:S(2)}, u32[]{:S(2)}) collective-permute-start(bf16[32,4096]{1,0:T(8,128)(2,1)S(1)} %get-tuple-element.36), channel_id=1, source_target_pairs={{0,1},{1,0},{2,3},{3,2},{4,5},{5,4},{6,7},{7,6},{8,9},{9,8},{10,11... | collective-permute-start | bytes 786440 | tf_op jit(solution)/shard_map/ppermute | solution.py:394
  107.3 2.1 %collective-permute-start.20 = (bf16[32,4096]{1,0:T(8,128)(2,1)S(1)}, bf16[32,4096]{1,0:T(8,128)(2,1)S(1)}, u32[]{:S(2)}, u32[]{:S(2)}) collective-permute-start(bf16[32,4096]{1,0:T(8,128)(2,1)S(1)} %get-tuple-element.35), channel_id=1, source_target_pairs={{0,1},{1,0},{2,3},{3,2},{4,5},{5,4},{6,7},{7,6},{8,9},{9,8},{10,11... | collective-permute-start | bytes 786440 | tf_op jit(solution)/shard_map/ppermute | solution.py:394
  109.4 7.1 %collective-permute-done.21 = bf16[32,4096]{1,0:T(8,128)(2,1)S(1)} collective-permute-done((bf16[32,4096]{1,0:T(8,128)(2,1)S(1)}, bf16[32,4096]{1,0:T(8,128)(2,1)S(1)}, u32[]{:S(2)}, u32[]{:S(2)}) %collective-permute-start.21) | collective-permute-done | bytes 262176 | tf_op jit(solution)/shard_map/ppermute | solution.py:394
  116.5 4.2 %collective-permute-done.20 = bf16[32,4096]{1,0:T(8,128)(2,1)S(1)} collective-permute-done((bf16[32,4096]{1,0:T(8,128)(2,1)S(1)}, bf16[32,4096]{1,0:T(8,128)(2,1)S(1)}, u32[]{:S(2)}, u32[]{:S(2)}) %collective-permute-start.20) | collective-permute-done | bytes 262176 | tf_op jit(solution)/shard_map/ppermute | solution.py:394
  120.8 1.5 %pad_maximum_fusion = f32[32,16384]{1,0:T(8,128)} fusion(f32[32,8192]{1,0:T(8,128)S(1)} %get-tuple-element.38, f32[32,8192]{1,0:T(8,128)S(1)} %get-tuple-element.37), kind=kLoop, calls=%fused_computation.1 | loop fusion | flops 524288 | bytes 4194304 | tf_op jit(solution)/shard_map/concatenate | solution.py:522
  (62 shorter events, 4.0 us)
Async XLA Ops:
  1.5 1.6 %copy-start = (f32[32,16384]{1,0:T(8,128)S(1)}, f32[32,16384]{1,0:T(8,128)}, u32[]{:S(2)}) copy-start(f32[32,16384]{1,0:T(8,128)} %x_ref.3) | copy-start | bytes 6291460
  6.8 10.2 %collective-permute-start = (f32[32,256]{1,0:T(8,128)S(1)}, f32[32,256]{1,0:T(8,128)S(1)}, u32[]{:S(2)}, u32[]{:S(2)}) collective-permute-start(f32[32,256]{1,0:T(8,128)S(1)} %get-tuple-element.21.own_ref), channel_id=1, source_target_pairs={{0,1},{1,0},{2,3},{3,2},{4,5},{5,4},{6,7},{7,6},{8,9},{9,8},{10,11... | collective-permute-start | bytes 98312 | tf_op jit(solution)/shard_map/ppermute | solution.py:394
  10.0 6.9 %copy-start.3 = (s32[5]{0:T(128)S(1)}, s32[5]{0:T(128)}, u32[]{:S(2)}) copy-start(s32[5]{0:T(128)} %constant.103.clone) | copy-start | bytes 64
  10.0 32.1 %copy-start.1 = (s32[5]{0:T(128)S(1)}, s32[5]{0:T(128)}, u32[]{:S(2)}) copy-start(s32[5]{0:T(128)} %constant.107) | copy-start | bytes 64
  10.0 32.1 %copy-start.2 = (f32[5]{0:T(128)S(1)}, f32[5]{0:T(128)}, u32[]{:S(2)}) copy-start(f32[5]{0:T(128)} %constant.109) | copy-start | bytes 64
  13.3 67.2 %collective-permute-start.18 = (bf16[32,8192]{1,0:T(8,128)(2,1)S(1)}, bf16[32,8192]{1,0:T(8,128)(2,1)}, u32[]{:S(2)}, u32[]{:S(2)}) collective-permute-start(bf16[32,8192]{1,0:T(8,128)(2,1)S(1)} %get-tuple-element.31), channel_id=1, source_target_pairs={{0,1},{1,0},{2,3},{3,2},{4,5},{5,4},{6,7},{7,6},{8,9},{9,8},{10,11... | collective-permute-start | bytes 1572872 | tf_op jit(solution)/shard_map/ppermute | solution.py:394
  13.8 28.6 %collective-permute-start.5 = (f32[32,768]{1,0:T(8,128)S(1)}, f32[32,768]{1,0:T(8,128)S(1)}, u32[]{:S(2)}, u32[]{:S(2)}) collective-permute-start(f32[32,768]{1,0:T(8,128)S(1)} %get-tuple-element.24.rest_0_), channel_id=1, source_target_pairs={{0,1},{1,0},{2,3},{3,2},{4,5},{5,4},{6,7},{7,6},{8,9},{9,8},{10,11... | collective-permute-start | bytes 294920 | tf_op jit(solution)/shard_map/ppermute | solution.py:394
  17.2 19.9 %collective-permute-start.1 = (bf16[272,128]{1,0:T(8,128)(2,1)S(1)}, bf16[272,128]{1,0:T(8,128)(2,1)S(1)}, u32[]{:S(2)}, u32[]{:S(2)}) collective-permute-start(bf16[272,128]{1,0:T(8,128)(2,1)S(1)} %shard_map.65.aw2), channel_id=1, source_target_pairs={{124,0},{126,2},{0,4},{2,6},{4,8},{6,10},{8,12},{10,14},{12,16},{1... | collective-permute-start | bytes 208904 | tf_op jit(solution)/shard_map/ppermute | solution.py:383
  17.8 19.8 %collective-permute-start.2 = (bf16[272,128]{1,0:T(8,128)(2,1)S(1)}, bf16[272,128]{1,0:T(8,128)(2,1)S(1)}, u32[]{:S(2)}, u32[]{:S(2)}) collective-permute-start(bf16[272,128]{1,0:T(8,128)(2,1)S(1)} %shard_map.65.aw2), channel_id=1, source_target_pairs={{126,0},{0,2},{2,4},{4,6},{6,8},{8,10},{10,12},{12,14},{14,16},{16... | collective-permute-start | bytes 208904 | tf_op jit(solution)/shard_map/ppermute | solution.py:383
  17.8 19.8 %collective-permute-start.3 = (bf16[272,128]{1,0:T(8,128)(2,1)S(1)}, bf16[272,128]{1,0:T(8,128)(2,1)S(1)}, u32[]{:S(2)}, u32[]{:S(2)}) collective-permute-start(bf16[272,128]{1,0:T(8,128)(2,1)S(1)} %shard_map.65.aw2), channel_id=1, source_target_pairs={{2,0},{4,2},{6,4},{8,6},{10,8},{12,10},{14,12},{16,14},{18,16},{20... | collective-permute-start | bytes 208904 | tf_op jit(solution)/shard_map/ppermute | solution.py:383
  37.1 5.0 %collective-permute-start.4 = (bf16[272,128]{1,0:T(8,128)(2,1)S(1)}, bf16[272,128]{1,0:T(8,128)(2,1)S(1)}, u32[]{:S(2)}, u32[]{:S(2)}) collective-permute-start(bf16[272,128]{1,0:T(8,128)(2,1)S(1)} %shard_map.65.aw2), channel_id=1, source_target_pairs={{4,0},{6,2},{8,4},{10,6},{12,8},{14,10},{16,12},{18,14},{20,16},{2... | collective-permute-start | bytes 208904 | tf_op jit(solution)/shard_map/ppermute | solution.py:383
  44.0 9.5 %collective-permute-start.6 = (bf16[256,128]{1,0:T(8,128)(2,1)S(1)}, bf16[256,128]{1,0:T(8,128)(2,1)S(1)}, u32[]{:S(2)}, u32[]{:S(2)}) collective-permute-start(bf16[256,128]{1,0:T(8,128)(2,1)S(1)} %get-tuple-element.25.aw2), channel_id=1, source_target_pairs={{124,0},{126,2},{0,4},{2,6},{4,8},{6,10},{8,12},{10,14},{12,16},{1... | collective-permute-start | bytes 196616 | tf_op jit(solution)/shard_map/ppermute | solution.py:383
  44.1 12.2 %collective-permute-start.7 = (bf16[256,128]{1,0:T(8,128)(2,1)S(1)}, bf16[256,128]{1,0:T(8,128)(2,1)S(1)}, u32[]{:S(2)}, u32[]{:S(2)}) collective-permute-start(bf16[256,128]{1,0:T(8,128)(2,1)S(1)} %get-tuple-element.25.aw2), channel_id=1, source_target_pairs={{126,0},{0,2},{2,4},{4,6},{6,8},{8,10},{10,12},{12,14},{14,16},{16... | collective-permute-start | bytes 196616 | tf_op jit(solution)/shard_map/ppermute | solution.py:383
  44.1 12.1 %collective-permute-start.8 = (bf16[256,128]{1,0:T(8,128)(2,1)S(1)}, bf16[256,128]{1,0:T(8,128)(2,1)S(1)}, u32[]{:S(2)}, u32[]{:S(2)}) collective-permute-start(bf16[256,128]{1,0:T(8,128)(2,1)S(1)} %get-tuple-element.25.aw2), channel_id=1, source_target_pairs={{2,0},{4,2},{6,4},{8,6},{10,8},{12,10},{14,12},{16,14},{18,16},{20... | collective-permute-start | bytes 196616 | tf_op jit(solution)/shard_map/ppermute | solution.py:383
  50.1 6.2 %collective-permute-start.9 = (bf16[256,128]{1,0:T(8,128)(2,1)S(1)}, bf16[256,128]{1,0:T(8,128)(2,1)S(1)}, u32[]{:S(2)}, u32[]{:S(2)}) collective-permute-start(bf16[256,128]{1,0:T(8,128)(2,1)S(1)} %get-tuple-element.25.aw2), channel_id=1, source_target_pairs={{4,0},{6,2},{8,4},{10,6},{12,8},{14,10},{16,12},{18,14},{20,16},{2... | collective-permute-start | bytes 196616 | tf_op jit(solution)/shard_map/ppermute | solution.py:383
  53.4 25.0 %collective-permute-start.19 = (f32[1,8192]{1,0:T(1,128)S(1)}, f32[1,8192]{1,0:T(1,128)S(1)}, u32[]{:S(2)}, u32[]{:S(2)}) collective-permute-start(f32[1,8192]{1,0:T(1,128)S(1)} %get-tuple-element.32), channel_id=1, source_target_pairs={{0,1},{1,0},{2,3},{3,2},{4,5},{5,4},{6,7},{7,6},{8,9},{9,8},{10,11... | collective-permute-start | bytes 98312 | tf_op jit(solution)/shard_map/ppermute | solution.py:394
  57.6 9.1 %collective-permute-start.10 = (bf16[256,128]{1,0:T(8,128)(2,1)S(1)}, bf16[256,128]{1,0:T(8,128)(2,1)S(1)}, u32[]{:S(2)}, u32[]{:S(2)}) collective-permute-start(bf16[256,128]{1,0:T(8,128)(2,1)S(1)} %get-tuple-element.27.aw2), channel_id=1, source_target_pairs={{124,0},{126,2},{0,4},{2,6},{4,8},{6,10},{8,12},{10,14},{12,16},{1... | collective-permute-start | bytes 196616 | tf_op jit(solution)/shard_map/ppermute | solution.py:383
  58.0 8.8 %collective-permute-start.11 = (bf16[256,128]{1,0:T(8,128)(2,1)S(1)}, bf16[256,128]{1,0:T(8,128)(2,1)S(1)}, u32[]{:S(2)}, u32[]{:S(2)}) collective-permute-start(bf16[256,128]{1,0:T(8,128)(2,1)S(1)} %get-tuple-element.27.aw2), channel_id=1, source_target_pairs={{126,0},{0,2},{2,4},{4,6},{6,8},{8,10},{10,12},{12,14},{14,16},{16... | collective-permute-start | bytes 196616 | tf_op jit(solution)/shard_map/ppermute | solution.py:383
  58.1 8.7 %collective-permute-start.12 = (bf16[256,128]{1,0:T(8,128)(2,1)S(1)}, bf16[256,128]{1,0:T(8,128)(2,1)S(1)}, u32[]{:S(2)}, u32[]{:S(2)}) collective-permute-start(bf16[256,128]{1,0:T(8,128)(2,1)S(1)} %get-tuple-element.27.aw2), channel_id=1, source_target_pairs={{2,0},{4,2},{6,4},{8,6},{10,8},{12,10},{14,12},{16,14},{18,16},{20... | collective-permute-start | bytes 196616 | tf_op jit(solution)/shard_map/ppermute | solution.py:383
  66.7 4.3 %collective-permute-start.13 = (bf16[256,128]{1,0:T(8,128)(2,1)S(1)}, bf16[256,128]{1,0:T(8,128)(2,1)S(1)}, u32[]{:S(2)}, u32[]{:S(2)}) collective-permute-start(bf16[256,128]{1,0:T(8,128)(2,1)S(1)} %get-tuple-element.27.aw2), channel_id=1, source_target_pairs={{4,0},{6,2},{8,4},{10,6},{12,8},{14,10},{16,12},{18,14},{20,16},{2... | collective-permute-start | bytes 196616 | tf_op jit(solution)/shard_map/ppermute | solution.py:383
  72.5 26.2 %collective-permute-start.14 = (bf16[256,128]{1,0:T(8,128)(2,1)S(1)}, bf16[256,128]{1,0:T(8,128)(2,1)S(1)}, u32[]{:S(2)}, u32[]{:S(2)}) collective-permute-start(bf16[256,128]{1,0:T(8,128)(2,1)S(1)} %get-tuple-element.29.aw2), channel_id=1, source_target_pairs={{124,0},{126,2},{0,4},{2,6},{4,8},{6,10},{8,12},{10,14},{12,16},{1... | collective-permute-start | bytes 196616 | tf_op jit(solution)/shard_map/ppermute | solution.py:383
  72.5 26.2 %collective-permute-start.15 = (bf16[256,128]{1,0:T(8,128)(2,1)S(1)}, bf16[256,128]{1,0:T(8,128)(2,1)S(1)}, u32[]{:S(2)}, u32[]{:S(2)}) collective-permute-start(bf16[256,128]{1,0:T(8,128)(2,1)S(1)} %get-tuple-element.29.aw2), channel_id=1, source_target_pairs={{126,0},{0,2},{2,4},{4,6},{6,8},{8,10},{10,12},{12,14},{14,16},{16... | collective-permute-start | bytes 196616 | tf_op jit(solution)/shard_map/ppermute | solution.py:383
  72.5 26.2 %collective-permute-start.16 = (bf16[256,128]{1,0:T(8,128)(2,1)S(1)}, bf16[256,128]{1,0:T(8,128)(2,1)S(1)}, u32[]{:S(2)}, u32[]{:S(2)}) collective-permute-start(bf16[256,128]{1,0:T(8,128)(2,1)S(1)} %get-tuple-element.29.aw2), channel_id=1, source_target_pairs={{2,0},{4,2},{6,4},{8,6},{10,8},{12,10},{14,12},{16,14},{18,16},{20... | collective-permute-start | bytes 196616 | tf_op jit(solution)/shard_map/ppermute | solution.py:383
  78.5 20.3 %collective-permute-start.17 = (bf16[256,128]{1,0:T(8,128)(2,1)S(1)}, bf16[256,128]{1,0:T(8,128)(2,1)S(1)}, u32[]{:S(2)}, u32[]{:S(2)}) collective-permute-start(bf16[256,128]{1,0:T(8,128)(2,1)S(1)} %get-tuple-element.29.aw2), channel_id=1, source_target_pairs={{4,0},{6,2},{8,4},{10,6},{12,8},{14,10},{16,12},{18,14},{20,16},{2... | collective-permute-start | bytes 196616 | tf_op jit(solution)/shard_map/ppermute | solution.py:383
  105.8 10.8 %collective-permute-start.21 = (bf16[32,4096]{1,0:T(8,128)(2,1)S(1)}, bf16[32,4096]{1,0:T(8,128)(2,1)S(1)}, u32[]{:S(2)}, u32[]{:S(2)}) collective-permute-start(bf16[32,4096]{1,0:T(8,128)(2,1)S(1)} %get-tuple-element.36), channel_id=1, source_target_pairs={{0,1},{1,0},{2,3},{3,2},{4,5},{5,4},{6,7},{7,6},{8,9},{9,8},{10,11... | collective-permute-start | bytes 786440 | tf_op jit(solution)/shard_map/ppermute | solution.py:394
  107.3 13.4 %collective-permute-start.20 = (bf16[32,4096]{1,0:T(8,128)(2,1)S(1)}, bf16[32,4096]{1,0:T(8,128)(2,1)S(1)}, u32[]{:S(2)}, u32[]{:S(2)}) collective-permute-start(bf16[32,4096]{1,0:T(8,128)(2,1)S(1)} %get-tuple-element.35), channel_id=1, source_target_pairs={{0,1},{1,0},{2,3},{3,2},{4,5},{5,4},{6,7},{7,6},{8,9},{9,8},{10,11... | collective-permute-start | bytes 786440 | tf_op jit(solution)/shard_map/ppermute | solution.py:394

commit v3 on v2

--- a/solution.py
+++ b/solution.py
@@ -23,7 +23,7 @@
 F32 = jnp.float32
 
 
-def vmem_call(body, outs, ins, scratch=(), aliases=None, cost=None):
+def vmem_call(body, outs, ins, scratch=(), aliases=None, cost=None, room=12):
     return pl.pallas_call(
         body,
         out_shape=outs,
@@ -31,13 +31,18 @@
         out_specs=jax.tree.map(lambda _: pl.BlockSpec(memory_space=pltpu.VMEM), outs),
         scratch_shapes=list(scratch),
         input_output_aliases=aliases or {},
-        compiler_params=pltpu.CompilerParams(vmem_limit_bytes=48 << 20),
+        compiler_params=pltpu.CompilerParams(vmem_limit_bytes=room << 20),
         cost_estimate=cost,
     )
 
 
 VM = pl.BlockSpec(memory_space=pltpu.VMEM)
 SM = pl.BlockSpec(memory_space=pltpu.SMEM)
+HBM = pl.BlockSpec(memory_space=pltpu.MemorySpace.HBM)
+
+
+def in_hbm(array):
+    return pltpu.with_memory_space_constraint(array, pltpu.MemorySpace.HBM)
 
 
 def cost(flops, moved):
@@ -60,48 +65,84 @@
     return jnp.where(rank == place, 1.0, 0.0).astype(BF16)
 
 
-def gather_batch(b, members, rows, cols, hot, index_ref, turned_ref, rows_ref):
+def table_of(local, values, variances):
+    key = local * local.shape[1] + lax.broadcasted_iota(jnp.int32, local.shape, 1)
+    return jnp.concatenate([key.astype(F32), local.astype(F32), values, variances], axis=0)
+
+
+def gather_batch(b, members, rows, cols, hot, spot_ref, turned_ref, rows_ref):
     count = rows.shape[1]
     batches = rows.shape[0] // 4
+    groups = LANES // members
     unroll = 16
 
     def pick(i, carry):
         for u in range(unroll):
             k = i * unroll + u
-            rows_ref[pl.ds(k, 1), :] = turned_ref[pl.ds(index_ref[8 + b * count + k], 1), :]
+            rows_ref[pl.ds(k, 1), :] = turned_ref[pl.ds(spot_ref[b, k], 1), :]
         return carry
 
     lax.fori_loop(0, count // unroll, pick, 0)
-    group = (cols[:, batches + b : batches + b + 1].astype(jnp.int32) // LANES) % (LANES // members)
+    group = (cols[:, batches + b : batches + b + 1].astype(jnp.int32) // LANES) % groups
     lane = lax.broadcasted_iota(jnp.int32, (count, LANES), 1) // members
     found = jnp.where(lane == group, rows_ref[...], 0.0)
     parts = [jnp.dot(hot, t, preferred_element_type=F32) for t in thirds(found)]
     placed = jnp.transpose((parts[0] + parts[1]) + parts[2])
     total = placed[:members]
-    for g in range(1, LANES // members):
+    for g in range(1, groups):
         total = total + placed[g * members : (g + 1) * members]
     return total
 
 
-def prep_body(index_ref, table_ref, x_ref, turned_ref, own_ref, sorted_ref, rows_ref):
-    batches = table_ref.shape[0] // 4
-    members = x_ref.shape[0]
+def prep_body(
+    half_ref, base_ref, index_any, value_any, var_any, x_ref,
+    turned_ref, own_ref, sorted_ref, keep_ref, send0_ref, send1_ref, mean_ref, table_ref, row_ref,
+    rows_ref, state_ref, index_ref, value_ref, var_ref, spot_ref, sems,
+):
+    half, base = half_ref[0], base_ref[0]
+    members, block_width = x_ref.shape
+    batches = index_ref.shape[0]
     groups = LANES // members
-
-    def turn(i, carry):
-        at = [
-            pl.ds(pl.multiple_of((i * groups + g) * LANES, LANES), LANES) for g in range(groups)
-        ]
-        block = jnp.concatenate([x_ref[:, a] for a in at], axis=0)
-        turned_ref[pl.ds(pl.multiple_of(i * LANES, LANES), LANES), :] = jnp.transpose(block)
-        return carry
-
-    lax.fori_loop(0, x_ref.shape[1] // (groups * LANES), turn, 0, unroll=2)
-    rows = table_ref[...]
+    width = block_width // 2
+    piece = width // 2
+
+    small = [
+        pltpu.make_async_copy(source, target, sems.at[5 + i])
+        for i, (source, target) in enumerate(
+            ((index_any, index_ref), (value_any, value_ref), (var_any, var_ref))
+        )
+    ]
+    for copy in small:
+        copy.start()
+    copies = []
+    for i in range(4):
+        at = pl.multiple_of(((2 - 2 * half + i) % 4) * piece, piece)
+        copies.append(
+            pltpu.make_async_copy(
+                x_ref.at[:, pl.ds(at, piece)], state_ref.at[:, pl.ds(at, piece)], sems.at[i]
+            )
+        )
+        copies[-1].start()
+    mine = pltpu.make_async_copy(
+        x_ref.at[:, pl.ds(pl.multiple_of(half * width, width), width)], keep_ref, sems.at[4]
+    )
+    mine.start()
+    for copy in small:
+        copy.wait()
+    local = index_ref[...] - base
+    span = groups * LANES
+    row_ref[...] = local // span * LANES + local % LANES
+    spots = pltpu.make_async_copy(row_ref, spot_ref, sems.at[8])
+    spots.start()
+
+    rows = table_of(local, value_ref[...], var_ref[...])
+    table_ref[...] = rows
     cols = jnp.transpose(rows)
-    for b in range(batches):
-        hot = placement(rows, cols, b)
-        values = jnp.concatenate([rows[(q + 1) * batches + b : (q + 1) * batches + b + 1] for q in range(3)], axis=0)
+    hots = [placement(rows, cols, b) for b in range(batches)]
+    for b, hot in enumerate(hots):
+        values = jnp.concatenate(
+            [rows[(q + 1) * batches + b : (q + 1) * batches + b + 1] for q in range(3)], axis=0
+        )
         parts = [
             lax.dot_general(t, hot, (((1,), (1,)), ((), ())), preferred_element_type=F32)
             for t in thirds(values)
@@ -109,41 +150,51 @@
         ordered = (parts[0] + parts[1]) + parts[2]
         for q in range(3):
             sorted_ref[q * batches + b : q * batches + b + 1, :] = ordered[q : q + 1]
-        if b == 0:
-            own_ref[...] = gather_batch(
-                b, members, rows, cols, hot, index_ref, turned_ref, rows_ref
+
+    for i in range(4):
+        copies[i].wait()
+        start = ((2 - 2 * half + i) % 4) * piece
+
+        def turn(j, carry, start=start, i=i):
+            at = pl.multiple_of(start + j * span, span)
+            block = state_ref[:, pl.ds(at, span)]
+            stack = jnp.concatenate(
+                [block[:, g * LANES : (g + 1) * LANES] for g in range(groups)], axis=0
             )
-
-
-def prep_rest_body(
-    index_ref, table_ref, x_ref, turned_ref, own_ref, keep_ref, send_ref, mean_ref, rows_ref
-):
-    batches = table_ref.shape[0] // 4
-    count = table_ref.shape[1]
-    members = x_ref.shape[0]
-    half = index_ref[0]
-    width = keep_ref.shape[1]
-    step = 2048
-
-    def split(i, carry):
-        at = pl.ds(pl.multiple_of(i * step, step), step)
-        here = pl.ds(pl.multiple_of(half * width + i * step, step), step)
-        there = pl.ds(pl.multiple_of((1 - half) * width + i * step, step), step)
-        keep_ref[:, at] = x_ref[:, here]
-        out = x_ref[:, there]
-        mean = jnp.sum(out, axis=0, keepdims=True) * (1.0 / members)
-        mean_ref[:, at] = mean
-        send_ref[:, at] = (out - mean).astype(BF16)
-        return carry
-
-    lax.fori_loop(0, width // step, split, 0)
+            place = pl.multiple_of(start // groups + j * LANES, LANES)
+            turned_ref[pl.ds(place, LANES), :] = jnp.transpose(stack)
+            if i < 2:
+                to = pl.ds(pl.multiple_of(i * piece + j * span, span), span)
+                mean = jnp.sum(block, axis=0, keepdims=True) * (1.0 / members)
+                mean_ref[:, to] = mean
+                here = pl.ds(pl.multiple_of(j * span, span), span)
+                (send0_ref, send1_ref)[i][:, here] = (block - mean).astype(BF16)
+            return carry
+
+        lax.fori_loop(0, piece // span, turn, 0, unroll=2)
+    spots.wait()
+    own_ref[...] = gather_batch(
+        0, members, rows, cols, hots[0], spot_ref, turned_ref, rows_ref
+    )
+    mine.wait()
+
+
+def prep_rest_body(spot_ref, table_ref, turned_ref, mean_ref, own_ref, rows_ref):
+    batches, count = table_ref.shape[0] // 4, table_ref.shape[1]
+    members = own_ref.shape[0] - mean_ref.shape[1] // own_ref.shape[1]
     rows = table_ref[...]
     cols = jnp.transpose(rows)
     for b in range(1, batches):
         hot = placement(rows, cols, b)
-        own_ref[:, (b - 1) * count : b * count] = gather_batch(
-            b, members, rows, cols, hot, index_ref, turned_ref, rows_ref
-        )
+        own_ref[:members, (b - 1) * count : b * count] = gather_batch(
+            b, members, rows, cols, hot, spot_ref, turned_ref, rows_ref
+        )
+    wide = own_ref.shape[1]
+    own_ref[:members, (batches - 1) * count :] = jnp.zeros(
+        (members, wide - (batches - 1) * count), F32
+    )
+    for c in range(mean_ref.shape[1] // wide):
+        own_ref[members + c : members + c + 1, :] = mean_ref[:, c * wide : (c + 1) * wide]
 
 
 def summary_rows(prior, values, variances):
@@ -184,7 +235,8 @@
     batches = sorted_ref.shape[0] // 3
     new_ref, pay_ref = rest[-2:]
     if batch == 1:
-        old = jnp.concatenate([rest[0][...], rest[1][...]], axis=0)
+        have = (aw0.shape[1] // 4, (batches - 1) * count)
+        old = jnp.concatenate([r[: have[0], : have[1]] for r in rest[:2]], axis=0)
     else:
         old = rest[0][:, count:]
     members = old.shape[0]
@@ -212,29 +264,32 @@
 
 
 def bulk_body(
-    batch, first_chunk, n_in, n_out, table_ref, aw0, aw1, aw2, aw3, aw4, pcol_ref, prow_ref, *rest
+    batch, all_chunks, first_chunk, skip, n_in, n_out, table_ref, aw0, aw1, aw2, aw3, aw4, pcol_ref, prow_ref, *rest
 ):
     first = n_in == 3
     last = n_out == 2
     ins, outs, scratch = rest[:n_in], rest[n_in : n_in + n_out], rest[n_in + n_out :]
-    poly_ref, band_ref, place_ref, gain_ref, part_ref, total_scratch = scratch
+    poly_ref, band_ref, place_ref, gain_ref, part_ref, anom_ref, total_scratch, spot_ref, dev_ref, sems = scratch
+    fetch = pltpu.make_async_copy(table_ref, spot_ref, sems.at[0])
+    fetch.start()
+    if first:
+        bring = pltpu.make_async_copy(ins[1], dev_ref, sems.at[1])
+        bring.start()
     aws = (aw0, aw1, aw2, aw3, aw4)
     count = pcol_ref.shape[0] // len(OFFSETS)
     members = aw0.shape[1] // 2
     padded = count + PAD
-    half = table_ref[0]
     chunks = outs[0].shape[1] // CHUNK
-    all_chunks = table_ref[1]
-    width = all_chunks * CHUNK
-    base = half * width
-    middle = (base + width // 2).astype(F32) * (1.0 / RADIUS)
+    middle = all_chunks * CHUNK // 2 / RADIUS
     position_row = prow_ref[batch : batch + 1, :]
 
     def entry(c, kind, what):
-        return table_ref[8 + ((batch * len(KINDS) + kind) * all_chunks + c) * 2 + what]
+        return spot_ref[batch, (kind * all_chunks + c) * 2 + what]
 
     def centre_of(c):
-        return (base + c * CHUNK + CHUNK // 2).astype(F32) * (1.0 / RADIUS)
+        if isinstance(c, int):
+            return (c * CHUNK + CHUNK // 2) / RADIUS
+        return (c * CHUNK + CHUNK // 2).astype(F32) * (1.0 / RADIUS)
 
     def weights_of(o):
         return jnp.transpose(aws[o][:count, :].astype(F32))[members:, :]
@@ -259,6 +314,8 @@
         part = jnp.dot(scaled, aws[o][:count, :members], preferred_element_type=F32)
         wide = part if wide is None else wide + part
     wide = [wide[r * members : (r + 1) * members, :] for r in range(3)]
+
+    fetch.wait()
 
     order = lax.broadcasted_iota(jnp.int32, (1, count), 1)
     for n in range(chunks):
@@ -315,15 +372,20 @@
     def one(n, slot):
         c = first_chunk + n
         local = pl.ds(pl.multiple_of(n * CHUNK, CHUNK), CHUNK)
-        span = pl.ds(pl.multiple_of(c * CHUNK, CHUNK), CHUNK)
         if first:
+            span = pl.ds(pl.multiple_of(c * CHUNK, CHUNK), CHUNK)
             x = jnp.concatenate(
-                [ins[0][:, span], ins[1][:, span].astype(F32) + ins[2][:, span]], axis=0
+                [
+                    ins[0][:, span],
+                    dev_ref[:, local].astype(F32) + ins[2][pl.ds(members // 2 + c, 1), :],
+                ],
+                axis=0,
             )
         else:
-            x = ins[0][:, span]
+            x = ins[0][:, pl.ds(pl.multiple_of((skip + n) * CHUNK, CHUNK), CHUNK)]
         mean = jnp.sum(x, axis=0, keepdims=True) * (1.0 / members)
         anom = (x - mean).astype(BF16)
+        anom_ref[:, local] = anom
         column = centre_of(c) + ramp
         starts = [pl.multiple_of(entry(c, i, 0), 16) for i in range(len(KINDS))]
         near = [band_ref[pl.ds(i * padded + starts[i], WINDOW), :] for i in range(len(KINDS))]
@@ -347,15 +409,27 @@
         change = change + ramp * (
             both[members : 2 * members] + ramp * both[2 * members : 3 * members]
         )
-        return x + change, anom, column, starts, c, local
-
-    def extend(anom, column, starts, c, local):
+        total_ref[:, local] = x + change
+
+    def several(m, carry):
+        for slot in range(UNROLL):
+            one(m * UNROLL + slot, slot)
+        return carry
+
+    if first:
+        bring.wait()
+    lax.fori_loop(0, chunks // UNROLL, several, 0)
+
+    def extend(n, carry):
+        c = first_chunk + n
+        local = pl.ds(pl.multiple_of(n * CHUNK, CHUNK), CHUNK)
+        column = centre_of(c) + ramp
         for i in range(len(KINDS)):
 
             def more(k, carry, i=i):
-                start = pl.multiple_of(i * padded + starts[i] + WINDOW + k * MORE, 16)
+                start = pl.multiple_of(i * padded + entry(c, i, 0) + WINDOW + k * MORE, 16)
                 aw = band_ref[pl.ds(start, MORE), :]
-                cov = jnp.dot(aw[:, :members], anom, preferred_element_type=F32)
+                cov = jnp.dot(aw[:, :members], anom_ref[:, local], preferred_element_type=F32)
                 gain = (taper(i, place_ref[pl.ds(start, MORE), :], column) * cov).astype(BF16)
                 total_ref[:, local] = total_ref[:, local] + lax.dot_general(
                     aw[:, members:], gain, (((0,), (0,)), ((), ())), preferred_element_type=F32
@@ -363,19 +437,12 @@
                 return carry
 
             lax.fori_loop(0, entry(c, i, 1), more, 0)
-
-    def pair(m, carry):
-        found = [one(m * UNROLL + slot, slot) for slot in range(UNROLL)]
-        for total, anom, column, starts, c, local in found:
-            total_ref[:, local] = total
-        for total, anom, column, starts, c, local in found:
-            extend(anom, column, starts, c, local)
-            if last:
-                outs[0][:, local] = total_ref[: members // 2, local]
-                outs[1][:, local] = total_ref[members // 2 :, local].astype(BF16)
+        if last:
+            outs[0][:, local] = total_ref[: members // 2, local]
+            outs[1][:, local] = total_ref[members // 2 :, local].astype(BF16)
         return carry
 
-    lax.fori_loop(0, chunks // UNROLL, pair, 0)
+    lax.fori_loop(0, chunks, extend, 0)
 
 
 def cyclic(block, distance):
@@ -403,41 +470,46 @@
     width = block_width // 2
     batches, count = obs_index.shape
 
-    local = obs_index - space_index * block_width
-    key = local * count + lax.broadcasted_iota(jnp.int32, local.shape, 1)
-    table = jnp.concatenate([key.astype(F32), local.astype(F32), obs_value, obs_var], axis=0)
     half = mem_index.astype(jnp.int32).reshape(1)
+    base = (space_index * block_width).astype(jnp.int32).reshape(1)
     groups = LANES // members_here
-    place = local // (groups * LANES) * LANES + local % LANES
-    index = jnp.concatenate([jnp.broadcast_to(half, (8,)), place.reshape(-1)])
+    part = width // PIECES
     shape = jax.ShapeDtypeStruct
-    turned, own0, srt = vmem_call(
+    turned, own0, srt, keep, send0, send1, mean, sort_table, spots = vmem_call(
         prep_body,
         (
             shape((block_width // groups, LANES), F32),
             shape((members_here, count), F32),
             shape((3 * batches, count), F32),
+            shape((members_here, width), F32),
+            shape((members_here, part), BF16),
+            shape((members_here, part), BF16),
+            shape((1, width), F32),
+            shape((4 * batches, count), F32),
+            shape((batches, count), jnp.int32),
         ),
-        [SM, VM, VM],
-        scratch=[pltpu.VMEM((count, LANES), F32)],
+        [SM, SM, HBM, HBM, HBM, HBM],
+        scratch=[
+            pltpu.VMEM((count, LANES), F32),
+            pltpu.VMEM((members_here, block_width), F32),
+            pltpu.VMEM((batches, count), jnp.int32),
+            pltpu.VMEM((batches, count), F32),
+            pltpu.VMEM((batches, count), F32),
+            pltpu.SMEM((batches, count), jnp.int32),
+            pltpu.SemaphoreType.DMA((9,)),
+        ],
         cost=cost(1e7, 6e6),
-    )(index, table, state)
+    )(half, base, *(in_hbm(a) for a in (obs_index, obs_value, obs_var, state)))
     other0 = traded(own0)
-    own, keep, send, mean = vmem_call(
+    devs = [traded(send) for send in (send0, send1)]
+    own = vmem_call(
         prep_rest_body,
-        (
-            shape((members_here, (batches - 1) * count), F32),
-            shape((members_here, width), F32),
-            shape((members_here, width), BF16),
-            shape((1, width), F32),
-        ),
+        shape((members_here + width // CHUNK, CHUNK), F32),
         [SM, VM, VM, VM],
         scratch=[pltpu.VMEM((count, LANES), F32)],
         cost=cost(1e7, 6e6),
-    )(index, table, state, turned)
+    )(spots, sort_table, turned, mean)
     other = traded(own)
-    dev = traded(send)
-    dev_mean = traded(mean)
 
     pay = vmem_call(
         first_body, shape((count + 16, 2 * members), BF16), [VM, VM, VM], cost=cost(1e6, 1e6)
@@ -464,28 +536,34 @@
     k0, k1 = below[:, :, :-1], below[:, :, 1:]
     w0 = k0 // 16 * 16
     more = jnp.maximum((k1 - w0 - WINDOW + MORE - 1) // MORE, 0)
-    head = jnp.where(lax.iota(jnp.int32, 8) == 1, chunks, half)
-    windows = jnp.concatenate([head, jnp.stack([w0, more], axis=-1).reshape(-1)])
-
-    def bulk(batch, state_args, outs, first_chunk):
+    table = jnp.stack([w0, more], axis=-1).reshape(batches, -1)
+    table = jnp.pad(table, ((0, 8 - batches), (0, LANES - table.shape[1])))
+    start = (mem_index * width).astype(F32) * (1.0 / RADIUS)
+    brow, bcol = prow - start, pcol - start
+
+    def bulk(batch, aws, state_args, outs, first_chunk):
         kinds = len(KINDS)
         here = outs[0].shape[1] // CHUNK
         return vmem_call(
-            functools.partial(bulk_body, batch, first_chunk, len(state_args), len(outs)),
+            functools.partial(bulk_body, batch, width // CHUNK, *first_chunk, len(state_args), len(outs)),
             outs,
-            [SM] + [VM] * (7 + len(state_args)),
+            [VM] * 8 + ([VM, HBM, VM] if len(state_args) == 3 else [VM]),
             scratch=[
                 pltpu.VMEM((here * 3 * members, members), BF16),
                 pltpu.VMEM((kinds * (count + PAD), 2 * members), BF16),
                 pltpu.VMEM((kinds * (count + PAD), 1), F32),
                 pltpu.VMEM((UNROLL * kinds * WINDOW, CHUNK), BF16),
                 pltpu.VMEM((here * 3 * members, members), F32),
+                pltpu.VMEM((members, outs[0].shape[1]), BF16),
                 pltpu.VMEM((members, outs[0].shape[1] if len(outs) == 2 else LANES), F32),
+                pltpu.SMEM((8, LANES), jnp.int32),
+                pltpu.VMEM((members_here, part) if len(state_args) == 3 else (16, LANES), BF16),
+                pltpu.SemaphoreType.DMA((2,)),
             ],
             cost=cost(2e9, 6e6),
-        )(windows, *aws, pcol, prow, *state_args)
-
-    x = None
+        )(table, *aws, bcol, brow, *state_args)
+
+    every = []
     tracked = (own, other)
     for batch in range(batches - 1):
         later = (batches - batch - 1) * count
@@ -498,22 +576,29 @@
         )(*aws, pcol, srt, *extra)
         tracked = (new,)
         following = band(pay)
-        state_args = (keep, dev, dev_mean) if batch == 0 else (x,)
-        (x,) = bulk(batch, state_args, (shape((members, width), F32),), 0)
+        every.append(aws)
         aws = following
-
-    pieces = PIECES
+    every.append(aws)
+
     mine, theirs = [], []
-    for piece in range(pieces):
-        size = width // pieces
-        kept, sent = bulk(
-            batches - 1,
-            (x,),
-            (shape((members_here, size), F32), shape((members_here, size), BF16)),
-            piece * size // CHUNK,
-        )
-        mine.append(kept)
-        theirs.append(traded(sent))
+    for piece in range(PIECES):
+        x = (keep, devs[piece], other)
+        for batch in range(batches - 1):
+            x = bulk(
+                batch, every[batch], x, (shape((members, part), F32),), (piece * part // CHUNK, 0)
+            )
+        parts = 2 if piece == PIECES - 1 else 1
+        size = part // parts
+        for p in range(parts):
+            kept, sent = bulk(
+                batches - 1,
+                every[-1],
+                x,
+                (shape((members_here, size), F32), shape((members_here, size), BF16)),
+                ((piece * part + p * size) // CHUNK, p * size // CHUNK),
+            )
+            mine.append(kept)
+            theirs.append(traded(sent))
     mine = jnp.concatenate(mine, axis=1)
     theirs = jnp.concatenate(theirs, axis=1).astype(F32)
     first = mem_index == 0

time: 123 us -> 124 us (level)
  Pallas kernels: 36.8 us -> 41.4 us
  starting transfers between devices: 42.5 us -> 40 us
  other arithmetic: 3.86 us -> 2.42 us
    ppermute x16, waiting for transfers between devices: 24.5 us -> 29.8 us  [cyclic(): lax.ppermute(block, 'space', [((i + distance) % n, i) for i in range(n)])]
    ppermute x6 -> x7, waiting for transfers between devices: 11.3 us -> 7.14 us  [traded(): return lax.ppermute(block, 'mem', [(0, 1), (1, 0)])]
    pallas_call x6 -> x10, Pallas kernels: 28.4 us -> 32.5 us  [the longest x9 28.4 us: bulk(): vmem_call(functools.partial(bulk_body, batch, width // CHUNK, *first_chun...]
    ppermute x6 -> x7, starting transfers between devices: 13.2 us -> 11.4 us  [traded(): return lax.ppermute(block, 'mem', [(0, 1), (1, 0)])]
  transfers between devices with their start and end apart: 22 -> 23, of which waited for: 6 -> 7; matrix products, arithmetic and copies ran while one was open for 2% -> 2% of each run, Pallas kernels for 21% -> 26%
where the time goes in v3:
time: 124 us
  Pallas kernels  41.4 us (33%)
  starting transfers between devices  40 us (32%)
  waiting for transfers between devices  37 us (30%)
  local copies, waits for them, and re-layouts  2.56 us (2%)
  other arithmetic  2.42 us (2%)
    ppermute x16, waiting for transfers between devices, cyclic(): lax.ppermute(block, 'space', [((i + distance) % n, i) for i in range(n)])  29.8 us
    ppermute x16, starting transfers between devices, cyclic(): lax.ppermute(block, 'space', [((i + distance) % n, i) for i in range(n)])  28.6 us
    pallas_call x9, Pallas kernels, bulk(): vmem_call(functools.partial(bulk_body, batch, width // CHUNK, *first_chun...  28.4 us
    ppermute x7, starting transfers between devices, traded(): return lax.ppermute(block, 'mem', [(0, 1), (1, 0)])  11.4 us
    ppermute x7, waiting for transfers between devices, traded(): return lax.ppermute(block, 'mem', [(0, 1), (1, 0)])  7.14 us
    pallas_call x3, Pallas kernels, shards(): vmem_call(functools.partial(step_body, batch + 1), (shape((members, later...  4.44 us
    pallas_call x1, Pallas kernels, shards(): vmem_call(prep_body, (shape((block_width // groups, LANES), F32), shape((...  4.33 us
    pallas_call x1, Pallas kernels, shards(): vmem_call(prep_rest_body, shape((members_here + width // CHUNK, CHUNK), F...  4.04 us
  transfers between devices with their start and end apart: 23, of which 7 were waited for; matrix products, arithmetic and copies ran while one was open for 2% of the time, Pallas kernels for 26%

profile of v3, /device:TPU:0, one launch (start us, length us, event | category | flops | bytes accessed | tf_op | source)
XLA Modules:
  0.0 123.7 jit_solution(13307241048294302804)
XLA Ops:
  0.0 4.3 %shard_map.64 = (f32[4096,128]{1,0:T(8,128)S(1)}, f32[32,256]{1,0:T(8,128)S(1)}, f32[12,256]{1,0:T(8,128)S(1)}, f32[32,8192]{1,0:T(8,128)S(1)}, bf16[32,4096]{1,...) custom-call(s32[1]{0:T(128)} %bitcast.half_ref, ...), custom_call_target="tpu_custom_call" | custom-call | flops 10000000 | bytes 6000000 | tf_op jit(solution)/shard_map/pallas_call | solution.py:478
  4.4 3.2 %collective-permute-start = (f32[32,256]{1,0:T(8,128)S(1)}, f32[32,256]{1,0:T(8,128)S(1)}, u32[]{:S(2)}, u32[]{:S(2)}) collective-permute-start(f32[32,256]{1,0:T(8,128)S(1)} %get-tuple-element.25.own_ref), channel_id=1, source_target_pairs={{0,1},{1,0},{2,3},{3,2},{4,5},{5,4},{6,7},{7,6},{8,9},{9,8},{10,11... | collective-permute-start | bytes 98312 | tf_op jit(solution)/shard_map/ppermute | solution.py:461
  7.6 4.0 %shard_map.66.rest_0_ = f32[40,1024]{1,0:T(8,128)S(1)} custom-call(s32[4,256]{1,0:T(4,128)S(1)} %get-tuple-element.27.spot_ref, f32[16,256]{1,0:T(8,128)S(1)} %get-tuple-element.28.table_ref, f32[4096,128]{1,0:T(8,128)S(1)} %get-tuple-element.29.turned_ref, f32[1,8192]{1,0:T(1,128)S(1)} %get-tuple-element.30.mean_ref), custom_call_target="tpu_custom_call" | custom-call | flops 10000000 | bytes 6000000 | tf_op jit(solution)/shard_map/pallas_call | solution.py:505
  12.1 3.1 %collective-permute-start.18 = (bf16[32,4096]{1,0:T(8,128)(2,1)S(1)}, bf16[32,4096]{1,0:T(8,128)(2,1)S(1)}, u32[]{:S(2)}, u32[]{:S(2)}) collective-permute-start(bf16[32,4096]{1,0:T(8,128)(2,1)S(1)} %get-tuple-element.37), channel_id=1, source_target_pairs={{0,1},{1,0},{2,3},{3,2},{4,5},{5,4},{6,7},{7,6},{8,9},{9,8},{10,11... | collective-permute-start | bytes 786440 | tf_op jit(solution)/shard_map/ppermute | solution.py:461
  15.8 1.7 %collective-permute-start.1 = (bf16[272,128]{1,0:T(8,128)(2,1)S(1)}, bf16[272,128]{1,0:T(8,128)(2,1)S(1)}, u32[]{:S(2)}, u32[]{:S(2)}) collective-permute-start(bf16[272,128]{1,0:T(8,128)(2,1)S(1)} %shard_map.65.aw2), channel_id=1, source_target_pairs={{124,0},{126,2},{0,4},{2,6},{4,8},{6,10},{8,12},{10,14},{12,16},{1... | collective-permute-start | bytes 208904 | tf_op jit(solution)/shard_map/ppermute | solution.py:450
  17.5 6.0 %collective-permute-start.4 = (bf16[272,128]{1,0:T(8,128)(2,1)S(1)}, bf16[272,128]{1,0:T(8,128)(2,1)S(1)}, u32[]{:S(2)}, u32[]{:S(2)}) collective-permute-start(bf16[272,128]{1,0:T(8,128)(2,1)S(1)} %shard_map.65.aw2), channel_id=1, source_target_pairs={{4,0},{6,2},{8,4},{10,6},{12,8},{14,10},{16,12},{18,14},{20,16},{2... | collective-permute-start | bytes 208904 | tf_op jit(solution)/shard_map/ppermute | solution.py:450
  23.5 13.2 %collective-permute-done.1.aw0 = bf16[272,128]{1,0:T(8,128)(2,1)S(1)} collective-permute-done((bf16[272,128]{1,0:T(8,128)(2,1)S(1)}, bf16[272,128]{1,0:T(8,128)(2,1)S(1)}, u32[]{:S(2)}, u32[]{:S(2)}) %collective-permute-start.1) | collective-permute-done | bytes 69664 | tf_op jit(solution)/shard_map/ppermute | solution.py:450
  36.7 7.9 %collective-permute-done.2.aw1 = bf16[272,128]{1,0:T(8,128)(2,1)S(1)} collective-permute-done((bf16[272,128]{1,0:T(8,128)(2,1)S(1)}, bf16[272,128]{1,0:T(8,128)(2,1)S(1)}, u32[]{:S(2)}, u32[]{:S(2)}) %collective-permute-start.2) | collective-permute-done | bytes 69664 | tf_op jit(solution)/shard_map/ppermute | solution.py:450
  44.7 1.9 %collective-permute-done.3.aw3 = bf16[272,128]{1,0:T(8,128)(2,1)S(1)} collective-permute-done((bf16[272,128]{1,0:T(8,128)(2,1)S(1)}, bf16[272,128]{1,0:T(8,128)(2,1)S(1)}, u32[]{:S(2)}, u32[]{:S(2)}) %collective-permute-start.3) | collective-permute-done | bytes 69664 | tf_op jit(solution)/shard_map/ppermute | solution.py:450
  48.3 1.5 %shard_map.67 = (f32[64,768]{1,0:T(8,128)S(1)}, bf16[256,128]{1,0:T(8,128)(2,1)S(1)}) custom-call(bf16[272,128]{1,0:T(8,128)(2,1)S(1)} %collective-permute-done.1.aw0, bf16[272,128]{1,0:T(8,128)(2,1)S(1)} %collective-permute-done.2.aw1, bf16[272,128]{1,0:T(8,128)(2,1)S(1)} %shard_map.65.aw2, bf16[272,128]{1,0:T(8,128)(2,1)S(1)} %collective-permute-done.3.aw3, ...), custom_call_target="tpu_custom_call" | custom-call | flops 251658240 | bytes 1000000 | tf_op jit(solution)/shard_map/pallas_call | solution.py:571
  50.1 6.0 %collective-permute-start.8 = (bf16[256,128]{1,0:T(8,128)(2,1)S(1)}, bf16[256,128]{1,0:T(8,128)(2,1)S(1)}, u32[]{:S(2)}, u32[]{:S(2)}) collective-permute-start(bf16[256,128]{1,0:T(8,128)(2,1)S(1)} %get-tuple-element.31.aw2), channel_id=1, source_target_pairs={{2,0},{4,2},{6,4},{8,6},{10,8},{12,10},{14,12},{16,14},{18,16},{20... | collective-permute-start | bytes 196616 | tf_op jit(solution)/shard_map/ppermute | solution.py:450
  56.3 1.6 %collective-permute-start.6 = (bf16[256,128]{1,0:T(8,128)(2,1)S(1)}, bf16[256,128]{1,0:T(8,128)(2,1)S(1)}, u32[]{:S(2)}, u32[]{:S(2)}) collective-permute-start(bf16[256,128]{1,0:T(8,128)(2,1)S(1)} %get-tuple-element.31.aw2), channel_id=1, source_target_pairs={{124,0},{126,2},{0,4},{2,6},{4,8},{6,10},{8,12},{10,14},{12,16},{1... | collective-permute-start | bytes 196616 | tf_op jit(solution)/shard_map/ppermute | solution.py:450
  58.1 6.0 %collective-permute-done.7.aw1 = bf16[256,128]{1,0:T(8,128)(2,1)S(1)} collective-permute-done((bf16[256,128]{1,0:T(8,128)(2,1)S(1)}, bf16[256,128]{1,0:T(8,128)(2,1)S(1)}, u32[]{:S(2)}, u32[]{:S(2)}) %collective-permute-start.7) | collective-permute-done | bytes 65568 | tf_op jit(solution)/shard_map/ppermute | solution.py:450
  66.3 1.8 %collective-permute-start.12 = (bf16[256,128]{1,0:T(8,128)(2,1)S(1)}, bf16[256,128]{1,0:T(8,128)(2,1)S(1)}, u32[]{:S(2)}, u32[]{:S(2)}) collective-permute-start(bf16[256,128]{1,0:T(8,128)(2,1)S(1)} %get-tuple-element.33.aw2), channel_id=1, source_target_pairs={{2,0},{4,2},{6,4},{8,6},{10,8},{12,10},{14,12},{16,14},{18,16},{20... | collective-permute-start | bytes 196616 | tf_op jit(solution)/shard_map/ppermute | solution.py:450
  68.1 1.6 %collective-permute-start.10 = (bf16[256,128]{1,0:T(8,128)(2,1)S(1)}, bf16[256,128]{1,0:T(8,128)(2,1)S(1)}, u32[]{:S(2)}, u32[]{:S(2)}) collective-permute-start(bf16[256,128]{1,0:T(8,128)(2,1)S(1)} %get-tuple-element.33.aw2), channel_id=1, source_target_pairs={{124,0},{126,2},{0,4},{2,6},{4,8},{6,10},{8,12},{10,14},{12,16},{1... | collective-permute-start | bytes 196616 | tf_op jit(solution)/shard_map/ppermute | solution.py:450
  71.0 3.7 %shard_map.74.rest_0_ = f32[64,4096]{1,0:T(8,128)S(1)} custom-call(s32[8,128]{1,0:T(8,128)S(1)} %pad.4.table_ref, bf16[272,128]{1,0:T(8,128)(2,1)S(1)} %collective-permute-done.1.aw0, bf16[272,128]{1,0:T(8,128)(2,1)S(1)} %collective-permute-done.2.aw1, bf16[272,128]{1,0:T(8,128)(2,1)S(1)} %shard_map.65.aw2, bf16[272,128]{1,0:T(8,128)(2,1)S(1)} %collective-permute-done.3.aw3, ...), custom_call_target="tpu_custom_call" | custom-call | flops 2000000000 | bytes 6000000 | tf_op jit(solution)/shard_map/pallas_call | solution.py:547
  74.7 3.7 %shard_map.70.rest_0_ = f32[64,4096]{1,0:T(8,128)S(1)} custom-call(s32[8,128]{1,0:T(8,128)S(1)} %pad.4.table_ref, bf16[272,128]{1,0:T(8,128)(2,1)S(1)} %collective-permute-done.1.aw0, bf16[272,128]{1,0:T(8,128)(2,1)S(1)} %collective-permute-done.2.aw1, bf16[272,128]{1,0:T(8,128)(2,1)S(1)} %shard_map.65.aw2, bf16[272,128]{1,0:T(8,128)(2,1)S(1)} %collective-permute-done.3.aw3, ...), custom_call_target="tpu_custom_call" | custom-call | flops 2000000000 | bytes 6000000 | tf_op jit(solution)/shard_map/pallas_call | solution.py:547
  78.4 3.0 %shard_map.71.rest_0_ = f32[64,4096]{1,0:T(8,128)S(1)} custom-call(s32[8,128]{1,0:T(8,128)S(1)} %pad.4.table_ref, bf16[256,128]{1,0:T(8,128)(2,1)S(1)} %collective-permute-done.6.aw0, bf16[256,128]{1,0:T(8,128)(2,1)S(1)} %collective-permute-done.7.aw1, bf16[256,128]{1,0:T(8,128)(2,1)S(1)} %get-tuple-element.31.aw2, ...), custom_call_target="tpu_custom_call" | custom-call | flops 2000000000 | bytes 6000000 | tf_op jit(solution)/shard_map/pallas_call | solution.py:547
  81.4 3.0 %shard_map.75.rest_0_ = f32[64,4096]{1,0:T(8,128)S(1)} custom-call(s32[8,128]{1,0:T(8,128)S(1)} %pad.4.table_ref, bf16[256,128]{1,0:T(8,128)(2,1)S(1)} %collective-permute-done.6.aw0, bf16[256,128]{1,0:T(8,128)(2,1)S(1)} %collective-permute-done.7.aw1, bf16[256,128]{1,0:T(8,128)(2,1)S(1)} %get-tuple-element.31.aw2, ...), custom_call_target="tpu_custom_call" | custom-call | flops 2000000000 | bytes 6000000 | tf_op jit(solution)/shard_map/pallas_call | solution.py:547
  84.4 1.6 %shard_map.69 = (f32[64,256]{1,0:T(8,128)}, bf16[256,128]{1,0:T(8,128)(2,1)S(1)}) custom-call(bf16[256,128]{1,0:T(8,128)(2,1)S(1)} %collective-permute-done.10.aw0, bf16[256,128]{1,0:T(8,128)(2,1)S(1)} %collective-permute-done.11.aw1, bf16[256,128]{1,0:T(8,128)(2,1)S(1)} %get-tuple-element.33.aw2, bf16[256,128]{1,0:T(8,128)(2,1)S(1)} %collective-permute-done.12.aw3, ...), custom_call_target="tpu_custom_call" | custom-call | flops 83886080 | bytes 1000000 | tf_op jit(solution)/shard_map/pallas_call | solution.py:571
  86.0 4.6 %collective-permute-start.17 = (bf16[256,128]{1,0:T(8,128)(2,1)S(1)}, bf16[256,128]{1,0:T(8,128)(2,1)S(1)}, u32[]{:S(2)}, u32[]{:S(2)}) collective-permute-start(bf16[256,128]{1,0:T(8,128)(2,1)S(1)} %get-tuple-element.35.aw2), channel_id=1, source_target_pairs={{4,0},{6,2},{8,4},{10,6},{12,8},{14,10},{16,12},{18,14},{20,16},{2... | collective-permute-start | bytes 196616 | tf_op jit(solution)/shard_map/ppermute | solution.py:450
  90.6 3.2 %collective-permute-start.16 = (bf16[256,128]{1,0:T(8,128)(2,1)S(1)}, bf16[256,128]{1,0:T(8,128)(2,1)S(1)}, u32[]{:S(2)}, u32[]{:S(2)}) collective-permute-start(bf16[256,128]{1,0:T(8,128)(2,1)S(1)} %get-tuple-element.35.aw2), channel_id=1, source_target_pairs={{2,0},{4,2},{6,4},{8,6},{10,8},{12,10},{14,12},{16,14},{18,16},{20... | collective-permute-start | bytes 196616 | tf_op jit(solution)/shard_map/ppermute | solution.py:450
  93.8 1.6 %collective-permute-start.14 = (bf16[256,128]{1,0:T(8,128)(2,1)S(1)}, bf16[256,128]{1,0:T(8,128)(2,1)S(1)}, u32[]{:S(2)}, u32[]{:S(2)}) collective-permute-start(bf16[256,128]{1,0:T(8,128)(2,1)S(1)} %get-tuple-element.35.aw2), channel_id=1, source_target_pairs={{124,0},{126,2},{0,4},{2,6},{4,8},{6,10},{8,12},{10,14},{12,16},{1... | collective-permute-start | bytes 196616 | tf_op jit(solution)/shard_map/ppermute | solution.py:450
  95.5 3.7 %shard_map.76.rest_0_ = f32[64,4096]{1,0:T(8,128)S(1)} custom-call(s32[8,128]{1,0:T(8,128)S(1)} %pad.4.table_ref, bf16[256,128]{1,0:T(8,128)(2,1)S(1)} %collective-permute-done.10.aw0, bf16[256,128]{1,0:T(8,128)(2,1)S(1)} %collective-permute-done.11.aw1, bf16[256,128]{1,0:T(8,128)(2,1)S(1)} %get-tuple-element.33.aw2, ...), custom_call_target="tpu_custom_call" | custom-call | flops 2000000000 | bytes 6000000 | tf_op jit(solution)/shard_map/pallas_call | solution.py:547
  99.2 3.7 %shard_map.72.rest_0_ = f32[64,4096]{1,0:T(8,128)S(1)} custom-call(s32[8,128]{1,0:T(8,128)S(1)} %pad.4.table_ref, bf16[256,128]{1,0:T(8,128)(2,1)S(1)} %collective-permute-done.10.aw0, bf16[256,128]{1,0:T(8,128)(2,1)S(1)} %collective-permute-done.11.aw1, bf16[256,128]{1,0:T(8,128)(2,1)S(1)} %get-tuple-element.33.aw2, ...), custom_call_target="tpu_custom_call" | custom-call | flops 2000000000 | bytes 6000000 | tf_op jit(solution)/shard_map/pallas_call | solution.py:547
  102.9 3.7 %shard_map.73 = (f32[32,4096]{1,0:T(8,128)S(1)}, bf16[32,4096]{1,0:T(8,128)(2,1)S(1)}) custom-call(s32[8,128]{1,0:T(8,128)S(1)} %pad.4.table_ref, bf16[256,128]{1,0:T(8,128)(2,1)S(1)} %collective-permute-done.14.aw0, bf16[256,128]{1,0:T(8,128)(2,1)S(1)} %collective-permute-done.15.aw1, bf16[256,128]{1,0:T(8,128)(2,1)S(1)} %get-tuple-element.35.aw2, ...), custom_call_target="tpu_custom_call" | custom-call | flops 2000000000 | bytes 6000000 | tf_op jit(solution)/shard_map/pallas_call | solution.py:547
  107.5 1.8 %shard_map.78 = (f32[32,2048]{1,0:T(8,128)S(1)}, bf16[32,2048]{1,0:T(8,128)(2,1)S(1)}) custom-call(s32[8,128]{1,0:T(8,128)S(1)} %pad.4.table_ref, bf16[256,128]{1,0:T(8,128)(2,1)S(1)} %collective-permute-done.14.aw0, bf16[256,128]{1,0:T(8,128)(2,1)S(1)} %collective-permute-done.15.aw1, bf16[256,128]{1,0:T(8,128)(2,1)S(1)} %get-tuple-element.35.aw2, ...), custom_call_target="tpu_custom_call" | custom-call | flops 2000000000 | bytes 6000000 | tf_op jit(solution)/shard_map/pallas_call | solution.py:547
  109.3 2.8 %collective-permute-start.22 = (bf16[32,2048]{1,0:T(8,128)(2,1)S(1)}, bf16[32,2048]{1,0:T(8,128)(2,1)S(1)}, u32[]{:S(2)}, u32[]{:S(2)}) collective-permute-start(bf16[32,2048]{1,0:T(8,128)(2,1)S(1)} %get-tuple-element.44), channel_id=1, source_target_pairs={{0,1},{1,0},{2,3},{3,2},{4,5},{5,4},{6,7},{7,6},{8,9},{9,8},{10,11... | collective-permute-start | bytes 393224 | tf_op jit(solution)/shard_map/ppermute | solution.py:461
  112.2 2.2 %shard_map.77 = (f32[32,2048]{1,0:T(8,128)S(1)}, bf16[32,2048]{1,0:T(8,128)(2,1)S(1)}) custom-call(s32[8,128]{1,0:T(8,128)S(1)} %pad.4.table_ref, bf16[256,128]{1,0:T(8,128)(2,1)S(1)} %collective-permute-done.14.aw0, bf16[256,128]{1,0:T(8,128)(2,1)S(1)} %collective-permute-done.15.aw1, bf16[256,128]{1,0:T(8,128)(2,1)S(1)} %get-tuple-element.35.aw2, ...), custom_call_target="tpu_custom_call" | custom-call | flops 2000000000 | bytes 6000000 | tf_op jit(solution)/shard_map/pallas_call | solution.py:547
  114.9 5.2 %collective-permute-done.22 = bf16[32,2048]{1,0:T(8,128)(2,1)S(1)} collective-permute-done((bf16[32,2048]{1,0:T(8,128)(2,1)S(1)}, bf16[32,2048]{1,0:T(8,128)(2,1)S(1)}, u32[]{:S(2)}, u32[]{:S(2)}) %collective-permute-start.22) | collective-permute-done | bytes 131104 | tf_op jit(solution)/shard_map/ppermute | solution.py:461
  120.2 1.9 %collective-permute-done.21 = bf16[32,2048]{1,0:T(8,128)(2,1)S(1)} collective-permute-done((bf16[32,2048]{1,0:T(8,128)(2,1)S(1)}, bf16[32,2048]{1,0:T(8,128)(2,1)S(1)}, u32[]{:S(2)}, u32[]{:S(2)}) %collective-permute-start.21) | collective-permute-done | bytes 131104 | tf_op jit(solution)/shard_map/ppermute | solution.py:461
  122.2 1.5 %pad_maximum_fusion = f32[32,16384]{1,0:T(8,128)} fusion(f32[32,8192]{1,0:T(8,128)S(1)} %get-tuple-element.46, f32[32,8192]{1,0:T(8,128)S(1)} %get-tuple-element.45), kind=kLoop, calls=%fused_computation.1 | loop fusion | flops 524288 | bytes 4194304 | tf_op jit(solution)/shard_map/concatenate | solution.py:607
  (68 shorter events, 8.5 us)
Async XLA Ops:
  0.0 15.6 %copy-start.4 = (s32[5]{0:T(128)S(1)}, s32[5]{0:T(128)}, u32[]{:S(2)}) copy-start(s32[5]{0:T(128)} %constant.74.clone) | copy-start | bytes 64
  0.0 46.7 %copy-start.2 = (f32[5]{0:T(128)S(1)}, f32[5]{0:T(128)}, u32[]{:S(2)}) copy-start(f32[5]{0:T(128)} %constant.80) | copy-start | bytes 64
  0.0 46.7 %copy-start.3 = (s32[5]{0:T(128)S(1)}, s32[5]{0:T(128)}, u32[]{:S(2)}) copy-start(s32[5]{0:T(128)} %constant.78) | copy-start | bytes 64
  4.3 7.3 %copy-start = (f32[32,8192]{1,0:T(8,128)}, f32[32,8192]{1,0:T(8,128)S(1)}, u32[]{:S(2)}) copy-start(f32[32,8192]{1,0:T(8,128)S(1)} %get-tuple-element.36.rest_0_) | copy-start | bytes 3145732
  4.4 11.3 %collective-permute-start = (f32[32,256]{1,0:T(8,128)S(1)}, f32[32,256]{1,0:T(8,128)S(1)}, u32[]{:S(2)}, u32[]{:S(2)}) collective-permute-start(f32[32,256]{1,0:T(8,128)S(1)} %get-tuple-element.25.own_ref), channel_id=1, source_target_pairs={{0,1},{1,0},{2,3},{3,2},{4,5},{5,4},{6,7},{7,6},{8,9},{9,8},{10,11... | collective-permute-start | bytes 98312 | tf_op jit(solution)/shard_map/ppermute | solution.py:461
  11.6 36.7 %collective-permute-start.5 = (f32[40,1024]{1,0:T(8,128)S(1)}, f32[40,1024]{1,0:T(8,128)S(1)}, u32[]{:S(2)}, u32[]{:S(2)}) collective-permute-start(f32[40,1024]{1,0:T(8,128)S(1)} %shard_map.66.rest_0_), channel_id=1, source_target_pairs={{0,1},{1,0},{2,3},{3,2},{4,5},{5,4},{6,7},{7,6},{8,9},{9,8},{10,11... | collective-permute-start | bytes 491528 | tf_op jit(solution)/shard_map/ppermute | solution.py:461
  12.1 62.6 %collective-permute-start.18 = (bf16[32,4096]{1,0:T(8,128)(2,1)S(1)}, bf16[32,4096]{1,0:T(8,128)(2,1)S(1)}, u32[]{:S(2)}, u32[]{:S(2)}) collective-permute-start(bf16[32,4096]{1,0:T(8,128)(2,1)S(1)} %get-tuple-element.37), channel_id=1, source_target_pairs={{0,1},{1,0},{2,3},{3,2},{4,5},{5,4},{6,7},{7,6},{8,9},{9,8},{10,11... | collective-permute-start | bytes 786440 | tf_op jit(solution)/shard_map/ppermute | solution.py:461
  15.2 52.9 %collective-permute-start.19 = (bf16[32,4096]{1,0:T(8,128)(2,1)S(1)}, bf16[32,4096]{1,0:T(8,128)(2,1)}, u32[]{:S(2)}, u32[]{:S(2)}) collective-permute-start(bf16[32,4096]{1,0:T(8,128)(2,1)S(1)} %get-tuple-element.39), channel_id=1, source_target_pairs={{0,1},{1,0},{2,3},{3,2},{4,5},{5,4},{6,7},{7,6},{8,9},{9,8},{10,11... | collective-permute-start | bytes 786440 | tf_op jit(solution)/shard_map/ppermute | solution.py:461
  15.8 20.9 %collective-permute-start.1 = (bf16[272,128]{1,0:T(8,128)(2,1)S(1)}, bf16[272,128]{1,0:T(8,128)(2,1)S(1)}, u32[]{:S(2)}, u32[]{:S(2)}) collective-permute-start(bf16[272,128]{1,0:T(8,128)(2,1)S(1)} %shard_map.65.aw2), channel_id=1, source_target_pairs={{124,0},{126,2},{0,4},{2,6},{4,8},{6,10},{8,12},{10,14},{12,16},{1... | collective-permute-start | bytes 208904 | tf_op jit(solution)/shard_map/ppermute | solution.py:450
  17.5 29.1 %collective-permute-start.4 = (bf16[272,128]{1,0:T(8,128)(2,1)S(1)}, bf16[272,128]{1,0:T(8,128)(2,1)S(1)}, u32[]{:S(2)}, u32[]{:S(2)}) collective-permute-start(bf16[272,128]{1,0:T(8,128)(2,1)S(1)} %shard_map.65.aw2), channel_id=1, source_target_pairs={{4,0},{6,2},{8,4},{10,6},{12,8},{14,10},{16,12},{18,14},{20,16},{2... | collective-permute-start | bytes 208904 | tf_op jit(solution)/shard_map/ppermute | solution.py:450
  36.7 8.0 %collective-permute-start.2 = (bf16[272,128]{1,0:T(8,128)(2,1)S(1)}, bf16[272,128]{1,0:T(8,128)(2,1)S(1)}, u32[]{:S(2)}, u32[]{:S(2)}) collective-permute-start(bf16[272,128]{1,0:T(8,128)(2,1)S(1)} %shard_map.65.aw2), channel_id=1, source_target_pairs={{126,0},{0,2},{2,4},{4,6},{6,8},{8,10},{10,12},{12,14},{14,16},{16... | collective-permute-start | bytes 208904 | tf_op jit(solution)/shard_map/ppermute | solution.py:450
  44.7 1.9 %collective-permute-start.3 = (bf16[272,128]{1,0:T(8,128)(2,1)S(1)}, bf16[272,128]{1,0:T(8,128)(2,1)S(1)}, u32[]{:S(2)}, u32[]{:S(2)}) collective-permute-start(bf16[272,128]{1,0:T(8,128)(2,1)S(1)} %shard_map.65.aw2), channel_id=1, source_target_pairs={{2,0},{4,2},{6,4},{8,6},{10,8},{12,10},{14,12},{16,14},{18,16},{20... | collective-permute-start | bytes 208904 | tf_op jit(solution)/shard_map/ppermute | solution.py:450
  49.8 6.5 %collective-permute-start.9 = (bf16[256,128]{1,0:T(8,128)(2,1)S(1)}, bf16[256,128]{1,0:T(8,128)(2,1)S(1)}, u32[]{:S(2)}, u32[]{:S(2)}) collective-permute-start(bf16[256,128]{1,0:T(8,128)(2,1)S(1)} %get-tuple-element.31.aw2), channel_id=1, source_target_pairs={{4,0},{6,2},{8,4},{10,6},{12,8},{14,10},{16,12},{18,14},{20,16},{2... | collective-permute-start | bytes 196616 | tf_op jit(solution)/shard_map/ppermute | solution.py:450
  50.1 8.0 %collective-permute-start.8 = (bf16[256,128]{1,0:T(8,128)(2,1)S(1)}, bf16[256,128]{1,0:T(8,128)(2,1)S(1)}, u32[]{:S(2)}, u32[]{:S(2)}) collective-permute-start(bf16[256,128]{1,0:T(8,128)(2,1)S(1)} %get-tuple-element.31.aw2), channel_id=1, source_target_pairs={{2,0},{4,2},{6,4},{8,6},{10,8},{12,10},{14,12},{16,14},{18,16},{20... | collective-permute-start | bytes 196616 | tf_op jit(solution)/shard_map/ppermute | solution.py:450
  56.2 7.9 %collective-permute-start.7 = (bf16[256,128]{1,0:T(8,128)(2,1)S(1)}, bf16[256,128]{1,0:T(8,128)(2,1)S(1)}, u32[]{:S(2)}, u32[]{:S(2)}) collective-permute-start(bf16[256,128]{1,0:T(8,128)(2,1)S(1)} %get-tuple-element.31.aw2), channel_id=1, source_target_pairs={{126,0},{0,2},{2,4},{4,6},{6,8},{8,10},{10,12},{12,14},{14,16},{16... | collective-permute-start | bytes 196616 | tf_op jit(solution)/shard_map/ppermute | solution.py:450
  56.3 8.5 %collective-permute-start.6 = (bf16[256,128]{1,0:T(8,128)(2,1)S(1)}, bf16[256,128]{1,0:T(8,128)(2,1)S(1)}, u32[]{:S(2)}, u32[]{:S(2)}) collective-permute-start(bf16[256,128]{1,0:T(8,128)(2,1)S(1)} %get-tuple-element.31.aw2), channel_id=1, source_target_pairs={{124,0},{126,2},{0,4},{2,6},{4,8},{6,10},{8,12},{10,14},{12,16},{1... | collective-permute-start | bytes 196616 | tf_op jit(solution)/shard_map/ppermute | solution.py:450
  66.2 18.2 %collective-permute-start.13 = (bf16[256,128]{1,0:T(8,128)(2,1)S(1)}, bf16[256,128]{1,0:T(8,128)(2,1)S(1)}, u32[]{:S(2)}, u32[]{:S(2)}) collective-permute-start(bf16[256,128]{1,0:T(8,128)(2,1)S(1)} %get-tuple-element.33.aw2), channel_id=1, source_target_pairs={{4,0},{6,2},{8,4},{10,6},{12,8},{14,10},{16,12},{18,14},{20,16},{2... | collective-permute-start | bytes 196616 | tf_op jit(solution)/shard_map/ppermute | solution.py:450
  66.3 18.1 %collective-permute-start.12 = (bf16[256,128]{1,0:T(8,128)(2,1)S(1)}, bf16[256,128]{1,0:T(8,128)(2,1)S(1)}, u32[]{:S(2)}, u32[]{:S(2)}) collective-permute-start(bf16[256,128]{1,0:T(8,128)(2,1)S(1)} %get-tuple-element.33.aw2), channel_id=1, source_target_pairs={{2,0},{4,2},{6,4},{8,6},{10,8},{12,10},{14,12},{16,14},{18,16},{20... | collective-permute-start | bytes 196616 | tf_op jit(solution)/shard_map/ppermute | solution.py:450
  68.1 16.3 %collective-permute-start.11 = (bf16[256,128]{1,0:T(8,128)(2,1)S(1)}, bf16[256,128]{1,0:T(8,128)(2,1)S(1)}, u32[]{:S(2)}, u32[]{:S(2)}) collective-permute-start(bf16[256,128]{1,0:T(8,128)(2,1)S(1)} %get-tuple-element.33.aw2), channel_id=1, source_target_pairs={{126,0},{0,2},{2,4},{4,6},{6,8},{8,10},{10,12},{12,14},{14,16},{16... | collective-permute-start | bytes 196616 | tf_op jit(solution)/shard_map/ppermute | solution.py:450
  68.1 16.3 %collective-permute-start.10 = (bf16[256,128]{1,0:T(8,128)(2,1)S(1)}, bf16[256,128]{1,0:T(8,128)(2,1)S(1)}, u32[]{:S(2)}, u32[]{:S(2)}) collective-permute-start(bf16[256,128]{1,0:T(8,128)(2,1)S(1)} %get-tuple-element.33.aw2), channel_id=1, source_target_pairs={{124,0},{126,2},{0,4},{2,6},{4,8},{6,10},{8,12},{10,14},{12,16},{1... | collective-permute-start | bytes 196616 | tf_op jit(solution)/shard_map/ppermute | solution.py:450
  69.7 1.2 copy-start.1
  86.0 16.9 %collective-permute-start.17 = (bf16[256,128]{1,0:T(8,128)(2,1)S(1)}, bf16[256,128]{1,0:T(8,128)(2,1)S(1)}, u32[]{:S(2)}, u32[]{:S(2)}) collective-permute-start(bf16[256,128]{1,0:T(8,128)(2,1)S(1)} %get-tuple-element.35.aw2), channel_id=1, source_target_pairs={{4,0},{6,2},{8,4},{10,6},{12,8},{14,10},{16,12},{18,14},{20,16},{2... | collective-permute-start | bytes 196616 | tf_op jit(solution)/shard_map/ppermute | solution.py:450
  90.6 12.3 %collective-permute-start.16 = (bf16[256,128]{1,0:T(8,128)(2,1)S(1)}, bf16[256,128]{1,0:T(8,128)(2,1)S(1)}, u32[]{:S(2)}, u32[]{:S(2)}) collective-permute-start(bf16[256,128]{1,0:T(8,128)(2,1)S(1)} %get-tuple-element.35.aw2), channel_id=1, source_target_pairs={{2,0},{4,2},{6,4},{8,6},{10,8},{12,10},{14,12},{16,14},{18,16},{20... | collective-permute-start | bytes 196616 | tf_op jit(solution)/shard_map/ppermute | solution.py:450
  93.7 9.1 %collective-permute-start.15 = (bf16[256,128]{1,0:T(8,128)(2,1)S(1)}, bf16[256,128]{1,0:T(8,128)(2,1)S(1)}, u32[]{:S(2)}, u32[]{:S(2)}) collective-permute-start(bf16[256,128]{1,0:T(8,128)(2,1)S(1)} %get-tuple-element.35.aw2), channel_id=1, source_target_pairs={{126,0},{0,2},{2,4},{4,6},{6,8},{8,10},{10,12},{12,14},{14,16},{16... | collective-permute-start | bytes 196616 | tf_op jit(solution)/shard_map/ppermute | solution.py:450
  93.8 9.0 %collective-permute-start.14 = (bf16[256,128]{1,0:T(8,128)(2,1)S(1)}, bf16[256,128]{1,0:T(8,128)(2,1)S(1)}, u32[]{:S(2)}, u32[]{:S(2)}) collective-permute-start(bf16[256,128]{1,0:T(8,128)(2,1)S(1)} %get-tuple-element.35.aw2), channel_id=1, source_target_pairs={{124,0},{126,2},{0,4},{2,6},{4,8},{6,10},{8,12},{10,14},{12,16},{1... | collective-permute-start | bytes 196616 | tf_op jit(solution)/shard_map/ppermute | solution.py:450
  106.6 15.5 %collective-permute-start.20 = (bf16[32,4096]{1,0:T(8,128)(2,1)S(1)}, bf16[32,4096]{1,0:T(8,128)(2,1)S(1)}, u32[]{:S(2)}, u32[]{:S(2)}) collective-permute-start(bf16[32,4096]{1,0:T(8,128)(2,1)S(1)} %get-tuple-element.42), channel_id=1, source_target_pairs={{0,1},{1,0},{2,3},{3,2},{4,5},{5,4},{6,7},{7,6},{8,9},{9,8},{10,11... | collective-permute-start | bytes 786440 | tf_op jit(solution)/shard_map/ppermute | solution.py:461
  109.3 10.9 %collective-permute-start.22 = (bf16[32,2048]{1,0:T(8,128)(2,1)S(1)}, bf16[32,2048]{1,0:T(8,128)(2,1)S(1)}, u32[]{:S(2)}, u32[]{:S(2)}) collective-permute-start(bf16[32,2048]{1,0:T(8,128)(2,1)S(1)} %get-tuple-element.44), channel_id=1, source_target_pairs={{0,1},{1,0},{2,3},{3,2},{4,5},{5,4},{6,7},{7,6},{8,9},{9,8},{10,11... | collective-permute-start | bytes 393224 | tf_op jit(solution)/shard_map/ppermute | solution.py:461
  114.4 7.7 %collective-permute-start.21 = (bf16[32,2048]{1,0:T(8,128)(2,1)S(1)}, bf16[32,2048]{1,0:T(8,128)(2,1)S(1)}, u32[]{:S(2)}, u32[]{:S(2)}) collective-permute-start(bf16[32,2048]{1,0:T(8,128)(2,1)S(1)} %get-tuple-element.43), channel_id=1, source_target_pairs={{0,1},{1,0},{2,3},{3,2},{4,5},{5,4},{6,7},{7,6},{8,9},{9,8},{10,11... | collective-permute-start | bytes 393224 | tf_op jit(solution)/shard_map/ppermute | solution.py:461

commit v4 on v3

--- a/solution.py
+++ b/solution.py
@@ -14,7 +14,7 @@
 WINDOW = 32
 MORE = 128
 PAD = 128
-UNROLL = 2
+UNROLL = 4
 PIECES = 2
 KINDS = (0, 2, 4)
 LANES = 128
@@ -281,6 +281,7 @@
     padded = count + PAD
     chunks = outs[0].shape[1] // CHUNK
     middle = all_chunks * CHUNK // 2 / RADIUS
+    unroll = min(UNROLL, chunks)
     position_row = prow_ref[batch : batch + 1, :]
 
     def entry(c, kind, what):
@@ -412,13 +413,13 @@
         total_ref[:, local] = x + change
 
     def several(m, carry):
-        for slot in range(UNROLL):
-            one(m * UNROLL + slot, slot)
+        for slot in range(unroll):
+            one(m * unroll + slot, slot)
         return carry
 
     if first:
         bring.wait()
-    lax.fori_loop(0, chunks // UNROLL, several, 0)
+    lax.fori_loop(0, chunks // unroll, several, 0)
 
     def extend(n, carry):
         c = first_chunk + n

time: 124 us -> 124 us (level)
  Pallas kernels: 41.4 us -> 40.1 us
    pallas_call x9, Pallas kernels: 28.4 us -> 27.1 us  [bulk(): vmem_call(functools.partial(bulk_body, batch, width // CHUNK, *first_chun...]
  transfers between devices with their start and end apart: 23 -> 23, of which waited for: 7 -> 7; matrix products, arithmetic and copies ran while one was open for 2% -> 2% of each run, Pallas kernels for 26% -> 25%
where the time goes in v4:
time: 124 us; the launch traced here: 123 us
  starting transfers between devices  40.4 us (33%)
  Pallas kernels  40.1 us (32%)
  waiting for transfers between devices  37 us (30%)
  local copies, waits for them, and re-layouts  2.56 us (2%)
  other arithmetic  2.42 us (2%)
    ppermute x16, waiting for transfers between devices, cyclic(): lax.ppermute(block, 'space', [((i + distance) % n, i) for i in range(n)])  29.8 us
    ppermute x16, starting transfers between devices, cyclic(): lax.ppermute(block, 'space', [((i + distance) % n, i) for i in range(n)])  28.6 us
    pallas_call x9, Pallas kernels, bulk(): vmem_call(functools.partial(bulk_body, batch, width // CHUNK, *first_chun...  27.1 us
    ppermute x7, starting transfers between devices, traded(): return lax.ppermute(block, 'mem', [(0, 1), (1, 0)])  11.9 us
    ppermute x7, waiting for transfers between devices, traded(): return lax.ppermute(block, 'mem', [(0, 1), (1, 0)])  7.15 us
    pallas_call x3, Pallas kernels, shards(): vmem_call(functools.partial(step_body, batch + 1), (shape((members, later...  4.44 us
    pallas_call x1, Pallas kernels, shards(): vmem_call(prep_body, (shape((block_width // groups, LANES), F32), shape((...  4.33 us
    pallas_call x1, Pallas kernels, shards(): vmem_call(prep_rest_body, shape((members_here + width // CHUNK, CHUNK), F...  4.04 us
  transfers between devices with their start and end apart: 23, of which 7 were waited for; matrix products, arithmetic and copies ran while one was open for 2% of the time, Pallas kernels for 25%

profile of v4, /device:TPU:0, one launch (start us, length us, event | category | flops | bytes accessed | tf_op | source)
XLA Modules:
  0.0 122.8 jit_solution(6237219653551215561)
XLA Ops:
  0.0 4.3 %shard_map.64 = (f32[4096,128]{1,0:T(8,128)S(1)}, f32[32,256]{1,0:T(8,128)S(1)}, f32[12,256]{1,0:T(8,128)S(1)}, f32[32,8192]{1,0:T(8,128)S(1)}, bf16[32,4096]{1,...) custom-call(s32[1]{0:T(128)} %bitcast.half_ref, ...), custom_call_target="tpu_custom_call" | custom-call | flops 10000000 | bytes 6000000 | tf_op jit(solution)/shard_map/pallas_call | solution.py:479
  4.4 3.2 %collective-permute-start = (f32[32,256]{1,0:T(8,128)S(1)}, f32[32,256]{1,0:T(8,128)S(1)}, u32[]{:S(2)}, u32[]{:S(2)}) collective-permute-start(f32[32,256]{1,0:T(8,128)S(1)} %get-tuple-element.25.own_ref), channel_id=1, source_target_pairs={{0,1},{1,0},{2,3},{3,2},{4,5},{5,4},{6,7},{7,6},{8,9},{9,8},{10,11... | collective-permute-start | bytes 98312 | tf_op jit(solution)/shard_map/ppermute | solution.py:462
  7.6 4.0 %shard_map.66.rest_0_ = f32[40,1024]{1,0:T(8,128)S(1)} custom-call(s32[4,256]{1,0:T(4,128)S(1)} %get-tuple-element.27.spot_ref, f32[16,256]{1,0:T(8,128)S(1)} %get-tuple-element.28.table_ref, f32[4096,128]{1,0:T(8,128)S(1)} %get-tuple-element.29.turned_ref, f32[1,8192]{1,0:T(1,128)S(1)} %get-tuple-element.30.mean_ref), custom_call_target="tpu_custom_call" | custom-call | flops 10000000 | bytes 6000000 | tf_op jit(solution)/shard_map/pallas_call | solution.py:506
  12.1 3.1 %collective-permute-start.18 = (bf16[32,4096]{1,0:T(8,128)(2,1)S(1)}, bf16[32,4096]{1,0:T(8,128)(2,1)S(1)}, u32[]{:S(2)}, u32[]{:S(2)}) collective-permute-start(bf16[32,4096]{1,0:T(8,128)(2,1)S(1)} %get-tuple-element.37), channel_id=1, source_target_pairs={{0,1},{1,0},{2,3},{3,2},{4,5},{5,4},{6,7},{7,6},{8,9},{9,8},{10,11... | collective-permute-start | bytes 786440 | tf_op jit(solution)/shard_map/ppermute | solution.py:462
  15.8 1.7 %collective-permute-start.1 = (bf16[272,128]{1,0:T(8,128)(2,1)S(1)}, bf16[272,128]{1,0:T(8,128)(2,1)S(1)}, u32[]{:S(2)}, u32[]{:S(2)}) collective-permute-start(bf16[272,128]{1,0:T(8,128)(2,1)S(1)} %shard_map.65.aw2), channel_id=1, source_target_pairs={{124,0},{126,2},{0,4},{2,6},{4,8},{6,10},{8,12},{10,14},{12,16},{1... | collective-permute-start | bytes 208904 | tf_op jit(solution)/shard_map/ppermute | solution.py:451
  17.5 6.0 %collective-permute-start.4 = (bf16[272,128]{1,0:T(8,128)(2,1)S(1)}, bf16[272,128]{1,0:T(8,128)(2,1)S(1)}, u32[]{:S(2)}, u32[]{:S(2)}) collective-permute-start(bf16[272,128]{1,0:T(8,128)(2,1)S(1)} %shard_map.65.aw2), channel_id=1, source_target_pairs={{4,0},{6,2},{8,4},{10,6},{12,8},{14,10},{16,12},{18,14},{20,16},{2... | collective-permute-start | bytes 208904 | tf_op jit(solution)/shard_map/ppermute | solution.py:451
  23.5 13.2 %collective-permute-done.1.aw0 = bf16[272,128]{1,0:T(8,128)(2,1)S(1)} collective-permute-done((bf16[272,128]{1,0:T(8,128)(2,1)S(1)}, bf16[272,128]{1,0:T(8,128)(2,1)S(1)}, u32[]{:S(2)}, u32[]{:S(2)}) %collective-permute-start.1) | collective-permute-done | bytes 69664 | tf_op jit(solution)/shard_map/ppermute | solution.py:451
  36.7 7.9 %collective-permute-done.2.aw1 = bf16[272,128]{1,0:T(8,128)(2,1)S(1)} collective-permute-done((bf16[272,128]{1,0:T(8,128)(2,1)S(1)}, bf16[272,128]{1,0:T(8,128)(2,1)S(1)}, u32[]{:S(2)}, u32[]{:S(2)}) %collective-permute-start.2) | collective-permute-done | bytes 69664 | tf_op jit(solution)/shard_map/ppermute | solution.py:451
  44.7 1.9 %collective-permute-done.3.aw3 = bf16[272,128]{1,0:T(8,128)(2,1)S(1)} collective-permute-done((bf16[272,128]{1,0:T(8,128)(2,1)S(1)}, bf16[272,128]{1,0:T(8,128)(2,1)S(1)}, u32[]{:S(2)}, u32[]{:S(2)}) %collective-permute-start.3) | collective-permute-done | bytes 69664 | tf_op jit(solution)/shard_map/ppermute | solution.py:451
  48.3 1.5 %shard_map.67 = (f32[64,768]{1,0:T(8,128)S(1)}, bf16[256,128]{1,0:T(8,128)(2,1)S(1)}) custom-call(bf16[272,128]{1,0:T(8,128)(2,1)S(1)} %collective-permute-done.1.aw0, bf16[272,128]{1,0:T(8,128)(2,1)S(1)} %collective-permute-done.2.aw1, bf16[272,128]{1,0:T(8,128)(2,1)S(1)} %shard_map.65.aw2, bf16[272,128]{1,0:T(8,128)(2,1)S(1)} %collective-permute-done.3.aw3, ...), custom_call_target="tpu_custom_call" | custom-call | flops 251658240 | bytes 1000000 | tf_op jit(solution)/shard_map/pallas_call | solution.py:572
  50.1 6.0 %collective-permute-start.8 = (bf16[256,128]{1,0:T(8,128)(2,1)S(1)}, bf16[256,128]{1,0:T(8,128)(2,1)S(1)}, u32[]{:S(2)}, u32[]{:S(2)}) collective-permute-start(bf16[256,128]{1,0:T(8,128)(2,1)S(1)} %get-tuple-element.31.aw2), channel_id=1, source_target_pairs={{2,0},{4,2},{6,4},{8,6},{10,8},{12,10},{14,12},{16,14},{18,16},{20... | collective-permute-start | bytes 196616 | tf_op jit(solution)/shard_map/ppermute | solution.py:451
  56.3 1.6 %collective-permute-start.6 = (bf16[256,128]{1,0:T(8,128)(2,1)S(1)}, bf16[256,128]{1,0:T(8,128)(2,1)S(1)}, u32[]{:S(2)}, u32[]{:S(2)}) collective-permute-start(bf16[256,128]{1,0:T(8,128)(2,1)S(1)} %get-tuple-element.31.aw2), channel_id=1, source_target_pairs={{124,0},{126,2},{0,4},{2,6},{4,8},{6,10},{8,12},{10,14},{12,16},{1... | collective-permute-start | bytes 196616 | tf_op jit(solution)/shard_map/ppermute | solution.py:451
  58.1 6.0 %collective-permute-done.7.aw1 = bf16[256,128]{1,0:T(8,128)(2,1)S(1)} collective-permute-done((bf16[256,128]{1,0:T(8,128)(2,1)S(1)}, bf16[256,128]{1,0:T(8,128)(2,1)S(1)}, u32[]{:S(2)}, u32[]{:S(2)}) %collective-permute-start.7) | collective-permute-done | bytes 65568 | tf_op jit(solution)/shard_map/ppermute | solution.py:451
  66.3 1.8 %collective-permute-start.12 = (bf16[256,128]{1,0:T(8,128)(2,1)S(1)}, bf16[256,128]{1,0:T(8,128)(2,1)S(1)}, u32[]{:S(2)}, u32[]{:S(2)}) collective-permute-start(bf16[256,128]{1,0:T(8,128)(2,1)S(1)} %get-tuple-element.33.aw2), channel_id=1, source_target_pairs={{2,0},{4,2},{6,4},{8,6},{10,8},{12,10},{14,12},{16,14},{18,16},{20... | collective-permute-start | bytes 196616 | tf_op jit(solution)/shard_map/ppermute | solution.py:451
  68.1 1.6 %collective-permute-start.10 = (bf16[256,128]{1,0:T(8,128)(2,1)S(1)}, bf16[256,128]{1,0:T(8,128)(2,1)S(1)}, u32[]{:S(2)}, u32[]{:S(2)}) collective-permute-start(bf16[256,128]{1,0:T(8,128)(2,1)S(1)} %get-tuple-element.33.aw2), channel_id=1, source_target_pairs={{124,0},{126,2},{0,4},{2,6},{4,8},{6,10},{8,12},{10,14},{12,16},{1... | collective-permute-start | bytes 196616 | tf_op jit(solution)/shard_map/ppermute | solution.py:451
  71.0 3.6 %shard_map.74.rest_0_ = f32[64,4096]{1,0:T(8,128)S(1)} custom-call(s32[8,128]{1,0:T(8,128)S(1)} %pad.4.table_ref, bf16[272,128]{1,0:T(8,128)(2,1)S(1)} %collective-permute-done.1.aw0, bf16[272,128]{1,0:T(8,128)(2,1)S(1)} %collective-permute-done.2.aw1, bf16[272,128]{1,0:T(8,128)(2,1)S(1)} %shard_map.65.aw2, bf16[272,128]{1,0:T(8,128)(2,1)S(1)} %collective-permute-done.3.aw3, ...), custom_call_target="tpu_custom_call" | custom-call | flops 2000000000 | bytes 6000000 | tf_op jit(solution)/shard_map/pallas_call | solution.py:548
  74.6 3.6 %shard_map.70.rest_0_ = f32[64,4096]{1,0:T(8,128)S(1)} custom-call(s32[8,128]{1,0:T(8,128)S(1)} %pad.4.table_ref, bf16[272,128]{1,0:T(8,128)(2,1)S(1)} %collective-permute-done.1.aw0, bf16[272,128]{1,0:T(8,128)(2,1)S(1)} %collective-permute-done.2.aw1, bf16[272,128]{1,0:T(8,128)(2,1)S(1)} %shard_map.65.aw2, bf16[272,128]{1,0:T(8,128)(2,1)S(1)} %collective-permute-done.3.aw3, ...), custom_call_target="tpu_custom_call" | custom-call | flops 2000000000 | bytes 6000000 | tf_op jit(solution)/shard_map/pallas_call | solution.py:548
  78.2 2.8 %shard_map.71.rest_0_ = f32[64,4096]{1,0:T(8,128)S(1)} custom-call(s32[8,128]{1,0:T(8,128)S(1)} %pad.4.table_ref, bf16[256,128]{1,0:T(8,128)(2,1)S(1)} %collective-permute-done.6.aw0, bf16[256,128]{1,0:T(8,128)(2,1)S(1)} %collective-permute-done.7.aw1, bf16[256,128]{1,0:T(8,128)(2,1)S(1)} %get-tuple-element.31.aw2, ...), custom_call_target="tpu_custom_call" | custom-call | flops 2000000000 | bytes 6000000 | tf_op jit(solution)/shard_map/pallas_call | solution.py:548
  81.0 2.8 %shard_map.75.rest_0_ = f32[64,4096]{1,0:T(8,128)S(1)} custom-call(s32[8,128]{1,0:T(8,128)S(1)} %pad.4.table_ref, bf16[256,128]{1,0:T(8,128)(2,1)S(1)} %collective-permute-done.6.aw0, bf16[256,128]{1,0:T(8,128)(2,1)S(1)} %collective-permute-done.7.aw1, bf16[256,128]{1,0:T(8,128)(2,1)S(1)} %get-tuple-element.31.aw2, ...), custom_call_target="tpu_custom_call" | custom-call | flops 2000000000 | bytes 6000000 | tf_op jit(solution)/shard_map/pallas_call | solution.py:548
  83.8 1.6 %shard_map.69 = (f32[64,256]{1,0:T(8,128)}, bf16[256,128]{1,0:T(8,128)(2,1)S(1)}) custom-call(bf16[256,128]{1,0:T(8,128)(2,1)S(1)} %collective-permute-done.10.aw0, bf16[256,128]{1,0:T(8,128)(2,1)S(1)} %collective-permute-done.11.aw1, bf16[256,128]{1,0:T(8,128)(2,1)S(1)} %get-tuple-element.33.aw2, bf16[256,128]{1,0:T(8,128)(2,1)S(1)} %collective-permute-done.12.aw3, ...), custom_call_target="tpu_custom_call" | custom-call | flops 83886080 | bytes 1000000 | tf_op jit(solution)/shard_map/pallas_call | solution.py:572
  85.3 4.6 %collective-permute-start.17 = (bf16[256,128]{1,0:T(8,128)(2,1)S(1)}, bf16[256,128]{1,0:T(8,128)(2,1)S(1)}, u32[]{:S(2)}, u32[]{:S(2)}) collective-permute-start(bf16[256,128]{1,0:T(8,128)(2,1)S(1)} %get-tuple-element.35.aw2), channel_id=1, source_target_pairs={{4,0},{6,2},{8,4},{10,6},{12,8},{14,10},{16,12},{18,14},{20,16},{2... | collective-permute-start | bytes 196616 | tf_op jit(solution)/shard_map/ppermute | solution.py:451
  90.0 3.2 %collective-permute-start.16 = (bf16[256,128]{1,0:T(8,128)(2,1)S(1)}, bf16[256,128]{1,0:T(8,128)(2,1)S(1)}, u32[]{:S(2)}, u32[]{:S(2)}) collective-permute-start(bf16[256,128]{1,0:T(8,128)(2,1)S(1)} %get-tuple-element.35.aw2), channel_id=1, source_target_pairs={{2,0},{4,2},{6,4},{8,6},{10,8},{12,10},{14,12},{16,14},{18,16},{20... | collective-permute-start | bytes 196616 | tf_op jit(solution)/shard_map/ppermute | solution.py:451
  93.2 1.6 %collective-permute-start.14 = (bf16[256,128]{1,0:T(8,128)(2,1)S(1)}, bf16[256,128]{1,0:T(8,128)(2,1)S(1)}, u32[]{:S(2)}, u32[]{:S(2)}) collective-permute-start(bf16[256,128]{1,0:T(8,128)(2,1)S(1)} %get-tuple-element.35.aw2), channel_id=1, source_target_pairs={{124,0},{126,2},{0,4},{2,6},{4,8},{6,10},{8,12},{10,14},{12,16},{1... | collective-permute-start | bytes 196616 | tf_op jit(solution)/shard_map/ppermute | solution.py:451
  94.9 3.4 %shard_map.76.rest_0_ = f32[64,4096]{1,0:T(8,128)S(1)} custom-call(s32[8,128]{1,0:T(8,128)S(1)} %pad.4.table_ref, bf16[256,128]{1,0:T(8,128)(2,1)S(1)} %collective-permute-done.10.aw0, bf16[256,128]{1,0:T(8,128)(2,1)S(1)} %collective-permute-done.11.aw1, bf16[256,128]{1,0:T(8,128)(2,1)S(1)} %get-tuple-element.33.aw2, ...), custom_call_target="tpu_custom_call" | custom-call | flops 2000000000 | bytes 6000000 | tf_op jit(solution)/shard_map/pallas_call | solution.py:548
  98.3 3.5 %shard_map.72.rest_0_ = f32[64,4096]{1,0:T(8,128)S(1)} custom-call(s32[8,128]{1,0:T(8,128)S(1)} %pad.4.table_ref, bf16[256,128]{1,0:T(8,128)(2,1)S(1)} %collective-permute-done.10.aw0, bf16[256,128]{1,0:T(8,128)(2,1)S(1)} %collective-permute-done.11.aw1, bf16[256,128]{1,0:T(8,128)(2,1)S(1)} %get-tuple-element.33.aw2, ...), custom_call_target="tpu_custom_call" | custom-call | flops 2000000000 | bytes 6000000 | tf_op jit(solution)/shard_map/pallas_call | solution.py:548
  101.8 3.5 %shard_map.73 = (f32[32,4096]{1,0:T(8,128)S(1)}, bf16[32,4096]{1,0:T(8,128)(2,1)S(1)}) custom-call(s32[8,128]{1,0:T(8,128)S(1)} %pad.4.table_ref, bf16[256,128]{1,0:T(8,128)(2,1)S(1)} %collective-permute-done.14.aw0, bf16[256,128]{1,0:T(8,128)(2,1)S(1)} %collective-permute-done.15.aw1, bf16[256,128]{1,0:T(8,128)(2,1)S(1)} %get-tuple-element.35.aw2, ...), custom_call_target="tpu_custom_call" | custom-call | flops 2000000000 | bytes 6000000 | tf_op jit(solution)/shard_map/pallas_call | solution.py:548
  106.6 1.8 %shard_map.78 = (f32[32,2048]{1,0:T(8,128)S(1)}, bf16[32,2048]{1,0:T(8,128)(2,1)S(1)}) custom-call(s32[8,128]{1,0:T(8,128)S(1)} %pad.4.table_ref, bf16[256,128]{1,0:T(8,128)(2,1)S(1)} %collective-permute-done.14.aw0, bf16[256,128]{1,0:T(8,128)(2,1)S(1)} %collective-permute-done.15.aw1, bf16[256,128]{1,0:T(8,128)(2,1)S(1)} %get-tuple-element.35.aw2, ...), custom_call_target="tpu_custom_call" | custom-call | flops 2000000000 | bytes 6000000 | tf_op jit(solution)/shard_map/pallas_call | solution.py:548
  108.5 2.4 %collective-permute-start.22 = (bf16[32,2048]{1,0:T(8,128)(2,1)S(1)}, bf16[32,2048]{1,0:T(8,128)(2,1)S(1)}, u32[]{:S(2)}, u32[]{:S(2)}) collective-permute-start(bf16[32,2048]{1,0:T(8,128)(2,1)S(1)} %get-tuple-element.44), channel_id=1, source_target_pairs={{0,1},{1,0},{2,3},{3,2},{4,5},{5,4},{6,7},{7,6},{8,9},{9,8},{10,11... | collective-permute-start | bytes 393224 | tf_op jit(solution)/shard_map/ppermute | solution.py:462
  110.9 2.2 %shard_map.77 = (f32[32,2048]{1,0:T(8,128)S(1)}, bf16[32,2048]{1,0:T(8,128)(2,1)S(1)}) custom-call(s32[8,128]{1,0:T(8,128)S(1)} %pad.4.table_ref, bf16[256,128]{1,0:T(8,128)(2,1)S(1)} %collective-permute-done.14.aw0, bf16[256,128]{1,0:T(8,128)(2,1)S(1)} %collective-permute-done.15.aw1, bf16[256,128]{1,0:T(8,128)(2,1)S(1)} %get-tuple-element.35.aw2, ...), custom_call_target="tpu_custom_call" | custom-call | flops 2000000000 | bytes 6000000 | tf_op jit(solution)/shard_map/pallas_call | solution.py:548
  114.1 4.8 %collective-permute-done.22 = bf16[32,2048]{1,0:T(8,128)(2,1)S(1)} collective-permute-done((bf16[32,2048]{1,0:T(8,128)(2,1)S(1)}, bf16[32,2048]{1,0:T(8,128)(2,1)S(1)}, u32[]{:S(2)}, u32[]{:S(2)}) %collective-permute-start.22) | collective-permute-done | bytes 131104 | tf_op jit(solution)/shard_map/ppermute | solution.py:462
  118.9 2.3 %collective-permute-done.21 = bf16[32,2048]{1,0:T(8,128)(2,1)S(1)} collective-permute-done((bf16[32,2048]{1,0:T(8,128)(2,1)S(1)}, bf16[32,2048]{1,0:T(8,128)(2,1)S(1)}, u32[]{:S(2)}, u32[]{:S(2)}) %collective-permute-start.21) | collective-permute-done | bytes 131104 | tf_op jit(solution)/shard_map/ppermute | solution.py:462
  121.4 1.5 %pad_maximum_fusion = f32[32,16384]{1,0:T(8,128)} fusion(f32[32,8192]{1,0:T(8,128)S(1)} %get-tuple-element.46, f32[32,8192]{1,0:T(8,128)S(1)} %get-tuple-element.45), kind=kLoop, calls=%fused_computation.1 | loop fusion | flops 524288 | bytes 4194304 | tf_op jit(solution)/shard_map/concatenate | solution.py:608
  (68 shorter events, 9.4 us)
Async XLA Ops:
  0.0 15.6 %copy-start.4 = (s32[5]{0:T(128)S(1)}, s32[5]{0:T(128)}, u32[]{:S(2)}) copy-start(s32[5]{0:T(128)} %constant.74.clone) | copy-start | bytes 64
  0.0 46.7 %copy-start.2 = (f32[5]{0:T(128)S(1)}, f32[5]{0:T(128)}, u32[]{:S(2)}) copy-start(f32[5]{0:T(128)} %constant.80) | copy-start | bytes 64
  0.0 46.7 %copy-start.3 = (s32[5]{0:T(128)S(1)}, s32[5]{0:T(128)}, u32[]{:S(2)}) copy-start(s32[5]{0:T(128)} %constant.78) | copy-start | bytes 64
  4.3 7.3 %copy-start = (f32[32,8192]{1,0:T(8,128)}, f32[32,8192]{1,0:T(8,128)S(1)}, u32[]{:S(2)}) copy-start(f32[32,8192]{1,0:T(8,128)S(1)} %get-tuple-element.36.rest_0_) | copy-start | bytes 3145732
  4.4 11.3 %collective-permute-start = (f32[32,256]{1,0:T(8,128)S(1)}, f32[32,256]{1,0:T(8,128)S(1)}, u32[]{:S(2)}, u32[]{:S(2)}) collective-permute-start(f32[32,256]{1,0:T(8,128)S(1)} %get-tuple-element.25.own_ref), channel_id=1, source_target_pairs={{0,1},{1,0},{2,3},{3,2},{4,5},{5,4},{6,7},{7,6},{8,9},{9,8},{10,11... | collective-permute-start | bytes 98312 | tf_op jit(solution)/shard_map/ppermute | solution.py:462
  11.6 36.7 %collective-permute-start.5 = (f32[40,1024]{1,0:T(8,128)S(1)}, f32[40,1024]{1,0:T(8,128)S(1)}, u32[]{:S(2)}, u32[]{:S(2)}) collective-permute-start(f32[40,1024]{1,0:T(8,128)S(1)} %shard_map.66.rest_0_), channel_id=1, source_target_pairs={{0,1},{1,0},{2,3},{3,2},{4,5},{5,4},{6,7},{7,6},{8,9},{9,8},{10,11... | collective-permute-start | bytes 491528 | tf_op jit(solution)/shard_map/ppermute | solution.py:462
  12.1 62.5 %collective-permute-start.18 = (bf16[32,4096]{1,0:T(8,128)(2,1)S(1)}, bf16[32,4096]{1,0:T(8,128)(2,1)S(1)}, u32[]{:S(2)}, u32[]{:S(2)}) collective-permute-start(bf16[32,4096]{1,0:T(8,128)(2,1)S(1)} %get-tuple-element.37), channel_id=1, source_target_pairs={{0,1},{1,0},{2,3},{3,2},{4,5},{5,4},{6,7},{7,6},{8,9},{9,8},{10,11... | collective-permute-start | bytes 786440 | tf_op jit(solution)/shard_map/ppermute | solution.py:462
  15.2 52.9 %collective-permute-start.19 = (bf16[32,4096]{1,0:T(8,128)(2,1)S(1)}, bf16[32,4096]{1,0:T(8,128)(2,1)}, u32[]{:S(2)}, u32[]{:S(2)}) collective-permute-start(bf16[32,4096]{1,0:T(8,128)(2,1)S(1)} %get-tuple-element.39), channel_id=1, source_target_pairs={{0,1},{1,0},{2,3},{3,2},{4,5},{5,4},{6,7},{7,6},{8,9},{9,8},{10,11... | collective-permute-start | bytes 786440 | tf_op jit(solution)/shard_map/ppermute | solution.py:462
  15.8 20.9 %collective-permute-start.1 = (bf16[272,128]{1,0:T(8,128)(2,1)S(1)}, bf16[272,128]{1,0:T(8,128)(2,1)S(1)}, u32[]{:S(2)}, u32[]{:S(2)}) collective-permute-start(bf16[272,128]{1,0:T(8,128)(2,1)S(1)} %shard_map.65.aw2), channel_id=1, source_target_pairs={{124,0},{126,2},{0,4},{2,6},{4,8},{6,10},{8,12},{10,14},{12,16},{1... | collective-permute-start | bytes 208904 | tf_op jit(solution)/shard_map/ppermute | solution.py:451
  17.5 29.1 %collective-permute-start.4 = (bf16[272,128]{1,0:T(8,128)(2,1)S(1)}, bf16[272,128]{1,0:T(8,128)(2,1)S(1)}, u32[]{:S(2)}, u32[]{:S(2)}) collective-permute-start(bf16[272,128]{1,0:T(8,128)(2,1)S(1)} %shard_map.65.aw2), channel_id=1, source_target_pairs={{4,0},{6,2},{8,4},{10,6},{12,8},{14,10},{16,12},{18,14},{20,16},{2... | collective-permute-start | bytes 208904 | tf_op jit(solution)/shard_map/ppermute | solution.py:451
  36.7 8.0 %collective-permute-start.2 = (bf16[272,128]{1,0:T(8,128)(2,1)S(1)}, bf16[272,128]{1,0:T(8,128)(2,1)S(1)}, u32[]{:S(2)}, u32[]{:S(2)}) collective-permute-start(bf16[272,128]{1,0:T(8,128)(2,1)S(1)} %shard_map.65.aw2), channel_id=1, source_target_pairs={{126,0},{0,2},{2,4},{4,6},{6,8},{8,10},{10,12},{12,14},{14,16},{16... | collective-permute-start | bytes 208904 | tf_op jit(solution)/shard_map/ppermute | solution.py:451
  44.7 1.9 %collective-permute-start.3 = (bf16[272,128]{1,0:T(8,128)(2,1)S(1)}, bf16[272,128]{1,0:T(8,128)(2,1)S(1)}, u32[]{:S(2)}, u32[]{:S(2)}) collective-permute-start(bf16[272,128]{1,0:T(8,128)(2,1)S(1)} %shard_map.65.aw2), channel_id=1, source_target_pairs={{2,0},{4,2},{6,4},{8,6},{10,8},{12,10},{14,12},{16,14},{18,16},{20... | collective-permute-start | bytes 208904 | tf_op jit(solution)/shard_map/ppermute | solution.py:451
  49.8 6.5 %collective-permute-start.9 = (bf16[256,128]{1,0:T(8,128)(2,1)S(1)}, bf16[256,128]{1,0:T(8,128)(2,1)S(1)}, u32[]{:S(2)}, u32[]{:S(2)}) collective-permute-start(bf16[256,128]{1,0:T(8,128)(2,1)S(1)} %get-tuple-element.31.aw2), channel_id=1, source_target_pairs={{4,0},{6,2},{8,4},{10,6},{12,8},{14,10},{16,12},{18,14},{20,16},{2... | collective-permute-start | bytes 196616 | tf_op jit(solution)/shard_map/ppermute | solution.py:451
  50.1 8.0 %collective-permute-start.8 = (bf16[256,128]{1,0:T(8,128)(2,1)S(1)}, bf16[256,128]{1,0:T(8,128)(2,1)S(1)}, u32[]{:S(2)}, u32[]{:S(2)}) collective-permute-start(bf16[256,128]{1,0:T(8,128)(2,1)S(1)} %get-tuple-element.31.aw2), channel_id=1, source_target_pairs={{2,0},{4,2},{6,4},{8,6},{10,8},{12,10},{14,12},{16,14},{18,16},{20... | collective-permute-start | bytes 196616 | tf_op jit(solution)/shard_map/ppermute | solution.py:451
  56.2 7.9 %collective-permute-start.7 = (bf16[256,128]{1,0:T(8,128)(2,1)S(1)}, bf16[256,128]{1,0:T(8,128)(2,1)S(1)}, u32[]{:S(2)}, u32[]{:S(2)}) collective-permute-start(bf16[256,128]{1,0:T(8,128)(2,1)S(1)} %get-tuple-element.31.aw2), channel_id=1, source_target_pairs={{126,0},{0,2},{2,4},{4,6},{6,8},{8,10},{10,12},{12,14},{14,16},{16... | collective-permute-start | bytes 196616 | tf_op jit(solution)/shard_map/ppermute | solution.py:451
  56.3 8.5 %collective-permute-start.6 = (bf16[256,128]{1,0:T(8,128)(2,1)S(1)}, bf16[256,128]{1,0:T(8,128)(2,1)S(1)}, u32[]{:S(2)}, u32[]{:S(2)}) collective-permute-start(bf16[256,128]{1,0:T(8,128)(2,1)S(1)} %get-tuple-element.31.aw2), channel_id=1, source_target_pairs={{124,0},{126,2},{0,4},{2,6},{4,8},{6,10},{8,12},{10,14},{12,16},{1... | collective-permute-start | bytes 196616 | tf_op jit(solution)/shard_map/ppermute | solution.py:451
  66.2 17.6 %collective-permute-start.13 = (bf16[256,128]{1,0:T(8,128)(2,1)S(1)}, bf16[256,128]{1,0:T(8,128)(2,1)S(1)}, u32[]{:S(2)}, u32[]{:S(2)}) collective-permute-start(bf16[256,128]{1,0:T(8,128)(2,1)S(1)} %get-tuple-element.33.aw2), channel_id=1, source_target_pairs={{4,0},{6,2},{8,4},{10,6},{12,8},{14,10},{16,12},{18,14},{20,16},{2... | collective-permute-start | bytes 196616 | tf_op jit(solution)/shard_map/ppermute | solution.py:451
  66.3 17.5 %collective-permute-start.12 = (bf16[256,128]{1,0:T(8,128)(2,1)S(1)}, bf16[256,128]{1,0:T(8,128)(2,1)S(1)}, u32[]{:S(2)}, u32[]{:S(2)}) collective-permute-start(bf16[256,128]{1,0:T(8,128)(2,1)S(1)} %get-tuple-element.33.aw2), channel_id=1, source_target_pairs={{2,0},{4,2},{6,4},{8,6},{10,8},{12,10},{14,12},{16,14},{18,16},{20... | collective-permute-start | bytes 196616 | tf_op jit(solution)/shard_map/ppermute | solution.py:451
  68.1 15.7 %collective-permute-start.11 = (bf16[256,128]{1,0:T(8,128)(2,1)S(1)}, bf16[256,128]{1,0:T(8,128)(2,1)S(1)}, u32[]{:S(2)}, u32[]{:S(2)}) collective-permute-start(bf16[256,128]{1,0:T(8,128)(2,1)S(1)} %get-tuple-element.33.aw2), channel_id=1, source_target_pairs={{126,0},{0,2},{2,4},{4,6},{6,8},{8,10},{10,12},{12,14},{14,16},{16... | collective-permute-start | bytes 196616 | tf_op jit(solution)/shard_map/ppermute | solution.py:451
  68.1 15.7 %collective-permute-start.10 = (bf16[256,128]{1,0:T(8,128)(2,1)S(1)}, bf16[256,128]{1,0:T(8,128)(2,1)S(1)}, u32[]{:S(2)}, u32[]{:S(2)}) collective-permute-start(bf16[256,128]{1,0:T(8,128)(2,1)S(1)} %get-tuple-element.33.aw2), channel_id=1, source_target_pairs={{124,0},{126,2},{0,4},{2,6},{4,8},{6,10},{8,12},{10,14},{12,16},{1... | collective-permute-start | bytes 196616 | tf_op jit(solution)/shard_map/ppermute | solution.py:451
  69.7 1.2 copy-start.1
  85.3 16.5 %collective-permute-start.17 = (bf16[256,128]{1,0:T(8,128)(2,1)S(1)}, bf16[256,128]{1,0:T(8,128)(2,1)S(1)}, u32[]{:S(2)}, u32[]{:S(2)}) collective-permute-start(bf16[256,128]{1,0:T(8,128)(2,1)S(1)} %get-tuple-element.35.aw2), channel_id=1, source_target_pairs={{4,0},{6,2},{8,4},{10,6},{12,8},{14,10},{16,12},{18,14},{20,16},{2... | collective-permute-start | bytes 196616 | tf_op jit(solution)/shard_map/ppermute | solution.py:451
  90.0 11.8 %collective-permute-start.16 = (bf16[256,128]{1,0:T(8,128)(2,1)S(1)}, bf16[256,128]{1,0:T(8,128)(2,1)S(1)}, u32[]{:S(2)}, u32[]{:S(2)}) collective-permute-start(bf16[256,128]{1,0:T(8,128)(2,1)S(1)} %get-tuple-element.35.aw2), channel_id=1, source_target_pairs={{2,0},{4,2},{6,4},{8,6},{10,8},{12,10},{14,12},{16,14},{18,16},{20... | collective-permute-start | bytes 196616 | tf_op jit(solution)/shard_map/ppermute | solution.py:451
  93.1 8.7 %collective-permute-start.15 = (bf16[256,128]{1,0:T(8,128)(2,1)S(1)}, bf16[256,128]{1,0:T(8,128)(2,1)S(1)}, u32[]{:S(2)}, u32[]{:S(2)}) collective-permute-start(bf16[256,128]{1,0:T(8,128)(2,1)S(1)} %get-tuple-element.35.aw2), channel_id=1, source_target_pairs={{126,0},{0,2},{2,4},{4,6},{6,8},{8,10},{10,12},{12,14},{14,16},{16... | collective-permute-start | bytes 196616 | tf_op jit(solution)/shard_map/ppermute | solution.py:451
  93.2 8.6 %collective-permute-start.14 = (bf16[256,128]{1,0:T(8,128)(2,1)S(1)}, bf16[256,128]{1,0:T(8,128)(2,1)S(1)}, u32[]{:S(2)}, u32[]{:S(2)}) collective-permute-start(bf16[256,128]{1,0:T(8,128)(2,1)S(1)} %get-tuple-element.35.aw2), channel_id=1, source_target_pairs={{124,0},{126,2},{0,4},{2,6},{4,8},{6,10},{8,12},{10,14},{12,16},{1... | collective-permute-start | bytes 196616 | tf_op jit(solution)/shard_map/ppermute | solution.py:451
  105.3 15.9 %collective-permute-start.20 = (bf16[32,4096]{1,0:T(8,128)(2,1)S(1)}, bf16[32,4096]{1,0:T(8,128)(2,1)S(1)}, u32[]{:S(2)}, u32[]{:S(2)}) collective-permute-start(bf16[32,4096]{1,0:T(8,128)(2,1)S(1)} %get-tuple-element.42), channel_id=1, source_target_pairs={{0,1},{1,0},{2,3},{3,2},{4,5},{5,4},{6,7},{7,6},{8,9},{9,8},{10,11... | collective-permute-start | bytes 786440 | tf_op jit(solution)/shard_map/ppermute | solution.py:462
  108.5 10.4 %collective-permute-start.22 = (bf16[32,2048]{1,0:T(8,128)(2,1)S(1)}, bf16[32,2048]{1,0:T(8,128)(2,1)S(1)}, u32[]{:S(2)}, u32[]{:S(2)}) collective-permute-start(bf16[32,2048]{1,0:T(8,128)(2,1)S(1)} %get-tuple-element.44), channel_id=1, source_target_pairs={{0,1},{1,0},{2,3},{3,2},{4,5},{5,4},{6,7},{7,6},{8,9},{9,8},{10,11... | collective-permute-start | bytes 393224 | tf_op jit(solution)/shard_map/ppermute | solution.py:462
  113.1 8.2 %collective-permute-start.21 = (bf16[32,2048]{1,0:T(8,128)(2,1)S(1)}, bf16[32,2048]{1,0:T(8,128)(2,1)S(1)}, u32[]{:S(2)}, u32[]{:S(2)}) collective-permute-start(bf16[32,2048]{1,0:T(8,128)(2,1)S(1)} %get-tuple-element.43), channel_id=1, source_target_pairs={{0,1},{1,0},{2,3},{3,2},{4,5},{5,4},{6,7},{7,6},{8,9},{9,8},{10,11... | collective-permute-start | bytes 393224 | tf_op jit(solution)/shard_map/ppermute | solution.py:462
